TPU v7x, 128 devices: a whole 4x4x4 slice. The times are simulated.
128 devices in a mesh: dp: 4 (over x), fy: 4 (over z_hi, core), fx: 8 (over z_lo, y).
Axes of the slice: x: 4, y: 4, z: 4 (z_hi: 2, z_lo: 2; z = z_hi * 2 + z_lo), core: 2. Of those that a mesh axis runs over, the one named last changes fastest.
Arguments:
- fine_tokens: bfloat16 [4, 64, 256, 768], P('dp', 'fy', 'fx'), may hold values from -40 to 40
- parent: int32 [4, 64, 64], P('dp', 'fy', 'fx'), may hold values from 0 to 511, as said below
- coarse_tokens: bfloat16 [4, 512, 768], P('dp', 'fx'), may hold values from -6 to 6
- tile_level: int32 [4, 512], P('dp', 'fx'), may hold values from 0 to 2
- level_table: float32 [3, 768], replicated, may hold values from -3 to 3
- norm_gain: float32 [768], replicated, may hold values from 0.5 to 1.5
- qkv_weight: bfloat16 [768, 2304], replicated, may hold values from -7 to 7
- out_weight: bfloat16 [768, 768], replicated, may hold values from -0.21875 to 0.21875
- cotangent: bfloat16 [4, 64, 256, 768], P('dp', 'fy', 'fx'), may hold values from -6 to 6
Outputs:
- mixed: bfloat16 [4, 64, 256, 768], P('dp', 'fy', 'fx')
- grad_tokens: bfloat16 [4, 64, 256, 768], P('dp', 'fy', 'fx')
- grad_coarse: float32 [4, 512, 768], P('dp', 'fx')
- grad_qkv: float32 [768, 2304], P('dp')
- grad_out: float32 [768, 768], P('dp')
- grad_gain: float32 [768], P('dp')
- grad_level: float32 [3, 768], replicated
Inputs may be any that keep to these rules, and one draw needn't show every extreme that they name: `parent`: each entry names a coarse token of the same frame; a token of level l is drawn with weight l + 1.
All inputs are finite; a program needn't handle non-finite values.
Results may differ from a plain program's by a relative error of at most 0.025.
Values may be sent and summed in bfloat16 or wider, within the bound.
A program may use at most 128 MiB of HBM per device.

v0:
```python
import functools
import math

import jax
import jax.numpy as jnp
from jax import lax
from jax.sharding import PartitionSpec as P

HEADS = 12
BLK = 4
LEVELS = 3


def as_sent(shard):
    return jax.tree.map(lambda a: a.astype(jnp.bfloat16) if a.dtype == jnp.float32 else a, shard)


def attend_forward(queries, key_rows, values, score_scale, query_form, key_form, score_form):
    scores = (
        jnp.einsum(
            query_form + "," + key_form + "->" + score_form,
            queries,
            key_rows,
            preferred_element_type=jnp.float32,
        )
        * score_scale
    )
    weights = jax.nn.softmax(scores, axis=-1)
    rounded = weights.astype(jnp.bfloat16)
    attended = jnp.einsum(
        score_form + "," + key_form + "->" + query_form,
        rounded,
        values,
        preferred_element_type=jnp.float32,
    )
    return attended.astype(jnp.bfloat16)


def attend_grads(
    weights,
    rounded,
    queries,
    key_rows,
    values,
    grad_out,
    score_scale,
    query_form,
    key_form,
    score_form,
):
    grad_values = jnp.einsum(
        score_form + "," + query_form + "->" + key_form,
        rounded,
        grad_out,
        preferred_element_type=jnp.float32,
    ).astype(jnp.bfloat16)
    grad_weights = jnp.einsum(
        query_form + "," + key_form + "->" + score_form,
        grad_out,
        values,
        preferred_element_type=jnp.float32,
    )
    inner = jnp.sum(weights * grad_weights, axis=-1, keepdims=True)
    grad_scores = (weights * (grad_weights - inner) * score_scale).astype(jnp.bfloat16)
    grad_queries = jnp.einsum(
        score_form + "," + key_form + "->" + query_form,
        grad_scores,
        key_rows,
        preferred_element_type=jnp.float32,
    ).astype(jnp.bfloat16)
    grad_keys = jnp.einsum(
        score_form + "," + query_form + "->" + key_form,
        grad_scores,
        queries,
        preferred_element_type=jnp.float32,
    ).astype(jnp.bfloat16)
    return (grad_queries, grad_keys, grad_values)


def attend_backward(
    queries, key_rows, values, grad_out, score_scale, query_form, key_form, score_form
):
    scores = (
        jnp.einsum(
            query_form + "," + key_form + "->" + score_form,
            queries,
            key_rows,
            preferred_element_type=jnp.float32,
        )
        * score_scale
    )
    weights = jax.nn.softmax(scores, axis=-1)
    rounded = weights.astype(jnp.bfloat16)
    return attend_grads(
        weights,
        rounded,
        queries,
        key_rows,
        values,
        grad_out,
        score_scale,
        query_form,
        key_form,
        score_form,
    )


def take_rows(table_rows, row_ids):
    return jnp.take(table_rows, row_ids, axis=0)


def rows_to_batch(tensor, head_dim):
    return tensor.reshape(tensor.shape[1], tensor.shape[2], -1, head_dim)


def batch_to_rows(tensor):
    return tensor.reshape(1, tensor.shape[0], tensor.shape[1], -1)


def columns_to_batch(tensor, head_dim):
    return tensor.reshape(tensor.shape[0], tensor.shape[1], tensor.shape[3], -1, head_dim)


def batch_to_columns(tensor):
    return tensor.reshape(tensor.shape[0], tensor.shape[1], 1, tensor.shape[2], -1)


def to_row_groups(tensor, groups):
    return tensor.reshape(groups, -1, tensor.shape[2], tensor.shape[3])


def to_column_groups(tensor, groups):
    return tensor.reshape(tensor.shape[0], tensor.shape[1], groups, -1, tensor.shape[3])


def local(
    fine_tokens,
    parent,
    coarse_tokens,
    tile_level,
    level_table,
    norm_gain,
    qkv_weight,
    out_weight,
    cotangent,
):
    frame_count, row_count, column_count, model_dim = fine_tokens.shape
    row_groups = lax.axis_size("fx")
    column_groups = lax.axis_size("fy")
    owners_dev = coarse_tokens.shape[1]
    half_width = model_dim // 2
    head_dim = model_dim // HEADS
    score_scale = head_dim ** (-0.5)
    block_count = column_count // BLK
    token_shape = (frame_count, row_count, column_count, half_width)
    level_onehot = (tile_level[:, :, None] == jnp.arange(LEVELS, dtype=jnp.int32)).astype(
        jnp.float32
    )
    level_add = jnp.sum(level_onehot[:, :, :, None] * level_table[None, None, :, :], axis=2)
    summary = (coarse_tokens.astype(jnp.float32) + level_add).astype(jnp.bfloat16)
    shard_piece = lax.all_gather(summary, "fx", axis=1, tiled=True)
    piece_rows = shard_piece.shape[1]
    inside = (parent >= 0) & (parent < piece_rows)
    local_index = jnp.clip(parent, 0, piece_rows - 1)
    picked = jax.vmap(take_rows)(shard_piece, local_index)
    read_rows = jnp.where(inside[..., None], picked.astype(jnp.float32), 0.0)
    spread = jnp.broadcast_to(
        read_rows[:, :, :, None, :], (frame_count, row_count, block_count, BLK, model_dim)
    )
    residual = fine_tokens.astype(jnp.float32) + spread.reshape(
        frame_count, row_count, column_count, model_dim
    )
    inv_rms = lax.rsqrt(jnp.mean(residual * residual, axis=-1, keepdims=True) + 1e-06)
    normed_pre = residual * inv_rms
    normed = (normed_pre * norm_gain).astype(jnp.bfloat16)
    flat_normed = normed.reshape(-1, model_dim)
    projected = jnp.dot(flat_normed, qkv_weight, preferred_element_type=jnp.float32).astype(
        jnp.bfloat16
    )
    projected = projected.reshape(frame_count, row_count, column_count, 3 * model_dim)
    row_query = projected[..., 0:half_width]
    column_query = projected[..., half_width:model_dim]
    row_key = projected[..., model_dim : model_dim + half_width]
    column_key = projected[..., model_dim + half_width : 2 * model_dim]
    row_value = projected[..., 2 * model_dim : 2 * model_dim + half_width]
    column_value = projected[..., 2 * model_dim + half_width : 3 * model_dim]
    flat_cot = cotangent.reshape(-1, model_dim)
    grad_att = jnp.dot(flat_cot, out_weight.T, preferred_element_type=jnp.float32).astype(
        jnp.bfloat16
    )
    grad_att = grad_att.reshape(frame_count, row_count, column_count, model_dim)
    row_grad_out = grad_att[..., 0:half_width]
    column_grad_out = grad_att[..., half_width:model_dim]
    queries = lax.all_to_all(
        to_row_groups(row_query, row_groups), "fx", split_axis=0, concat_axis=2, tiled=True
    )
    key_rows = lax.all_to_all(
        to_row_groups(row_key, row_groups), "fx", split_axis=0, concat_axis=2, tiled=True
    )
    values = lax.all_to_all(
        to_row_groups(row_value, row_groups), "fx", split_axis=0, concat_axis=2, tiled=True
    )
    attended_rows = attend_forward(
        rows_to_batch(queries, head_dim),
        rows_to_batch(key_rows, head_dim),
        rows_to_batch(values, head_dim),
        score_scale,
        "bqhd",
        "bkhd",
        "bhqk",
    )
    row_out = lax.all_to_all(
        batch_to_rows(attended_rows), "fx", split_axis=2, concat_axis=0, tiled=True
    )
    row_out = row_out.reshape(token_shape)
    queries = lax.all_to_all(
        to_column_groups(column_query, column_groups), "fy", split_axis=2, concat_axis=1, tiled=True
    )
    key_rows = lax.all_to_all(
        to_column_groups(column_key, column_groups), "fy", split_axis=2, concat_axis=1, tiled=True
    )
    values = lax.all_to_all(
        to_column_groups(column_value, column_groups), "fy", split_axis=2, concat_axis=1, tiled=True
    )
    attended_columns = attend_forward(
        columns_to_batch(queries, head_dim),
        columns_to_batch(key_rows, head_dim),
        columns_to_batch(values, head_dim),
        score_scale,
        "fqchd",
        "fkchd",
        "fchqk",
    )
    column_out = lax.all_to_all(
        batch_to_columns(attended_columns), "fy", split_axis=1, concat_axis=2, tiled=True
    )
    column_out = column_out.reshape(token_shape)
    queries = lax.all_to_all(
        to_row_groups(row_query, row_groups), "fx", split_axis=0, concat_axis=2, tiled=True
    )
    key_rows = lax.all_to_all(
        to_row_groups(row_key, row_groups), "fx", split_axis=0, concat_axis=2, tiled=True
    )
    values = lax.all_to_all(
        to_row_groups(row_value, row_groups), "fx", split_axis=0, concat_axis=2, tiled=True
    )
    grad_rows = lax.all_to_all(
        to_row_groups(row_grad_out, row_groups), "fx", split_axis=0, concat_axis=2, tiled=True
    )
    grads = attend_backward(
        rows_to_batch(queries, head_dim),
        rows_to_batch(key_rows, head_dim),
        rows_to_batch(values, head_dim),
        rows_to_batch(grad_rows, head_dim),
        score_scale,
        "bqhd",
        "bkhd",
        "bhqk",
    )
    row_back = (
        lax.all_to_all(batch_to_rows(grads[0]), "fx", split_axis=2, concat_axis=0, tiled=True),
        lax.all_to_all(batch_to_rows(grads[1]), "fx", split_axis=2, concat_axis=0, tiled=True),
        lax.all_to_all(batch_to_rows(grads[2]), "fx", split_axis=2, concat_axis=0, tiled=True),
    )
    queries = lax.all_to_all(
        to_column_groups(column_query, column_groups), "fy", split_axis=2, concat_axis=1, tiled=True
    )
    key_rows = lax.all_to_all(
        to_column_groups(column_key, column_groups), "fy", split_axis=2, concat_axis=1, tiled=True
    )
    values = lax.all_to_all(
        to_column_groups(column_value, column_groups), "fy", split_axis=2, concat_axis=1, tiled=True
    )
    grad_columns = lax.all_to_all(
        to_column_groups(column_grad_out, column_groups),
        "fy",
        split_axis=2,
        concat_axis=1,
        tiled=True,
    )
    grads = attend_backward(
        columns_to_batch(queries, head_dim),
        columns_to_batch(key_rows, head_dim),
        columns_to_batch(values, head_dim),
        columns_to_batch(grad_columns, head_dim),
        score_scale,
        "fqchd",
        "fkchd",
        "fchqk",
    )
    column_back = (
        lax.all_to_all(batch_to_columns(grads[0]), "fy", split_axis=1, concat_axis=2, tiled=True),
        lax.all_to_all(batch_to_columns(grads[1]), "fy", split_axis=1, concat_axis=2, tiled=True),
        lax.all_to_all(batch_to_columns(grads[2]), "fy", split_axis=1, concat_axis=2, tiled=True),
    )
    attended = jnp.concatenate([row_out, column_out], axis=-1)
    flat_att = attended.reshape(-1, model_dim)
    out_proj = jnp.dot(flat_att, out_weight, preferred_element_type=jnp.float32)
    mixed = (residual + out_proj.reshape(frame_count, row_count, column_count, model_dim)).astype(
        jnp.bfloat16
    )
    grad_out_local = jnp.dot(flat_att.T, flat_cot, preferred_element_type=jnp.float32)
    pieces = []
    for which in range(3):
        pieces.append(row_back[which].reshape(token_shape))
        pieces.append(column_back[which].reshape(token_shape))
    grad_projected = jnp.concatenate(pieces, axis=-1).reshape(-1, 3 * model_dim)
    grad_normed = jnp.dot(grad_projected, qkv_weight.T, preferred_element_type=jnp.float32)
    grad_qkv_local = jnp.dot(flat_normed.T, grad_projected, preferred_element_type=jnp.float32)
    flat_pre = normed_pre.reshape(-1, model_dim)
    grad_gain_local = jnp.sum(grad_normed * flat_pre, axis=0)
    grad_pre = grad_normed * norm_gain
    flat_inv = inv_rms.reshape(-1, 1)
    grad_residual = flat_inv * (
        grad_pre - flat_pre * jnp.mean(grad_pre * flat_pre, axis=-1, keepdims=True)
    ) + flat_cot.astype(jnp.float32)
    grad_fine = grad_residual.astype(jnp.bfloat16).reshape(
        frame_count, row_count, column_count, model_dim
    )
    block_grad = (
        grad_residual.reshape(frame_count, row_count, block_count, BLK, model_dim)
        .sum(axis=3)
        .reshape(frame_count, -1, model_dim)
    )
    parent_flat = parent.reshape(frame_count, -1)
    coarse_total = owners_dev * row_groups
    segment_rows = functools.partial(jax.ops.segment_sum, num_segments=coarse_total)
    dense_sum = jax.vmap(segment_rows)(block_grad, parent_flat)
    owned_rows = jax.tree.map(
        lambda part: part.astype(jnp.float32),
        lax.psum_scatter(as_sent(dense_sum), "fx", scatter_dimension=1, tiled=True),
    )
    grad_coarse = jax.tree.map(
        lambda part: part.astype(jnp.float32), lax.psum(as_sent(owned_rows), "fy")
    )
    level_part = jnp.sum(level_onehot[:, :, :, None] * grad_coarse[:, :, None, :], axis=(0, 1))
    grad_level = lax.psum(level_part, ("dp", "fx"))
    summed = (
        lax.psum(grad_qkv_local.astype(jnp.bfloat16), ("fy", "fx")).astype(jnp.float32),
        lax.psum(grad_out_local.astype(jnp.bfloat16), ("fy", "fx")).astype(jnp.float32),
        lax.psum(grad_gain_local.astype(jnp.bfloat16), ("fy", "fx")).astype(jnp.float32),
    )
    shares = (
        lax.psum_scatter(
            summed[0].astype(jnp.bfloat16), "dp", scatter_dimension=0, tiled=True
        ).astype(jnp.float32),
        lax.psum_scatter(
            summed[1].astype(jnp.bfloat16), "dp", scatter_dimension=0, tiled=True
        ).astype(jnp.float32),
        lax.psum_scatter(
            summed[2].astype(jnp.bfloat16), "dp", scatter_dimension=0, tiled=True
        ).astype(jnp.float32),
    )
    total_tokens = (
        frame_count * row_count * column_count * lax.axis_size("dp") * column_groups * row_groups
    )
    grad_scale = 1.0 / math.sqrt(total_tokens)
    return (
        mixed,
        grad_fine,
        grad_coarse,
        shares[0] * grad_scale,
        shares[1] * grad_scale,
        shares[2] * grad_scale,
        grad_level * grad_scale,
    )


def solution(mesh):
    return jax.shard_map(
        local,
        mesh=mesh,
        in_specs=(
            P("dp", "fy", "fx", None),
            P("dp", "fy", "fx"),
            P("dp", "fx", None),
            P("dp", "fx"),
            P(),
            P(),
            P(),
            P(),
            P("dp", "fy", "fx", None),
        ),
        out_specs=(
            P("dp", "fy", "fx", None),
            P("dp", "fy", "fx", None),
            P("dp", "fx", None),
            P("dp", None),
            P("dp", None),
            P("dp"),
            P(),
        ),
        check_vma=False,
    )
```

profile of v0, /device:TPU:0, one launch (start us, length us, event | category | flops | bytes accessed | tf_op | source)
XLA Modules:
  0.0 606.6 jit_solution(17159746881032802387)
XLA Ops:
  12.2 5.3 all-to-all-start.10
  23.4 31.8 %all_gather.3 = bf16[1,512,768]{2,1,0:T(8,128)(2,1)} all-gather(bf16[1,64,768]{2,1,0:T(8,128)(2,1)S(1)} %fusion.66), channel_id=1, replica_groups=mesh['dp'=4,'fy'=4,'fx'=8] {'fx'}, dimensions={1}, use_global_device_ids=true | all-gather | bytes 884736 | tf_op jit(solution)/shard_map/all_gather | solution.py:161
  55.2 2.7 gather_fusion
  60.5 2.8 broadcast_in_dim.39
  71.1 5.4 all-to-all-start.6
  78.3 7.2 %all-to-all-done.6 = bf16[1,16,4,8,384]{4,3,1,0,2:T(8,128)(2,1)} async-done(((bf16[1,16,4,8,384]{4,3,1,0,2:T(8,128)(2,1)}), bf16[1,16,4,8,384]{4,3,1,0,2:T(8,128)(2,1)}, u32[]{:S(2)}, u32[]{:S(2)}) %all-to-all-start.6) | async-done | bytes 393248 | tf_op jit(solution)/shard_map/all_to_all | solution.py:219
  85.5 4.1 all-to-all-start.5
  91.4 7.2 %all-to-all-done.5 = bf16[1,16,4,8,384]{4,3,1,0,2:T(8,128)(2,1)} async-done(((bf16[1,16,4,8,384]{4,3,1,0,2:T(8,128)(2,1)}), bf16[1,16,4,8,384]{4,3,1,0,2:T(8,128)(2,1)}, u32[]{:S(2)}, u32[]{:S(2)}) %all-to-all-start.5) | async-done | bytes 393248 | tf_op jit(solution)/shard_map/all_to_all | solution.py:216
  98.6 13.2 %all_to_all.270 = bf16[1,16,4,8,384]{4,3,1,0,2:T(8,128)(2,1)} all-to-all(bf16[1,16,4,8,384]{4,3,1,0,2:T(8,128)(2,1)} %copy.222), channel_id=1, replica_groups=mesh['dp'=4,'fy'=4,'fx'=8] {'fy'}, dimensions={2} | all-to-all | bytes 786432 | tf_op jit(solution)/shard_map/all_to_all | solution.py:222
  111.8 12.7 %all_to_all.271 = bf16[8,2,32,384]{3,2,1,0:T(8,128)(2,1)} all-to-all(bf16[8,2,32,384]{3,2,1,0:T(8,128)(2,1)} %bitcast.260), channel_id=1, replica_groups=mesh['dp'=4,'fy'=4,'fx'=8] {'fx'}, dimensions={0} | all-to-all | bytes 786432 | tf_op jit(solution)/shard_map/all_to_all | solution.py:247
  124.5 11.1 %all_to_all.272 = bf16[8,2,32,384]{3,2,1,0:T(8,128)(2,1)} all-to-all(bf16[8,2,32,384]{3,2,1,0:T(8,128)(2,1)S(1)} %bitcast.251), channel_id=1, replica_groups=mesh['dp'=4,'fy'=4,'fx'=8] {'fx'}, dimensions={0} | all-to-all | bytes 786432 | tf_op jit(solution)/shard_map/all_to_all | solution.py:197
  135.6 4.1 all-to-all-start.1
  157.4 3.3 fusion.59
  160.7 5.8 all-to-all-start
  166.6 4.0 fusion.89
  170.5 4.6 fusion.37
  177.3 4.1 all-to-all-start.11
  181.5 3.0 convolution_convert_fusion.2
  186.7 4.6 fusion.40
  193.6 2.7 copy.283
  196.3 3.0 reshape.446
  199.3 2.7 copy.279
  202.1 3.0 reshape.443
  205.1 2.7 copy.280
  207.8 3.0 reshape.444
  213.6 3.0 reshape.445
  216.6 4.8 all-to-all-start.13
  221.4 4.5 fusion.90
  225.9 4.5 all-to-all-done.13
  230.4 4.1 all-to-all-start.15
  234.5 3.3 convolution_convert_fusion.4
  239.8 3.7 all-to-all-done.15
  243.5 6.0 all-to-all-start.14
  249.5 3.4 fusion.91
  252.9 6.6 %fusion.43 = bf16[2,6,64,256]{3,2,1,0:T(8,128)(2,1)} fusion(bf16[2,256,6,64]{1,3,2,0:T(8,128)(2,1)} %reshape.445, f32[2,6,256,256]{2,3,1,0:T(8,128)} %fusion.91, f32[2,6,256,256]{2,3,1,0:T(8,128)} %get-tuple-element.28, f32[2,6,256]{2,1,0:T(8,128)} %get-tuple-element.27), kind=kOutput, calls=%fused_computation.49 | convolution fusion | flops 106368256 | bytes 7090176 | tf_op jit(solution)/shard_map/bhqk,bkhd->bqhd/dot_general | solution.py:65
  261.4 5.7 all-to-all-start.9
  267.1 6.6 %fusion.46 = bf16[2,6,64,256]{3,2,1,0:T(8,128)(2,1)} fusion(bf16[2,256,6,64]{1,3,2,0:T(8,128)(2,1)} %reshape.444, f32[2,6,256,256]{2,3,1,0:T(8,128)} %fusion.91, f32[2,6,256,256]{2,3,1,0:T(8,128)} %get-tuple-element.28, f32[2,6,256]{2,1,0:T(8,128)} %get-tuple-element.27), kind=kOutput, calls=%fused_computation.50 | convolution fusion | flops 106368256 | bytes 7090176 | tf_op jit(solution)/shard_map/bhqk,bqhd->bkhd/dot_general | solution.py:71
  275.6 5.7 all-to-all-start.12
  307.1 3.5 all-to-all-start.7
  314.0 6.9 %all-to-all-done.7 = bf16[1,64,1,8,384]{4,3,2,0,1:T(8,128)(2,1)S(1)} async-done(((bf16[1,64,1,8,384]{4,3,2,0,1:T(8,128)(2,1)}), bf16[1,64,1,8,384]{4,3,2,0,1:T(8,128)(2,1)S(1)}, u32[]{:S(2)}, u32[]{:S(2)}) %all-to-all-start.7) | async-done | bytes 393248 | tf_op jit(solution)/shard_map/all_to_all | solution.py:234
  320.9 5.1 all-to-all-start.3
  326.1 9.4 %all-to-all-done.3 = bf16[1,2,256,384]{3,1,0,2:T(2,128)(2,1)S(1)} async-done(((bf16[1,2,256,384]{3,1,0,2:T(2,128)(2,1)}), bf16[1,2,256,384]{3,1,0,2:T(2,128)(2,1)S(1)}, u32[]{:S(2)}, u32[]{:S(2)}) %all-to-all-start.3) | async-done | bytes 393248 | tf_op jit(solution)/shard_map/all_to_all | solution.py:212
  337.4 6.4 %reduce-scatter.4.cloned.1.call-done = bf16[1,64,768]{2,1,0:T(8,128)(2,1)} async-done(((bf16[1,512,768]{2,1,0:T(8,128)(2,1)}), bf16[1,64,768]{2,1,0:T(8,128)(2,1)}) %reduce-scatter.4.cloned.1.call-update) | async-done | bytes 98320 | tf_op jit(solution)/shard_map/reduce_scatter | solution.py:331
  352.3 5.5 bitcast_convert_fusion
  359.6 10.4 %all-reduce = bf16[768]{0:T(1024)(128)(2,1)S(1)} all-reduce(bf16[768]{0:T(1024)(128)(2,1)S(1)} %get-tuple-element.7), channel_id=5, replica_groups=mesh['dp'=4,'fy'=4,'fx'=8] {'dp'}, use_global_device_ids=true, to_apply=%region_19.20.clone | all-reduce | flops 768 | bytes 3072
  370.2 62.7 %psum.42 = bf16[192]{0:T(256)(128)(2,1)S(1)} all-reduce(bf16[192]{0:T(256)(128)(2,1)S(1)} %dynamic-slice.1), channel_id=1, replica_groups=mesh['dp'=4,'fy'=4,'fx'=8] {'fy','fx'}, use_global_device_ids=true, to_apply=%region_18.19 | all-reduce | flops 192 | bytes 768 | tf_op jit(solution)/shard_map/psum | solution.py:341
  433.5 2.9 fusion.23
  439.1 154.4 %psum.39 = f32[3,768]{1,0:T(4,128)S(1)} all-reduce(f32[3,768]{1,0:T(4,128)S(1)} %multiply_reduce_fusion.4), channel_id=1, replica_groups=mesh['dp'=4,'fy'=4,'fx'=8] {'dp','fx'}, use_global_device_ids=true, to_apply=%region_21.22 | all-reduce | flops 2304 | bytes 18432 | tf_op jit(solution)/shard_map/psum | solution.py:337
  (169 shorter events, 106.0 us)
Async XLA Ops:
  8.0 59.0 %copy-start = (bf16[768,2304]{1,0:T(8,128)(2,1)S(1)}, bf16[768,2304]{1,0:T(8,128)(2,1)}, u32[]{:S(2)}) copy-start(bf16[768,2304]{1,0:T(8,128)(2,1)} %param.15) | copy-start | bytes 10616836
  10.5 7.0 %copy-start.23 = (s32[1,16,8]{1,2,0:T(8,128)S(1)}, s32[1,16,8]{1,2,0:T(8,128)}, u32[]{:S(2)}) copy-start(s32[1,16,8]{1,2,0:T(8,128)} %param.10) | copy-start | bytes 1540
  10.5 7.5 %copy-start.27 = (s32[1,64]{1,0:T(1,128)S(1)}, s32[1,64]{1,0:T(1,128)}, u32[]{:S(2)}) copy-start(s32[1,64]{1,0:T(1,128)} %param.12) | copy-start | bytes 772
  12.2 58.9 %all-to-all-start.10 = ((bf16[1,16,4,8,384]{4,3,1,0,2:T(8,128)(2,1)}), bf16[1,16,4,8,384]{4,3,1,0,2:T(8,128)(2,1)}, u32[]{:S(2)}, u32[]{:S(2)}) async-start(bf16[1,16,4,8,384]{4,3,1,0,2:T(8,128)(2,1)} %copy.239), calls=%async_computation.10 | async-start | bytes 786432 | tf_op jit(solution)/shard_map/all_to_all | solution.py:274
  63.3 2.1 copy-start.2
  63.3 2.3 copy-start.12
  63.3 2.3 copy-start.25
  67.0 2.0 copy-start.21
  71.1 14.4 %all-to-all-start.6 = ((bf16[1,16,4,8,384]{4,3,1,0,2:T(8,128)(2,1)}), bf16[1,16,4,8,384]{4,3,1,0,2:T(8,128)(2,1)}, u32[]{:S(2)}, u32[]{:S(2)}) async-start(bf16[1,16,4,8,384]{4,3,1,0,2:T(8,128)(2,1)} %copy.224), calls=%async_computation.6 | async-start | bytes 786432 | tf_op jit(solution)/shard_map/all_to_all | solution.py:219
  85.5 13.1 %all-to-all-start.5 = ((bf16[1,16,4,8,384]{4,3,1,0,2:T(8,128)(2,1)}), bf16[1,16,4,8,384]{4,3,1,0,2:T(8,128)(2,1)}, u32[]{:S(2)}, u32[]{:S(2)}) async-start(bf16[1,16,4,8,384]{4,3,1,0,2:T(8,128)(2,1)} %copy.223), calls=%async_computation.5 | async-start | bytes 786432 | tf_op jit(solution)/shard_map/all_to_all | solution.py:216
  98.6 25.9 %copy-start.14 = (bf16[1,16,32,384]{3,2,1,0:T(8,128)(2,1)S(1)}, bf16[1,16,32,384]{3,2,1,0:T(8,128)(2,1)}, u32[]{:S(2)}) copy-start(bf16[1,16,32,384]{3,2,1,0:T(8,128)(2,1)} %get-tuple-element.15) | copy-start | bytes 1179652
  135.6 25.2 %all-to-all-start.1 = ((bf16[8,2,32,384]{3,2,1,0:T(8,128)(2,1)}), bf16[8,2,32,384]{3,2,1,0:T(8,128)(2,1)}, u32[]{:S(2)}, u32[]{:S(2)}) async-start(bf16[8,2,32,384]{3,2,1,0:T(8,128)(2,1)} %bitcast.250), calls=%async_computation.1 | async-start | bytes 786432 | tf_op jit(solution)/shard_map/all_to_all | solution.py:194
  160.7 16.6 %all-to-all-start = ((bf16[8,2,32,384]{3,2,1,0:T(8,128)(2,1)}), bf16[8,2,32,384]{3,2,1,0:T(8,128)(2,1)}, u32[]{:S(2)}, u32[]{:S(2)}) async-start(bf16[8,2,32,384]{3,2,1,0:T(8,128)(2,1)} %bitcast.249), calls=%async_computation | async-start | bytes 786432 | tf_op jit(solution)/shard_map/all_to_all | solution.py:200
  177.3 39.3 %all-to-all-start.11 = ((bf16[1,64,1,8,384]{4,3,2,0,1:T(8,128)(2,1)}), bf16[1,64,1,8,384]{4,3,2,0,1:T(8,128)(2,1)}, u32[]{:S(2)}, u32[]{:S(2)}) async-start(bf16[1,64,1,8,384]{4,3,2,0,1:T(8,128)(2,1)} %copy.244), calls=%async_computation.11 | async-start | bytes 786432 | tf_op jit(solution)/shard_map/all_to_all | solution.py:292
  216.6 13.8 %all-to-all-start.13 = ((bf16[1,64,1,8,384]{4,3,2,0,1:T(8,128)(2,1)}), bf16[1,64,1,8,384]{4,3,2,0,1:T(8,128)(2,1)}, u32[]{:S(2)}, u32[]{:S(2)}) async-start(bf16[1,64,1,8,384]{4,3,2,0,1:T(8,128)(2,1)} %copy.253), calls=%async_computation.13 | async-start | bytes 786432 | tf_op jit(solution)/shard_map/all_to_all | solution.py:293
  230.4 13.1 %all-to-all-start.15 = ((bf16[1,64,1,8,384]{4,3,2,0,1:T(8,128)(2,1)}), bf16[1,64,1,8,384]{4,3,2,0,1:T(8,128)(2,1)}, u32[]{:S(2)}, u32[]{:S(2)}) async-start(bf16[1,64,1,8,384]{4,3,2,0,1:T(8,128)(2,1)} %copy.262), calls=%async_computation.15 | async-start | bytes 786432 | tf_op jit(solution)/shard_map/all_to_all | solution.py:294
  243.5 17.9 %all-to-all-start.14 = ((bf16[1,2,256,384]{3,1,0,2:T(2,128)(2,1)}), bf16[1,2,256,384]{3,1,0,2:T(2,128)(2,1)}, u32[]{:S(2)}, u32[]{:S(2)}) async-start(bf16[1,2,256,384]{3,1,0,2:T(2,128)(2,1)} %copy.257), calls=%async_computation.14 | async-start | bytes 786432 | tf_op jit(solution)/shard_map/all_to_all | solution.py:263
  261.4 14.2 %all-to-all-start.9 = ((bf16[1,2,256,384]{3,1,0,2:T(2,128)(2,1)}), bf16[1,2,256,384]{3,1,0,2:T(2,128)(2,1)}, u32[]{:S(2)}, u32[]{:S(2)}) async-start(bf16[1,2,256,384]{3,1,0,2:T(2,128)(2,1)} %copy.236), calls=%async_computation.9 | async-start | bytes 786432 | tf_op jit(solution)/shard_map/all_to_all | solution.py:261
  275.6 16.9 %all-to-all-start.12 = ((bf16[1,2,256,384]{3,1,0,2:T(2,128)(2,1)}), bf16[1,2,256,384]{3,1,0,2:T(2,128)(2,1)}, u32[]{:S(2)}, u32[]{:S(2)}) async-start(bf16[1,2,256,384]{3,1,0,2:T(2,128)(2,1)} %copy.248), calls=%async_computation.12 | async-start | bytes 786432 | tf_op jit(solution)/shard_map/all_to_all | solution.py:262
  281.3 62.5 %reduce-scatter.4.cloned.1.call-start = ((), (), s32[]{:S(2)}) async-start(), calls=%async_computation.19 | async-start | bytes 884736 | tf_op jit(solution)/shard_map/reduce_scatter | solution.py:331
  292.5 1.2 copy-start.9
  292.5 1.3 copy-start.17
  293.6 1.1 copy-start.16
  293.6 1.1 copy-start.7
  293.7 1.2 copy-start.5
  293.7 1.2 copy-start.15
  293.8 1.7 copy-start.4
  293.8 1.7 copy-start.26
  295.5 2.2 copy-start.19
  302.3 1.5 copy-start.11
  302.4 1.5 copy-start.24
  305.9 4.6 copy-start.18
  306.0 4.6 copy-start.29
  307.1 13.8 %all-to-all-start.7 = ((bf16[1,64,1,8,384]{4,3,2,0,1:T(8,128)(2,1)}), bf16[1,64,1,8,384]{4,3,2,0,1:T(8,128)(2,1)S(1)}, u32[]{:S(2)}, u32[]{:S(2)}) async-start(bf16[1,64,1,8,384]{4,3,2,0,1:T(8,128)(2,1)} %copy.229), calls=%async_computation.7 | async-start | bytes 786432 | tf_op jit(solution)/shard_map/all_to_all | solution.py:234
  314.0 21.6 %copy-start.20 = (bf16[1,16,32,768]{3,2,1,0:T(8,128)(2,1)S(1)}, bf16[1,16,32,768]{3,2,1,0:T(8,128)(2,1)}, u32[]{:S(2)}) copy-start(bf16[1,16,32,768]{3,2,1,0:T(8,128)(2,1)} %param.17) | copy-start | bytes 2359300
  320.9 14.6 %all-to-all-start.3 = ((bf16[1,2,256,384]{3,1,0,2:T(2,128)(2,1)}), bf16[1,2,256,384]{3,1,0,2:T(2,128)(2,1)S(1)}, u32[]{:S(2)}, u32[]{:S(2)}) async-start(bf16[1,2,256,384]{3,1,0,2:T(2,128)(2,1)} %copy.219), calls=%async_computation.3 | async-start | bytes 786432 | tf_op jit(solution)/shard_map/all_to_all | solution.py:212
  326.0 110.5 %all-reduce.5.cloned.1.call-start = ((), (), s32[]{:S(2)}) async-start(), calls=%async_computation.20 | async-start | bytes 196608 | tf_op jit(solution)/shard_map/psum | solution.py:334
  335.5 8.3 %copy-start.10 = (bf16[8,1,2,32,384]{4,3,2,0,1:T(8,128)(2,1)S(1)}, bf16[8,1,2,32,384]{4,3,2,0,1:T(8,128)(2,1)}, u32[]{:S(2)}) copy-start(bf16[8,1,2,32,384]{4,3,2,0,1:T(8,128)(2,1)} %copy.238) | copy-start | bytes 1179652
  337.4 9.6 %copy-start.8 = (bf16[8,1,2,32,384]{4,3,2,0,1:T(8,128)(2,1)S(1)}, bf16[8,1,2,32,384]{4,3,2,0,1:T(8,128)(2,1)}, u32[]{:S(2)}) copy-start(bf16[8,1,2,32,384]{4,3,2,0,1:T(8,128)(2,1)} %copy-done.7) | copy-start | bytes 1179652
  343.8 94.2 %reduce-scatter.8.cloned.1.call-start = ((), (), s32[]{:S(2)}) async-start(), calls=%async_computation.22 | async-start | bytes 1474560 | tf_op jit(solution)/shard_map/reduce_scatter | solution.py:347
  344.8 4.9 copy-start.6
  344.8 93.2 %reduce-scatter.6.cloned.1.call-start = ((), (), s32[]{:S(2)}) async-start(), calls=%async_computation.21 | async-start | bytes 4423680 | tf_op jit(solution)/shard_map/reduce_scatter | solution.py:344
  346.9 5.3 copy-start.22
  357.8 0.7 copy-start.28
  357.8 75.7 %copy-start.3 = (f32[1,16,32,768]{3,2,1,0:T(8,128)S(1)}, f32[1,16,32,768]{3,2,1,0:T(8,128)}, u32[]{:S(2)}) copy-start(f32[1,16,32,768]{3,2,1,0:T(8,128)} %broadcast_in_dim.39) | copy-start | bytes 4718596
  357.8 75.7 %copy-start.13 = (bf16[1,16,32,768]{3,2,1,0:T(8,128)(2,1)S(1)}, bf16[1,16,32,768]{3,2,1,0:T(8,128)(2,1)}, u32[]{:S(2)}) copy-start(bf16[1,16,32,768]{3,2,1,0:T(8,128)(2,1)} %param.9) | copy-start | bytes 2359300
  357.8 236.3 %all-reduce.7.cloned.1.call-start = ((), (), s32[]{:S(2)}) async-start(), calls=%async_computation.23 | async-start | bytes 2359296 | tf_op jit(solution)/shard_map/psum | solution.py:339
  594.1 4.5 copy-start.1
Sparse Core Ops, SparseCore 0:
  303.5 40.2 reduce-scatter.3
  346.3 38.8 all-reduce.4
Sparse Core Ops, SparseCore 1:
  347.3 22.9 reduce-scatter.7
  372.6 41.2 reduce-scatter.5
  438.1 101.2 all-reduce.6
where the time goes:
time: 618 us; the launch traced here: 607 us
  blocking collectives  296 us (48%)
  local copies, waits for them, and re-layouts  97.6 us (16%)
  matrix products  65.2 us (11%)
  starting transfers between devices  64 us (10%)
  waiting for transfers between devices  45.4 us (7%)
  other arithmetic  20.7 us (3%)
  between operations  17.3 us (3%)
    psum x1, blocking collectives, local(): grad_level = lax.psum(level_part, ('dp', 'fx'))  154 us
    psum x1, blocking collectives, local(): lax.psum(grad_gain_local.astype(jnp.bfloat16), ('fy', 'fx'))  62.7 us
    all_gather x1, blocking collectives, local(): shard_piece = lax.all_gather(summary, 'fx', axis=1, tiled=True)  31.8 us
    reshape x8, local copies, waits for them, and re-layouts, rows_to_batch(): return tensor.reshape(tensor.shape[1], tensor.shape[2], -1, head_dim)  23 us
    another operation x7, local copies, waits for them, and re-layouts  17.7 us
    all_to_all x1, blocking collectives, local(): lax.all_to_all(to_column_groups(column_value, column_groups), 'fy', split...  13.2 us
    all_to_all x1, blocking collectives, local(): lax.all_to_all(to_row_groups(row_grad_out, row_groups), 'fx', split_axis=...  12.7 us
  transfers between devices with their start and end apart: 18, of which 7 were waited for; matrix products, arithmetic and copies ran while one was open for 27% of the time, Pallas kernels for 0%

commit v1 on v0

v1 whole, which is shorter than its diff:
```python
import functools
import math

import jax
import jax.numpy as jnp
from jax import lax
from jax.experimental import pallas as pl
from jax.experimental.pallas import tpu as pltpu
from jax.sharding import PartitionSpec as P

HEADS = 12
BLK = 4
LEVELS = 3
MESH = pl.DeviceIdType.MESH
F32 = jnp.float32
BF16 = jnp.bfloat16
FXP = [(a, b) for a in range(2) for b in range(4) if (a, b) != (0, 0)]
FYP = [(0, 1), (1, 0), (1, 1)]
YZP = [(a, b) for a in range(4) for b in range(4) if (a, b) != (0, 0)]
LANES = 128


def dims(a, b, ca, cb):
    return lax.dot_general(a, b, (((ca,), (cb,)), ((), ())), preferred_element_type=F32)


class Place:
    def __init__(self):
        self.dp = lax.axis_index("dp")
        self.fy = lax.axis_index("fy")
        self.fx = lax.axis_index("fx")
        self.zh, self.core = self.fy // 2, self.fy % 2
        self.zl, self.y = self.fx // 4, self.fx % 4
        self.z = self.zh * 2 + self.zl

    def fx_at(self, a, b):
        return lax.rem(self.zl + a, 2) * 4 + lax.rem(self.y + b, 4)

    def fy_at(self, a, c):
        return lax.rem(self.zh + a, 2) * 2 + lax.rem(self.core + c, 2)

    def yz(self, a, b):
        z, y = lax.rem(self.z + a, 4), lax.rem(self.y + b, 4)
        dev = {"fy": (z // 2) * 2 + self.core, "fx": (z % 2) * 4 + y}
        return dev, z * 4 + y

    def dp_at(self, d):
        return lax.rem(self.dp + d, 4)


def rcopy(src, dst, ss, rs, dev):
    return pltpu.make_async_remote_copy(
        src_ref=src, dst_ref=dst, send_sem=ss, recv_sem=rs, device_id=dev, device_id_type=MESH
    )


def greet(devs):
    barrier = pltpu.get_barrier_semaphore()
    for dev in devs:
        pl.semaphore_signal(barrier, inc=1, device_id=dev, device_id_type=MESH)
    pl.semaphore_wait(barrier, len(devs))


def onehot(cond):
    return jnp.where(cond, 1.0, 0.0).astype(BF16)


def to_columns(rows, cols):
    n = rows * cols
    new = lax.broadcasted_iota(jnp.int32, (n, n), 0)
    old = lax.broadcasted_iota(jnp.int32, (n, n), 1)
    return onehot(old == lax.rem(new, rows) * cols + new // rows)


def front_kernel(
    rows, cols, fine, cot, ptok, coarse, level, table, gain, wo,
    rown, rowd, coln, cold, res, lv,
    tab, sn, sd, snc, sdc,
    ag_s, ag_r, fw_s, fw_r, row_s, row_r, col_s, col_r, loc,
):
    at = Place()
    n, width = fine.shape
    half = width // 2
    own = coarse.shape[0]
    part = own // 2
    mine = pl.ds(at.fx * own, own)
    lev = level[...]
    add = jnp.where(
        lev == 0, table[0:1, :], jnp.where(lev == 1, table[1:2, :], table[2:3, :])
    )
    tab[mine, 0:width] = (coarse[...].astype(F32) + add).astype(BF16)
    lane = lax.broadcasted_iota(jnp.int32, (own, LANES), 1)
    tab[mine, width : width + LANES] = onehot(lane == lev + 1)
    fx_dev = [{"fx": at.fx_at(a, b)} for a, b in FXP]
    fy_dev = [{"fy": at.fy_at(a, c)} for a, c in FYP]
    greet(fx_dev + fy_dev)

    def chunk(owner, core):
        return tab.at[pl.ds(owner * own + core * part, part)]

    sent = []

    def go(c):
        c.start()
        sent.append(c)

    for i, dev in enumerate(fx_dev):
        go(rcopy(chunk(at.fx, at.core), chunk(at.fx, at.core), ag_s.at[i], ag_r.at[i], dev))

    def scatter(kind, src_row, dst_row, src_col, dst_col):
        rr, cc = src_row.shape[0] // 8, src_col.shape[0] // 4
        for i, (a, b) in enumerate(FXP):
            go(rcopy(
                src_row.at[pl.ds(at.fx_at(a, b) * rr, rr)], dst_row.at[:, pl.ds(at.fx * cols, cols)],
                row_s.at[kind, i], row_r.at[kind, i], fx_dev[i],
            ))
        for i, (a, c) in enumerate(FYP):
            go(rcopy(
                src_col.at[pl.ds(at.fy_at(a, c) * cc, cc)], dst_col.at[:, pl.ds(at.fy * rows, rows)],
                col_s.at[kind, i], col_r.at[kind, i], fy_dev[i],
            ))
        keep_row = pltpu.make_async_copy(
            src_row.at[pl.ds(at.fx * rr, rr)], dst_row.at[:, pl.ds(at.fx * cols, cols)], loc.at[kind, 0]
        )
        keep_col = pltpu.make_async_copy(
            src_col.at[pl.ds(at.fy * cc, cc)], dst_col.at[:, pl.ds(at.fy * rows, rows)], loc.at[kind, 1]
        )
        keep_row.start()
        keep_col.start()
        return [keep_row, keep_col]

    perm = to_columns(rows, cols)
    d = dims(cot[...], wo[...], 1, 1).astype(BF16)
    sd[...] = d[:, 0:half].reshape(rows, cols, half)
    sdc[...] = dims(perm, d[:, half:width], 1, 0).astype(BF16).reshape(cols, rows, half)
    kept = scatter(1, sd, rowd, sdc, cold)
    partner = {"fy": at.fy_at(0, 1)}
    for i, (a, b) in enumerate(FXP):
        src = at.fx_at(a, 4 - b)
        rcopy(chunk(src, at.core), chunk(src, at.core), ag_s.at[i], ag_r.at[i], fx_dev[i]).wait_recv()
        go(rcopy(chunk(src, at.core), chunk(src, at.core), fw_s.at[i], fw_r.at[i], partner))
    for i, (a, b) in enumerate(FXP):
        src = at.fx_at(a, 4 - b)
        rcopy(chunk(src, 1 - at.core), chunk(src, 1 - at.core), fw_s.at[i], fw_r.at[i], partner).wait_recv()
    pick = onehot(lax.broadcasted_iota(jnp.int32, (n, tab.shape[0]), 1) == ptok[...])
    read = dims(pick, tab[...], 1, 0)
    lv[...] = read[:, width : width + LANES].astype(BF16)
    residual = fine[...].astype(F32) + read[:, 0:width]
    res[...] = residual
    inv = lax.rsqrt(jnp.mean(residual * residual, axis=-1, keepdims=True) + 1e-06)
    normed = (residual * inv * gain[...]).astype(BF16)
    sn[...] = normed.reshape(rows, cols, width)
    snc[...] = dims(perm, normed, 1, 0).astype(BF16).reshape(cols, rows, width)
    kept += scatter(0, sn, rown, snc, coln)
    for kind, (dst_row, dst_col) in enumerate(((rown, coln), (rowd, cold))):
        for i, (a, b) in enumerate(FXP):
            ref = dst_row.at[:, pl.ds(at.fx_at(a, 4 - b) * cols, cols)]
            rcopy(ref, ref, row_s.at[kind, i], row_r.at[kind, i], fx_dev[i]).wait_recv()
        for i, (a, c) in enumerate(FYP):
            ref = dst_col.at[:, pl.ds(at.fy_at(a, c) * rows, rows)]
            rcopy(ref, ref, col_s.at[kind, i], col_r.at[kind, i], fy_dev[i]).wait_recv()
    for c in sent:
        c.wait_send()
    for c in kept:
        c.wait()


def front(fine, cot, ptok, coarse, level, table, gain, wo, rows, cols):
    n, width = fine.shape
    half = width // 2
    dma = pltpu.SemaphoreType.DMA
    wide = coarse.shape[0] * 8
    return pl.pallas_call(
        functools.partial(front_kernel, rows, cols),
        name="front",
        out_shape=[
            jax.ShapeDtypeStruct((rows // 8, cols * 8, width), BF16),
            jax.ShapeDtypeStruct((rows // 8, cols * 8, half), BF16),
            jax.ShapeDtypeStruct((cols // 4, rows * 4, width), BF16),
            jax.ShapeDtypeStruct((cols // 4, rows * 4, half), BF16),
            jax.ShapeDtypeStruct((n, width), F32),
            jax.ShapeDtypeStruct((n, LANES), BF16),
        ],
        in_specs=[pl.BlockSpec(memory_space=pltpu.VMEM)] * 8,
        out_specs=[pl.BlockSpec(memory_space=pltpu.VMEM)] * 6,
        scratch_shapes=[
            pltpu.VMEM((wide, width + LANES), BF16),
            pltpu.VMEM((rows, cols, width), BF16),
            pltpu.VMEM((rows, cols, half), BF16),
            pltpu.VMEM((cols, rows, width), BF16),
            pltpu.VMEM((cols, rows, half), BF16),
            dma((7,)), dma((7,)), dma((7,)), dma((7,)),
            dma((2, 7)), dma((2, 7)), dma((2, 3)), dma((2, 3)), dma((2, 2)),
        ],
        compiler_params=pltpu.CompilerParams(
            collective_id=0, has_side_effects=True, vmem_limit_bytes=48 << 20
        ),
    )(fine, cot, ptok, coarse, level, table, gain, wo)


def attend(q, k, v, d, scale, mask):
    size, lanes = q.shape
    first = lax.broadcasted_iota(jnp.int32, (size, lanes), 1) < lanes // 2

    def stack(t):
        zero = jnp.zeros_like(t)
        return jnp.concatenate([jnp.where(first, t, zero), jnp.where(first, zero, t)], axis=0)

    def join(t):
        return jnp.where(first, t[:size], t[size:])

    qs = stack((q.astype(F32) * scale).astype(BF16))
    ds_ = stack(d)
    s = dims(qs, k, 1, 1)
    if mask is not None:
        s = jnp.where(mask, s, -1e30)
    e = jnp.exp(s - jnp.max(s, axis=-1, keepdims=True))
    w = e * (1.0 / jnp.sum(e, axis=-1, keepdims=True))
    wb = w.astype(BF16)
    out = join(dims(wb, v, 1, 0)).astype(BF16)
    dv = dims(wb, ds_, 0, 0).astype(BF16)
    gw = dims(ds_, v, 1, 1)
    inner = jnp.sum(w * gw, axis=-1, keepdims=True)
    gs = (w * (gw - inner)).astype(BF16)
    dq = (join(dims(gs, k, 1, 0)) * scale).astype(BF16)
    dk = dims(gs, qs, 0, 0).astype(BF16)
    return out, dq, dk, dv


def attention_kernel(
    scale, col_rows, rown, rowd, coln, cold, wq, orow, gnr, ocol, gnc, w2, qkv, grads
):
    half = rowd.shape[1]
    for which, (x, d, out, gn) in enumerate(((rown, rowd, orow, gnr), (coln, cold, ocol, gnc))):
        for j in range(3):
            c0 = (2 * j + which) * half
            qkv[:, j * half : (j + 1) * half] = dims(x[...], wq[:, c0 : c0 + half], 1, 0).astype(BF16)
        size = 256 if which == 0 else 2 * col_rows
        mask = None
        if which:
            i = lax.broadcasted_iota(jnp.int32, (2 * size, size), 0)
            j = lax.broadcasted_iota(jnp.int32, (2 * size, size), 1)
            mask = lax.rem(i, size) // col_rows == j // col_rows

        def one(u, _, d=d, out=out, size=size, mask=mask):
            t = pl.ds(pl.multiple_of(u * size, size), size)
            for p in range(half // LANES):
                c = p * LANES
                q, k, v = (qkv[t, j * half + c : j * half + c + LANES] for j in range(3))
                o, dq, dk, dv = attend(q, k, v, d[t, c : c + LANES], scale, mask)
                out[t, c : c + LANES] = o
                for j, g in enumerate((dq, dk, dv)):
                    grads[t, j * half + c : j * half + c + LANES] = g
            return 0

        lax.fori_loop(0, x.shape[0] // size, one, 0)
        total = None
        for j in range(3):
            c0 = (2 * j + which) * half
            g = grads[:, j * half : (j + 1) * half]
            back = dims(g, wq[:, c0 : c0 + half], 1, 1)
            total = back if total is None else total + back
            w2[which, :, j * half : (j + 1) * half] = dims(x[...], g, 0, 0).astype(BF16)
        gn[...] = total.astype(BF16)


def attention(rown, rowd, coln, cold, wq, scale, col_rows):
    n, width = rown.shape
    half = width // 2
    return pl.pallas_call(
        functools.partial(attention_kernel, scale, col_rows),
        name="attention",
        out_shape=[
            jax.ShapeDtypeStruct((n, half), BF16),
            jax.ShapeDtypeStruct((n, width), BF16),
            jax.ShapeDtypeStruct((n, half), BF16),
            jax.ShapeDtypeStruct((n, width), BF16),
            jax.ShapeDtypeStruct((2, width, 3 * half), BF16),
        ],
        in_specs=[pl.BlockSpec(memory_space=pltpu.VMEM)] * 5,
        out_specs=[pl.BlockSpec(memory_space=pltpu.VMEM)] * 5,
        scratch_shapes=[pltpu.VMEM((n, 3 * half), BF16), pltpu.VMEM((n, 3 * half), BF16)],
        compiler_params=pltpu.CompilerParams(vmem_limit_bytes=48 << 20),
    )(rown, rowd, coln, cold, wq)


class Reduce:
    @staticmethod
    def scratch(rows, nb):
        dma = pltpu.SemaphoreType.DMA
        piece = -(-(rows * nb // 16) // 16) * 16
        return [
            pltpu.VMEM((4 * rows, nb * LANES), BF16),
            pltpu.VMEM((3, rows, nb * LANES), BF16),
            pltpu.VMEM((3, rows, nb * LANES), BF16),
            pltpu.VMEM((rows, nb * LANES), F32),
            pltpu.VMEM((16 * piece, LANES), BF16),
            pltpu.VMEM((15, piece, LANES), BF16),
            pltpu.VMEM((2, 16 * piece, LANES), BF16),
            dma((2,)), dma((2,)), dma((3,)), dma((3,)), dma((15,)), dma((15,)), dma((15,)), dma((15,)),
        ]

    def __init__(self, at, refs, rows, nb):
        (self.cx, self.xs, self.xr, self.acc, self.p16, self.r16, self.ag,
         self.c_s, self.c_r, self.x_s, self.x_r, self.r_s, self.r_r, self.g_s, self.g_r) = refs
        self.at, self.rows, self.nb = at, rows, nb
        self.piece = self.r16.shape[1]
        self.partner = {"fy": at.fy_at(0, 1)}
        self.sent = []

    def go(self, c):
        c.start()
        self.sent.append(c)
        return c

    def swap(self, src):
        self.first = self.go(rcopy(src, self.cx, self.c_s.at[0], self.c_r.at[0], self.partner))

    def along_x(self, mine):
        self.first.wait_recv()
        for d in (2, 1, 3, 0):
            i = self.at.dp_at(d)
            block = pl.ds(pl.multiple_of(i * self.rows, self.rows), self.rows)
            value = mine(block) + self.cx[block, :].astype(F32)
            if d == 0:
                self.acc[...] = value
            else:
                self.xs[d - 1] = value.astype(BF16)
                self.go(rcopy(
                    self.xs.at[d - 1], self.xr.at[d - 1], self.x_s.at[d - 1], self.x_r.at[d - 1], {"dp": i}
                ))

    def scatter_yz(self):
        for d in range(3):
            rcopy(self.xs.at[d], self.xr.at[d], self.x_s.at[d], self.x_r.at[d], {"dp": self.at.dp}).wait_recv()
        rows = self.rows
        for b in range(self.nb):
            lanes = slice(b * LANES, (b + 1) * LANES)
            value = self.acc[:, lanes]
            for d in range(3):
                value = value + self.xr[d, :, lanes].astype(F32)
            self.p16[b * rows : (b + 1) * rows, :] = value.astype(BF16)
        used = self.nb * rows
        if used < self.p16.shape[0]:
            self.p16[used:, :] = jnp.zeros((self.p16.shape[0] - used, LANES), BF16)
        for i, (a, b) in enumerate(YZP):
            dev, q = self.at.yz(a, b)
            self.go(rcopy(self.p16.at[self.slot(q)], self.r16.at[i], self.r_s.at[i], self.r_r.at[i], dev))

    def slot(self, q):
        return pl.ds(pl.multiple_of(q * self.piece, self.piece), self.piece)

    def gather_yz(self):
        at = self.at
        _, q = at.yz(0, 0)
        value = self.p16[self.slot(q), :].astype(F32)
        for i in range(15):
            dev, _ = at.yz(*YZP[i])
            rcopy(self.r16.at[i], self.r16.at[i], self.r_s.at[i], self.r_r.at[i], dev).wait_recv()
            value = value + self.r16[i].astype(F32)
        self.ag[at.core, self.slot(q), :] = value.astype(BF16)
        src = self.ag.at[at.core, self.slot(q)]
        for i, (a, b) in enumerate(YZP):
            dev, _ = at.yz(a, b)
            self.go(rcopy(src, src, self.g_s.at[i], self.g_r.at[i], dev))

    def swap_back(self):
        at = self.at
        for i, (a, b) in enumerate(YZP):
            dev, q = at.yz(4 - a, 4 - b)
            ref = self.ag.at[at.core, self.slot(q)]
            rcopy(ref, ref, self.g_s.at[i], self.g_r.at[i], dev).wait_recv()
        ref = self.ag.at[at.core]
        self.go(rcopy(ref, ref, self.c_s.at[1], self.c_r.at[1], self.partner))

    def finish(self):
        ref = self.ag.at[1 - self.at.core]
        rcopy(ref, ref, self.c_s.at[1], self.c_r.at[1], self.partner).wait_recv()

    def block(self, half, b):
        return self.ag[half, b * self.rows : (b + 1) * self.rows, :].astype(F32)


def back_kernel(
    rows, cols, grad_scale, orow, gnr, ocol, gnc, w2,
    orow_t, gnr_t, ocol_t, gnc_t, gq,
    row_s, row_r, col_s, col_r, loc, *red,
):
    at = Place()
    width = gnr.shape[2]
    half = width // 2
    fx_dev = [{"fx": at.fx_at(a, b)} for a, b in FXP]
    fy_dev = [{"fy": at.fy_at(a, c)} for a, c in FYP]
    dp_dev = [{"dp": at.dp_at(d)} for d in (1, 2, 3)]
    greet(fx_dev + fy_dev + extra_devs(at) + dp_dev)
    sent = []
    weights = Reduce(at, red, width // 4, 3 * half // LANES)
    weights.swap(w2.at[1 - at.core])
    kinds = ((orow, orow_t, ocol, ocol_t), (gnr, gnr_t, gnc, gnc_t))
    kept = []
    for kind, (src_row, dst_row, src_col, dst_col) in enumerate(kinds):
        rr, cc = src_row.shape[0], src_col.shape[0]
        for i, (a, b) in enumerate(FXP):
            c = rcopy(
                src_row.at[:, pl.ds(at.fx_at(a, b) * cols, cols)], dst_row.at[pl.ds(at.fx * rr, rr)],
                row_s.at[kind, i], row_r.at[kind, i], fx_dev[i],
            )
            c.start()
            sent.append(c)
        for i, (a, b) in enumerate(FYP):
            c = rcopy(
                src_col.at[:, pl.ds(at.fy_at(a, b) * rows, rows)], dst_col.at[pl.ds(at.fy * cc, cc)],
                col_s.at[kind, i], col_r.at[kind, i], fy_dev[i],
            )
            c.start()
            sent.append(c)
        for i, (src, dst) in enumerate((
            (src_row.at[:, pl.ds(at.fx * cols, cols)], dst_row.at[pl.ds(at.fx * rr, rr)]),
            (src_col.at[:, pl.ds(at.fy * rows, rows)], dst_col.at[pl.ds(at.fy * cc, cc)]),
        )):
            c = pltpu.make_async_copy(src, dst, loc.at[kind, i])
            c.start()
            kept.append(c)
    weights.along_x(lambda block: w2[at.core, block, :].astype(F32))
    weights.scatter_yz()
    weights.gather_yz()
    weights.swap_back()
    weights.finish()
    for h in range(2):
        for j in range(3):
            for b in range(half // LANES):
                c0 = (2 * j + h) * half + b * LANES
                gq[:, c0 : c0 + LANES] = weights.block(h, j * (half // LANES) + b) * grad_scale
    for kind, (src_row, dst_row, src_col, dst_col) in enumerate(kinds):
        rr, cc = src_row.shape[0], src_col.shape[0]
        for i, (a, b) in enumerate(FXP):
            ref = dst_row.at[pl.ds(at.fx_at(a, 4 - b) * rr, rr)]
            rcopy(ref, ref, row_s.at[kind, i], row_r.at[kind, i], fx_dev[i]).wait_recv()
        for i, (a, b) in enumerate(FYP):
            ref = dst_col.at[pl.ds(at.fy_at(a, b) * cc, cc)]
            rcopy(ref, ref, col_s.at[kind, i], col_r.at[kind, i], fy_dev[i]).wait_recv()
    for c in sent + weights.sent:
        c.wait_send()
    for c in kept:
        c.wait()


def extra_devs(at):
    return [
        {"fy": at.fy_at(1, 0), "fx": at.fx_at(a, b)} for a, b in FXP
    ]


def back(orow, gnr, ocol, gnc, w2, rows, cols, grad_scale):
    width = gnr.shape[2]
    half = width // 2
    dma = pltpu.SemaphoreType.DMA
    return pl.pallas_call(
        functools.partial(back_kernel, rows, cols, grad_scale),
        name="back",
        out_shape=[
            jax.ShapeDtypeStruct((rows, cols, half), BF16),
            jax.ShapeDtypeStruct((rows, cols, width), BF16),
            jax.ShapeDtypeStruct((cols, rows, half), BF16),
            jax.ShapeDtypeStruct((cols, rows, width), BF16),
            jax.ShapeDtypeStruct((width // 4, 6 * half), F32),
        ],
        in_specs=[pl.BlockSpec(memory_space=pltpu.VMEM)] * 5,
        out_specs=[pl.BlockSpec(memory_space=pltpu.VMEM)] * 5,
        scratch_shapes=[
            dma((2, 7)), dma((2, 7)), dma((2, 3)), dma((2, 3)), dma((2, 2)),
            *Reduce.scratch(width // 4, 3 * half // LANES),
        ],
        compiler_params=pltpu.CompilerParams(
            collective_id=1, has_side_effects=True, vmem_limit_bytes=48 << 20
        ),
    )(orow, gnr, ocol, gnc, w2)


def post_kernel(
    rows, cols, grad_scale, orow, gnr, ocol, gnc, res, cot, ptok, lv, gain, wo,
    mixed, gfine, gcoarse, gout, small,
    att, go_out, go_own, co_out, co_in, co_own, cf_out, cf_in, cy_out, cy_in, gc16,
    sm_own, sm_in, sm_mid, sm_in2,
    co_s, co_r, cf_s, cf_r, cy_s, cy_r, s1_s, s1_r, s2_s, s2_r, *red,
):
    at = Place()
    n, width = gnr.shape
    half = width // 2
    own = gcoarse.shape[0]
    part = own // 2
    fx_dev = [{"fx": at.fx_at(a, b)} for a, b in FXP]
    fy_dev = [{"fy": at.fy_at(a, c)} for a, c in FYP]
    dp_off = [(d, c) for d in range(4) for c in range(2) if (d, c) != (0, 0)]
    dp_dev = [{"dp": at.dp_at(d), "fy": at.fy_at(0, c)} for d, c in dp_off]
    partner = fy_dev[0]
    greet(fx_dev + fy_dev[1:] + extra_devs(at) + dp_dev)
    sent = []

    def go(c):
        c.start()
        sent.append(c)
        return c

    perm = to_columns(rows, cols)
    att[:, 0:half] = orow[...]
    att[:, half:width] = dims(perm, ocol[...], 0, 0).astype(BF16)
    weights = Reduce(at, red, width // 4, half // LANES)

    def cot_half(h):
        return cot[:, pl.ds(pl.multiple_of(h * half, LANES), half)]

    go_out[...] = dims(att[...], cot_half(1 - at.core), 0, 0).astype(BF16)
    weights.swap(go_out)
    residual = res[...]
    grad_normed = gnr[...].astype(F32) + dims(perm, gnc[...], 0, 0)
    inv = lax.rsqrt(jnp.mean(residual * residual, axis=-1, keepdims=True) + 1e-06)
    pre = residual * inv
    sm_gain = jnp.sum(grad_normed * pre, axis=0, keepdims=True)
    g = grad_normed * gain[...]
    grad_residual = inv * (g - pre * jnp.mean(g * pre, axis=-1, keepdims=True)) + cot[...].astype(F32)
    gf = grad_residual.astype(BF16)
    gfine[...] = gf
    coarse_row = lax.broadcasted_iota(jnp.int32, (n, 8 * part), 1)

    def dense(core):
        named = coarse_row // part * own + lax.rem(coarse_row, part) + core * part
        return dims(onehot(named == ptok[...]), gf, 0, 0)

    co_out[...] = dense(1 - at.core).astype(BF16)
    go(rcopy(co_out, co_in, co_s.at[0], co_r.at[0], partner))
    go_own[...] = dims(att[...], cot_half(at.core), 0, 0)
    weights.along_x(lambda block: go_own[block, :])
    levels = dims(lv[...], gf, 0, 0)[0:8]
    row = lax.broadcasted_iota(jnp.int32, (8, half), 0)
    low = jnp.where(row == 0, sm_gain[:, 0:half], levels[:, 0:half])
    high = jnp.where(row == 0, sm_gain[:, half:width], levels[:, half:width])
    sm_own[0] = low
    sm_own[1] = high
    for i, dev in enumerate(dp_dev):
        go(rcopy(sm_own, sm_in.at[i], s1_s.at[i], s1_r.at[i], dev))
    co_own[...] = dense(at.core)
    rcopy(co_out, co_in, co_s.at[0], co_r.at[0], partner).wait_recv()
    for i, (a, b) in enumerate(FXP):
        owner = at.fx_at(a, b)
        block = pl.ds(pl.multiple_of(owner * part, part), part)
        cf_out[i] = (co_own[block, :] + co_in[block, :].astype(F32)).astype(BF16)
        go(rcopy(cf_out.at[i], cf_in.at[i], cf_s.at[i], cf_r.at[i], fx_dev[i]))
    mixed[...] = (residual + dims(att[...], wo[...], 1, 0)).astype(BF16)
    total = sm_own[...]
    for i, dev in enumerate(dp_dev):
        rcopy(sm_own, sm_in.at[i], s1_s.at[i], s1_r.at[i], dev).wait_recv()
        total = total + sm_in[i]
    sm_mid[...] = total
    for i, (a, b) in enumerate(YZP):
        go(rcopy(sm_mid, sm_in2.at[i], s2_s.at[i], s2_r.at[i], at.yz(a, b)[0]))
    weights.scatter_yz()
    block = pl.ds(pl.multiple_of(at.fx * part, part), part)
    value = co_own[block, :] + co_in[block, :].astype(F32)
    for i in range(7):
        rcopy(cf_out.at[i], cf_in.at[i], cf_s.at[i], cf_r.at[i], fx_dev[i]).wait_recv()
        value = value + cf_in[i].astype(F32)
    cy_out[...] = value.astype(BF16)
    for i, (a, c) in enumerate(FYP):
        go(rcopy(cy_out, cy_in.at[i], cy_s.at[i], cy_r.at[i], fy_dev[i]))
    weights.gather_yz()
    for i in range(3):
        rcopy(cy_out, cy_in.at[i], cy_s.at[i], cy_r.at[i], fy_dev[i]).wait_recv()
    mine = cy_out[...].astype(F32) + cy_in[1].astype(F32)
    other = cy_in[0].astype(F32) + cy_in[2].astype(F32)
    gcoarse[pl.ds(pl.multiple_of(at.core * part, part), part), :] = mine
    gcoarse[pl.ds(pl.multiple_of((1 - at.core) * part, part), part), :] = other
    total = sm_mid[...]
    for i, (a, b) in enumerate(YZP):
        rcopy(sm_mid, sm_in2.at[i], s2_s.at[i], s2_r.at[i], at.yz(a, b)[0]).wait_recv()
        total = total + sm_in2[i]
    small[...] = total * grad_scale
    weights.swap_back()
    weights.finish()
    for h in range(2):
        for b in range(half // LANES):
            c0 = h * half + b * LANES
            gout[:, c0 : c0 + LANES] = weights.block(h, b) * grad_scale
    for c in sent + weights.sent:
        c.wait_send()


def post(orow, gnr, ocol, gnc, res, cot, ptok, lv, gain, wo, own, rows, cols, grad_scale):
    n, width = gnr.shape
    half = width // 2
    part = own // 2
    dma = pltpu.SemaphoreType.DMA
    return pl.pallas_call(
        functools.partial(post_kernel, rows, cols, grad_scale),
        name="post",
        out_shape=[
            jax.ShapeDtypeStruct((n, width), BF16),
            jax.ShapeDtypeStruct((n, width), BF16),
            jax.ShapeDtypeStruct((own, width), F32),
            jax.ShapeDtypeStruct((width // 4, width), F32),
            jax.ShapeDtypeStruct((2, 8, half), F32),
        ],
        in_specs=[pl.BlockSpec(memory_space=pltpu.VMEM)] * 10,
        out_specs=[pl.BlockSpec(memory_space=pltpu.VMEM)] * 5,
        scratch_shapes=[
            pltpu.VMEM((n, width), BF16),
            pltpu.VMEM((width, half), BF16),
            pltpu.VMEM((width, half), F32),
            pltpu.VMEM((8 * part, width), BF16),
            pltpu.VMEM((8 * part, width), BF16),
            pltpu.VMEM((8 * part, width), F32),
            pltpu.VMEM((7, part, width), BF16),
            pltpu.VMEM((7, part, width), BF16),
            pltpu.VMEM((part, width), BF16),
            pltpu.VMEM((3, part, width), BF16),
            pltpu.VMEM((part, width), BF16),
            pltpu.VMEM((2, 8, half), F32),
            pltpu.VMEM((7, 2, 8, half), F32),
            pltpu.VMEM((2, 8, half), F32),
            pltpu.VMEM((15, 2, 8, half), F32),
            dma((1,)), dma((1,)), dma((7,)), dma((7,)), dma((3,)), dma((3,)),
            dma((7,)), dma((7,)), dma((15,)), dma((15,)),
            *Reduce.scratch(width // 4, half // LANES),
        ],
        compiler_params=pltpu.CompilerParams(
            collective_id=2, has_side_effects=True, vmem_limit_bytes=48 << 20
        ),
    )(orow, gnr, ocol, gnc, res, cot, ptok, lv, gain, wo)


def local(
    fine_tokens,
    parent,
    coarse_tokens,
    tile_level,
    level_table,
    norm_gain,
    qkv_weight,
    out_weight,
    cotangent,
):
    _, rows, cols, width = fine_tokens.shape
    half = width // 2
    n = rows * cols
    own = coarse_tokens.shape[1]
    scale = (width // HEADS) ** (-0.5)
    total_tokens = n * lax.axis_size("dp") * lax.axis_size("fy") * lax.axis_size("fx")
    grad_scale = 1.0 / math.sqrt(total_tokens)
    fine = fine_tokens.reshape(n, width)
    cot = cotangent.reshape(n, width)
    ptok = jnp.broadcast_to(parent.reshape(n // BLK, 1), (n // BLK, BLK)).reshape(n, 1)
    gain = norm_gain.reshape(1, width)
    rown, rowd, coln, cold, res, lv = front(
        fine, cot, ptok, coarse_tokens.reshape(own, width), tile_level.reshape(own, 1),
        level_table, gain, out_weight, rows, cols,
    )
    orow, gnr, ocol, gnc, w2 = attention(
        rown.reshape(n, width), rowd.reshape(n, half), coln.reshape(n, width), cold.reshape(n, half),
        qkv_weight, scale, rows * 4,
    )
    orow, gnr, ocol, gnc, gq = back(
        orow.reshape(rows // 8, cols * 8, half), gnr.reshape(rows // 8, cols * 8, width),
        ocol.reshape(cols // 4, rows * 4, half), gnc.reshape(cols // 4, rows * 4, width),
        w2, rows, cols, grad_scale,
    )
    mixed, gfine, gcoarse, gout, small = post(
        orow.reshape(n, half), gnr.reshape(n, width), ocol.reshape(n, half), gnc.reshape(n, width),
        res, cot, ptok, lv, gain, out_weight, own, rows, cols, grad_scale,
    )
    vectors = jnp.concatenate([small[0], small[1]], axis=-1)
    share = width // 4
    ggain = lax.dynamic_slice_in_dim(vectors[0], lax.axis_index("dp") * share, share)
    return (
        mixed.reshape(fine_tokens.shape),
        gfine.reshape(fine_tokens.shape),
        gcoarse[None],
        gq,
        gout,
        ggain,
        vectors[1 : 1 + LEVELS],
    )


def solution(mesh):
    return jax.shard_map(
        local,
        mesh=mesh,
        in_specs=(
            P("dp", "fy", "fx", None),
            P("dp", "fy", "fx"),
            P("dp", "fx", None),
            P("dp", "fx"),
            P(),
            P(),
            P(),
            P(),
            P("dp", "fy", "fx", None),
        ),
        out_specs=(
            P("dp", "fy", "fx", None),
            P("dp", "fy", "fx", None),
            P("dp", "fx", None),
            P("dp", None),
            P("dp", None),
            P("dp"),
            P(),
        ),
        check_vma=False,
    )
```

time: 618 us -> 169 us (0.27); the launches traced: 607 us -> 167 us
  blocking collectives: 296 us -> 0 us
  Pallas kernels: 0 us -> 153 us
  local copies, waits for them, and re-layouts: 97.6 us -> 12.1 us
  matrix products: 65.2 us -> 0 us
  starting transfers between devices: 64 us -> 0 us
  waiting for transfers between devices: 45.4 us -> 0 us
  other arithmetic: 20.7 us -> 1.25 us
  between operations: 17.3 us -> 0.7 us
    psum x2 -> x0, blocking collectives: 217 us -> none  [the longest x1 154 us: local(): grad_level = lax.psum(level_part, ('dp', 'fx'))]
    pallas_call x0 -> x4, Pallas kernels: none -> 153 us  [the longest x1 51.2 us: back(): pl.pallas_call(functools.partial(back_kernel, rows, cols, grad_scale), na...]
    all_to_all x13 -> x0, starting transfers between devices: 63.6 us -> none  [the longest x1 5.97 us: local(): lax.all_to_all(batch_to_rows(grads[2]), 'fx', split_axis=2, concat_axis=0...]
    dot_general x16 -> x0, matrix products: 56.7 us -> none  [the longest x2 11.2 us: attend_grads(): jnp.einsum(score_form + ',' + query_form + '->' + key_form, grad_scores,...]
    reshape x22 -> x3, local copies, waits for them, and re-layouts: 44.2 us -> 1.57 us  [the longest x1 0.74 us: local(): tile_level.reshape(own, 1)]
    all_to_all x13 -> x0, waiting for transfers between devices: 38.9 us -> none  [the longest x1 9.37 us: local(): lax.all_to_all(batch_to_rows(attended_rows), 'fx', split_axis=2, concat_a...]
    all_to_all x3 -> x0, blocking collectives: 36.9 us -> none  [the longest x1 13.2 us: local(): lax.all_to_all(to_column_groups(column_value, column_groups), 'fy', split...]
    all_gather x1 -> x0, blocking collectives: 31.8 us -> none  [local(): shard_piece = lax.all_gather(summary, 'fx', axis=1, tiled=True)]
  transfers between devices with their start and end apart: 18 -> 0, of which waited for: 7 -> 0; matrix products, arithmetic and copies ran while one was open for 27% -> 0% of each run, Pallas kernels for 0% -> 0%
where the time goes in v1:
time: 169 us; the launch traced here: 167 us
  Pallas kernels  153 us (91%)
  local copies, waits for them, and re-layouts  12.1 us (7%)
    pallas_call x1, Pallas kernels, back(): pl.pallas_call(functools.partial(back_kernel, rows, cols, grad_scale), na...  51.2 us
    pallas_call x1, Pallas kernels, front(): pl.pallas_call(functools.partial(front_kernel, rows, cols), name='front',...  40.9 us
    pallas_call x1, Pallas kernels, post(): pl.pallas_call(functools.partial(post_kernel, rows, cols, grad_scale), na...  36.7 us
    pallas_call x1, Pallas kernels, attention(): pl.pallas_call(functools.partial(attention_kernel, scale, col_rows), name...  24.5 us
    unnamed x20, local copies, waits for them, and re-layouts  10.4 us

profile of v1, /device:TPU:0, one launch (start us, length us, event | category | flops | bytes accessed | tf_op | source)
XLA Modules:
  0.0 167.3 jit_solution(16897245844409484325)
XLA Ops:
  0.6 0.8 copy.18
  1.4 0.1 broadcast_in_dim.10
  1.5 0.1 broadcast_in_dim.11
  1.6 0.1 reshape.97.ptok
  1.7 0.7 reshape.82.gain
  2.4 0.7 copy.20.level
  3.1 0.0 copy-start
  3.1 1.3 copy-done
  4.4 0.0 copy-start.1
  4.4 1.1 copy-done.1
  5.5 0.0 copy-start.3
  5.5 1.1 copy-done.3
  6.7 0.0 copy-start.4
  6.7 0.9 copy-done.4
  7.6 0.0 copy-start.5
  7.6 0.7 copy-done.5
  8.3 40.9 %front.1 = (bf16[2,256,768]{2,1,0:T(8,128)(2,1)S(1)}, bf16[2,256,384]{2,1,0:T(8,128)(2,1)S(1)}, bf16[8,64,768]{2,1,0:T(8,128)(2,1)S(1)}, bf16[8,64,384]{2,1,0:T(...) custom-call(bf16[512,768]{1,0:T(8,128)(2,1)S(1)} %bitcast.30, bf16[512,768]{1,0:T(8,128)(2,1)S(1)} %bitcast.24, ...), custom_call_target="tpu_custom_call" | custom-call | tf_op jit(solution)/shard_map/front/pallas_call | solution.py:173
  49.1 24.5 %attention.1 = (bf16[512,384]{1,0:T(8,128)(2,1)S(1)}, bf16[512,768]{1,0:T(8,128)(2,1)S(1)}, bf16[512,384]{1,0:T(8,128)(2,1)S(1)}, bf16[512,768]{1,0:T(8,128)(2,1)S(1)}, bf16[2,768,1152]{2,1,0:T(8,128)(2,1)}) custom-call(bf16[512,768]{1,0:T(8,128)(2,1)S(1)} %bitcast.33, bf16[512,384]{1,0:T(8,128)(2,1)S(1)} %bitcast.39, bf16[512,768]{1,0:T(8,128)(2,1)S(1)} %bitcast.34, ...), custom_call_target="tpu_custom_call" | custom-call | tf_op jit(solution)/shard_map/attention/pallas_call | solution.py:270
  73.6 0.0 copy-start.2
  73.6 51.2 %back.1 = (bf16[16,32,384]{2,1,0:T(8,128)(2,1)S(1)}, bf16[16,32,768]{2,1,0:T(8,128)(2,1)S(1)}, bf16[32,16,384]{2,1,0:T(8,128)(2,1)S(1)}, bf16[32,16,768]{2,1,0:T(8,128)(2,1)S(1)}, f32[192,2304]{1,0:T(8,128)}) custom-call(bf16[2,256,384]{2,1,0:T(8,128)(2,1)S(1)} %bitcast.37, bf16[2,256,768]{2,1,0:T(8,128)(2,1)S(1)} %bitcast.31, ...), custom_call_target="tpu_custom_call" | custom-call | tf_op jit(solution)/shard_map/back/pallas_call | solution.py:458
  124.8 0.0 copy-done.2
  124.8 36.7 %post.1 = (bf16[512,768]{1,0:T(8,128)(2,1)S(1)}, bf16[512,768]{1,0:T(8,128)(2,1)S(1)}, f32[64,768]{1,0:T(8,128)S(1)}, f32[192,768]{1,0:T(8,128)S(1)}, f32[2,8,384]{2,1,0:T(8,128)S(1)}) custom-call(bf16[512,384]{1,0:T(8,128)(2,1)S(1)} %bitcast.35, bf16[512,768]{1,0:T(8,128)(2,1)S(1)} %bitcast.26, bf16[512,384]{1,0:T(8,128)(2,1)S(1)} %bitcast.36, ...), custom_call_target="tpu_custom_call" | custom-call | tf_op jit(solution)/shard_map/post/pallas_call | solution.py:593
  161.6 0.6 pad_maximum_fusion
  162.2 0.6 fusion
  162.8 0.0 copy-start.6
  162.8 0.9 copy.27
  163.7 0.9 copy.28
  164.6 0.7 copy.29
  165.2 0.0 copy-done.6
  165.3 1.2 copy.30
  166.5 0.8 copy.31
  (1 shorter events, 0.0 us)
Async XLA Ops:
  3.1 1.3 copy-start
  4.4 1.1 copy-start.1
  5.5 1.1 copy-start.3
  6.7 0.9 copy-start.4
  7.6 0.7 copy-start.5
  73.6 51.2 %copy-start.2 = (bf16[1,16,32,768]{3,2,1,0:T(8,128)(2,1)S(1)}, bf16[1,16,32,768]{3,2,1,0:T(8,128)(2,1)}, u32[]{:S(2)}) copy-start(bf16[1,16,32,768]{3,2,1,0:T(8,128)(2,1)} %param.17) | copy-start | bytes 2359300
  162.8 2.4 %copy-start.6 = (f32[192,2304]{1,0:T(8,128)S(1)}, f32[192,2304]{1,0:T(8,128)}, u32[]{:S(2)}) copy-start(f32[192,2304]{1,0:T(8,128)} %get-tuple-element.61) | copy-start | bytes 5308420

commit v2 on v1

v2 whole, which is shorter than its diff:
```python
import functools
import math

import jax
import jax.numpy as jnp
from jax import lax
from jax.experimental import pallas as pl
from jax.experimental.pallas import tpu as pltpu
from jax.sharding import PartitionSpec as P

HEADS = 12
BLK = 4
LEVELS = 3
MESH = pl.DeviceIdType.MESH
F32 = jnp.float32
BF16 = jnp.bfloat16
FXP = [(a, b) for a in range(2) for b in range(4) if (a, b) != (0, 0)]
FYP = [(0, 1), (1, 0), (1, 1)]
YZP = [(a, b) for a in range(4) for b in range(4) if (a, b) != (0, 0)]
LANES = 128


def dims(a, b, ca, cb):
    return lax.dot_general(a, b, (((ca,), (cb,)), ((), ())), preferred_element_type=F32)


class Place:
    def __init__(self):
        self.dp = lax.axis_index("dp")
        self.fy = lax.axis_index("fy")
        self.fx = lax.axis_index("fx")
        self.zh, self.core = self.fy // 2, self.fy % 2
        self.zl, self.y = self.fx // 4, self.fx % 4
        self.z = self.zh * 2 + self.zl

    def fx_at(self, a, b):
        return lax.rem(self.zl + a, 2) * 4 + lax.rem(self.y + b, 4)

    def fy_at(self, a, c):
        return lax.rem(self.zh + a, 2) * 2 + lax.rem(self.core + c, 2)

    def yz(self, a, b):
        z, y = lax.rem(self.z + a, 4), lax.rem(self.y + b, 4)
        dev = {"fy": (z // 2) * 2 + self.core, "fx": (z % 2) * 4 + y}
        return dev, z * 4 + y

    def dp_at(self, d):
        return lax.rem(self.dp + d, 4)


def rcopy(src, dst, ss, rs, dev):
    return pltpu.make_async_remote_copy(
        src_ref=src, dst_ref=dst, send_sem=ss, recv_sem=rs, device_id=dev, device_id_type=MESH
    )


def greet(devs):
    barrier = pltpu.get_barrier_semaphore()
    for dev in devs:
        pl.semaphore_signal(barrier, inc=1, device_id=dev, device_id_type=MESH)
    pl.semaphore_wait(barrier, len(devs))


def onehot(cond):
    return jnp.where(cond, 1.0, 0.0).astype(BF16)


def to_columns(rows, cols):
    n = rows * cols
    new = lax.broadcasted_iota(jnp.int32, (n, n), 0)
    old = lax.broadcasted_iota(jnp.int32, (n, n), 1)
    return onehot(old == lax.rem(new, rows) * cols + new // rows)


def attend(q, k, v, d, scale, mask):
    size, lanes = q.shape
    first = lax.broadcasted_iota(jnp.int32, (size, lanes), 1) < lanes // 2

    def stack(t):
        zero = jnp.zeros_like(t)
        return jnp.concatenate([jnp.where(first, t, zero), jnp.where(first, zero, t)], axis=0)

    def join(t):
        return jnp.where(first, t[:size], t[size:])

    qs = stack((q.astype(F32) * scale).astype(BF16))
    ds_ = stack(d)
    s = dims(qs, k, 1, 1)
    if mask is not None:
        s = jnp.where(mask, s, -1e30)
    e = jnp.exp(s - jnp.max(s, axis=-1, keepdims=True))
    w = e * (1.0 / jnp.sum(e, axis=-1, keepdims=True))
    wb = w.astype(BF16)
    out = join(dims(wb, v, 1, 0)).astype(BF16)
    dv = dims(wb, ds_, 0, 0).astype(BF16)
    gw = dims(ds_, v, 1, 1)
    inner = jnp.sum(w * gw, axis=-1, keepdims=True)
    gs = (w * (gw - inner)).astype(BF16)
    dq = (join(dims(gs, k, 1, 0)) * scale).astype(BF16)
    dk = dims(gs, qs, 0, 0).astype(BF16)
    return out, dq, dk, dv


class Reduce:
    @staticmethod
    def scratch(rows, nb):
        dma = pltpu.SemaphoreType.DMA
        piece = -(-(rows * nb // 16) // 16) * 16
        return [
            pltpu.VMEM((4 * rows, nb * LANES), BF16),
            pltpu.VMEM((3, rows, nb * LANES), BF16),
            pltpu.VMEM((3, rows, nb * LANES), BF16),
            pltpu.VMEM((rows, nb * LANES), F32),
            pltpu.VMEM((16 * piece, LANES), BF16),
            pltpu.VMEM((15, piece, LANES), BF16),
            pltpu.VMEM((2, 16 * piece, LANES), BF16),
            dma((2,)), dma((2,)), dma((3,)), dma((3,)), dma((15,)), dma((15,)), dma((15,)), dma((15,)),
        ]

    def __init__(self, at, refs, rows, nb):
        (self.cx, self.xs, self.xr, self.acc, self.p16, self.r16, self.ag,
         self.c_s, self.c_r, self.x_s, self.x_r, self.r_s, self.r_r, self.g_s, self.g_r) = refs
        self.at, self.rows, self.nb = at, rows, nb
        self.piece = self.r16.shape[1]
        self.partner = {"fy": at.fy_at(0, 1)}

    def go(self, c):
        c.start()

    def swap(self, src):
        return rcopy(src, self.cx, self.c_s.at[0], self.c_r.at[0], self.partner)

    def drain(self):
        rcopy(self.cx, self.cx, self.c_s.at[0], self.c_r.at[0], self.partner).wait_send()
        ref = self.ag.at[self.at.core]
        rcopy(ref, ref, self.c_s.at[1], self.c_r.at[1], self.partner).wait_send()
        for d in range(3):
            rcopy(self.xs.at[d], self.xr.at[d], self.x_s.at[d], self.x_r.at[d], self.partner).wait_send()
        for i in range(15):
            ref = self.r16.at[i]
            rcopy(ref, ref, self.r_s.at[i], self.r_r.at[i], self.partner).wait_send()
            rcopy(ref, ref, self.g_s.at[i], self.g_r.at[i], self.partner).wait_send()

    def along_x(self, mine):
        self.swap(self.cx).wait_recv()
        for d in (2, 1, 3, 0):
            i = self.at.dp_at(d)
            block = pl.ds(pl.multiple_of(i * self.rows, self.rows), self.rows)
            value = mine(block) + self.cx[block, :].astype(F32)
            if d == 0:
                self.acc[...] = value
            else:
                self.xs[d - 1] = value.astype(BF16)
                self.go(rcopy(
                    self.xs.at[d - 1], self.xr.at[d - 1], self.x_s.at[d - 1], self.x_r.at[d - 1], {"dp": i}
                ))

    def scatter_yz(self):
        for d in range(3):
            rcopy(self.xs.at[d], self.xr.at[d], self.x_s.at[d], self.x_r.at[d], {"dp": self.at.dp}).wait_recv()
        rows = self.rows
        for b in range(self.nb):
            lanes = slice(b * LANES, (b + 1) * LANES)
            value = self.acc[:, lanes]
            for d in range(3):
                value = value + self.xr[d, :, lanes].astype(F32)
            self.p16[b * rows : (b + 1) * rows, :] = value.astype(BF16)
        used = self.nb * rows
        if used < self.p16.shape[0]:
            self.p16[used:, :] = jnp.zeros((self.p16.shape[0] - used, LANES), BF16)
        for i, (a, b) in enumerate(YZP):
            dev, q = self.at.yz(a, b)
            self.go(rcopy(self.p16.at[self.slot(q)], self.r16.at[i], self.r_s.at[i], self.r_r.at[i], dev))

    def slot(self, q):
        return pl.ds(pl.multiple_of(q * self.piece, self.piece), self.piece)

    def gather_yz(self):
        at = self.at
        _, q = at.yz(0, 0)
        value = self.p16[self.slot(q), :].astype(F32)
        for i in range(15):
            dev, _ = at.yz(*YZP[i])
            rcopy(self.r16.at[i], self.r16.at[i], self.r_s.at[i], self.r_r.at[i], dev).wait_recv()
            value = value + self.r16[i].astype(F32)
        self.ag[at.core, self.slot(q), :] = value.astype(BF16)
        src = self.ag.at[at.core, self.slot(q)]
        for i, (a, b) in enumerate(YZP):
            dev, _ = at.yz(a, b)
            self.go(rcopy(src, src, self.g_s.at[i], self.g_r.at[i], dev))

    def swap_back(self):
        at = self.at
        for i, (a, b) in enumerate(YZP):
            dev, q = at.yz(4 - a, 4 - b)
            ref = self.ag.at[at.core, self.slot(q)]
            rcopy(ref, ref, self.g_s.at[i], self.g_r.at[i], dev).wait_recv()
        ref = self.ag.at[at.core]
        self.go(rcopy(ref, ref, self.c_s.at[1], self.c_r.at[1], self.partner))

    def finish(self):
        ref = self.ag.at[1 - self.at.core]
        rcopy(ref, ref, self.c_s.at[1], self.c_r.at[1], self.partner).wait_recv()

    def block(self, half, b):
        return self.ag[half, b * self.rows : (b + 1) * self.rows, :].astype(F32)


class Legs:
    def __init__(self, at, rows, cols, sems):
        self.at, self.rows, self.cols = at, rows, cols
        self.row_s, self.row_r, self.col_s, self.col_r, self.loc = sems
        self.fx_dev = [{"fx": at.fx_at(a, b)} for a, b in FXP]
        self.fy_dev = [{"fy": at.fy_at(a, c)} for a, c in FYP]
        self.sent = []
        self.kept = []

    def send(self, src, dst, ss, rs, dev):
        c = rcopy(src, dst, ss, rs, dev)
        c.start()
        self.sent.append(c)

    def keep(self, src, dst, sem):
        c = pltpu.make_async_copy(src, dst, sem)
        c.start()
        return c

    def token_row(self, ref, u, owner):
        return ref.at[pl.ds(owner * 2 + u, 1)]

    def token_col(self, ref, u, owner):
        return ref.at[pl.ds(owner * (self.cols // 4) + u * (self.cols // 8), self.cols // 8)]

    def owner_row(self, ref, u, member):
        return ref.at[pl.ds(u, 1), pl.ds(member * self.cols, self.cols)]

    def owner_col(self, ref, u, member):
        return ref.at[pl.ds(u * (self.cols // 8), self.cols // 8), pl.ds(member * self.rows, self.rows)]

    def out_row(self, kind, u, src, dst):
        at = self.at
        for i, (a, b) in enumerate(FXP):
            self.send(
                self.token_row(src, u, at.fx_at(a, b)), self.owner_row(dst, u, at.fx),
                self.row_s.at[kind, u, i], self.row_r.at[kind, u, i], self.fx_dev[i],
            )
        return self.keep(self.token_row(src, u, at.fx), self.owner_row(dst, u, at.fx), self.loc.at[kind, u])

    def out_col(self, kind, u, src, dst):
        at = self.at
        for i, (a, c) in enumerate(FYP):
            self.send(
                self.token_col(src, u, at.fy_at(a, c)), self.owner_col(dst, u, at.fy),
                self.col_s.at[kind, u, i], self.col_r.at[kind, u, i], self.fy_dev[i],
            )
        return self.keep(self.token_col(src, u, at.fy), self.owner_col(dst, u, at.fy), self.loc.at[kind, 2 + u])

    def got_row(self, kind, u, dst):
        for i, (a, b) in enumerate(FXP):
            ref = self.owner_row(dst, u, self.at.fx_at(a, 4 - b))
            rcopy(ref, ref, self.row_s.at[kind, u, i], self.row_r.at[kind, u, i], self.fx_dev[i]).wait_recv()

    def got_col(self, kind, u, dst):
        for i, (a, c) in enumerate(FYP):
            ref = self.owner_col(dst, u, self.at.fy_at(a, c))
            rcopy(ref, ref, self.col_s.at[kind, u, i], self.col_r.at[kind, u, i], self.fy_dev[i]).wait_recv()

    def home_row(self, kind, u, src, dst):
        at = self.at
        for i, (a, b) in enumerate(FXP):
            self.send(
                self.owner_row(src, u, at.fx_at(a, b)), self.token_row(dst, u, at.fx),
                self.row_s.at[kind, u, i], self.row_r.at[kind, u, i], self.fx_dev[i],
            )
        return self.keep(self.owner_row(src, u, at.fx), self.token_row(dst, u, at.fx), self.loc.at[kind, u])

    def home_col(self, kind, u, src, dst):
        at = self.at
        for i, (a, c) in enumerate(FYP):
            self.send(
                self.owner_col(src, u, at.fy_at(a, c)), self.token_col(dst, u, at.fy),
                self.col_s.at[kind, u, i], self.col_r.at[kind, u, i], self.fy_dev[i],
            )
        return self.keep(self.owner_col(src, u, at.fy), self.token_col(dst, u, at.fy), self.loc.at[kind, 2 + u])

    def back_row(self, kind, u, dst):
        for i, (a, b) in enumerate(FXP):
            ref = self.token_row(dst, u, self.at.fx_at(a, 4 - b))
            rcopy(ref, ref, self.row_s.at[kind, u, i], self.row_r.at[kind, u, i], self.fx_dev[i]).wait_recv()

    def back_col(self, kind, u, dst):
        for i, (a, c) in enumerate(FYP):
            ref = self.token_col(dst, u, self.at.fy_at(a, c))
            rcopy(ref, ref, self.col_s.at[kind, u, i], self.col_r.at[kind, u, i], self.fy_dev[i]).wait_recv()


def extra_devs(at):
    return [{"fy": at.fy_at(1, 0), "fx": at.fx_at(a, b)} for a, b in FXP]


N_RED = 15


def layer_kernel(
    rows, cols, scale, grad_scale, fine_h, cot_h, ptok, coarse, level, table, gain, wq_h, wo_h,
    mixed, gfine, gcoarse, gq, gout, small,
    fine, cot, wq, wo, tab, perm, res, lv,
    sn, sd, snc, sdc, rown, rowd, coln, cold, qkv, grads, w2,
    orow, gnr, ocol, gnc, orow_t, gnr_t, ocol_t, gnc_t, dd, oo, gg,
    att, go_out, go_own, co_out, co_in, co_own, cf_out, cf_in, cy_out, cy_in,
    sm_own, sm_in, sm_mid, sm_in2,
    ld, ag_s, ag_r, fw_s, fw_r, row_s, row_r, col_s, col_r, loc,
    co_s, co_r, cf_s, cf_r, cy_s, cy_r, s1_s, s1_r, s2_s, s2_r, *red,
):
    at = Place()
    n, width = fine.shape
    half = width // 2
    own = coarse.shape[0]
    part = own // 2
    legs = Legs(at, rows, cols, (row_s, row_r, col_s, col_r, loc))
    fx_dev, fy_dev = legs.fx_dev, legs.fy_dev
    partner = fy_dev[0]
    dp_off = [(d, c) for d in range(4) for c in range(2) if (d, c) != (0, 0)]
    dp_dev = [{"dp": at.dp_at(d), "fy": at.fy_at(0, c)} for d, c in dp_off]
    weights = Reduce(at, red[:N_RED], width // 4, 3 * half // LANES)
    outs = Reduce(at, red[N_RED:], width // 4, half // LANES)
    sent = legs.sent
    go = legs.send

    loads = [
        pltpu.make_async_copy(a, b, ld.at[i])
        for i, (a, b) in enumerate(((cot_h, cot), (wo_h, wo), (fine_h, fine), (wq_h, wq)))
    ]
    for c in loads:
        c.start()
    mine = pl.ds(at.fx * own, own)
    lev = level[...]
    add = jnp.where(lev == 0, table[0:1, :], jnp.where(lev == 1, table[1:2, :], table[2:3, :]))
    tab[mine, 0:width] = (coarse[...].astype(F32) + add).astype(BF16)
    lane = lax.broadcasted_iota(jnp.int32, (own, LANES), 1)
    tab[mine, width : width + LANES] = onehot(lane == lev + 1)
    perm[...] = to_columns(rows, cols)
    greet(fx_dev + fy_dev[1:] + extra_devs(at) + dp_dev)

    def chunk(owner, core):
        return tab.at[pl.ds(owner * own + core * part, part)]

    def across(a, b):
        fx = at.fx_at(a, b)
        return {"fx": fx} if a == 0 else {"fx": fx, "fy": at.fy_at(at.core, 0)}

    for i, (a, b) in enumerate(FXP):
        go(chunk(at.fx, at.core), chunk(at.fx, at.core), ag_s.at[i], ag_r.at[i], across(a, b))
    loads[0].wait()
    loads[1].wait()
    d = dims(cot[...], wo[...], 1, 1).astype(BF16)
    sd[...] = d[:, 0:half].reshape(rows, cols, half)
    kept = [legs.out_row(1, u, sd, rowd) for u in range(2)]
    sdc[...] = dims(perm[...], d[:, half:width], 1, 0).astype(BF16).reshape(cols, rows, half)
    kept += [legs.out_col(1, u, sdc, cold) for u in range(2)]
    for i, (a, b) in enumerate(FXP):
        src = chunk(at.fx_at(a, 4 - b), at.core)
        rcopy(src, src, ag_s.at[i], ag_r.at[i], across(a, b)).wait_recv()
        go(src, src, fw_s.at[i], fw_r.at[i], partner)
    loads[2].wait()
    for i, (a, b) in enumerate(FXP):
        src = chunk(at.fx_at(a, 4 - b), 1 - at.core)
        rcopy(src, src, fw_s.at[i], fw_r.at[i], partner).wait_recv()
    pick = onehot(lax.broadcasted_iota(jnp.int32, (n, tab.shape[0]), 1) == ptok[...])
    read = dims(pick, tab[...], 1, 0)
    lv[...] = read[:, width : width + LANES].astype(BF16)
    residual = fine[...].astype(F32) + read[:, 0:width]
    res[...] = residual
    inv = lax.rsqrt(jnp.mean(residual * residual, axis=-1, keepdims=True) + 1e-06)
    normed = (residual * inv * gain[...]).astype(BF16)
    sn[...] = normed.reshape(rows, cols, width)
    kept += [legs.out_row(0, u, sn, rown) for u in range(2)]
    snc[...] = dims(perm[...], normed, 1, 0).astype(BF16).reshape(cols, rows, width)
    kept += [legs.out_col(0, u, snc, coln) for u in range(2)]
    loads[3].wait()
    for c in kept:
        c.wait()
    kept = []

    size = n // 2
    pair = 2 * 4 * rows
    i = lax.broadcasted_iota(jnp.int32, (2 * pair, pair), 0)
    j = lax.broadcasted_iota(jnp.int32, (2 * pair, pair), 1)
    mask = lax.rem(i, pair) // (4 * rows) == j // (4 * rows)

    def unit(which, u, x, d, out, gn):
        for j in range(3):
            c0 = (2 * j + which) * half
            qkv[:, j * half : (j + 1) * half] = dims(x, wq[:, c0 : c0 + half], 1, 0).astype(BF16)
        t_size = size if which == 0 else pair
        base = u * size

        def one(t, _):
            r = pl.ds(pl.multiple_of(t * t_size, t_size), t_size)
            for p in range(half // LANES):
                c = p * LANES
                q, k, v = (qkv[r, j * half + c : j * half + c + LANES] for j in range(3))
                o, dq, dk, dv = attend(q, k, v, d[r, c : c + LANES], scale, mask if which else None)
                out[r, c : c + LANES] = o
                g = pl.ds(pl.multiple_of(base + t * t_size, t_size), t_size)
                for j, value in enumerate((dq, dk, dv)):
                    grads[which, g, j * half + c : j * half + c + LANES] = value
            return 0

        lax.fori_loop(0, size // t_size, one, 0)
        total = None
        for j in range(3):
            c0 = (2 * j + which) * half
            g = grads[which, base : base + size, j * half : (j + 1) * half]
            back = dims(g, wq[:, c0 : c0 + half], 1, 1)
            total = back if total is None else total + back
        gn[...] = total.astype(BF16)

    def wgrad(which, x):
        for j in range(3):
            g = grads[which, :, j * half : (j + 1) * half]
            w2[which, :, j * half : (j + 1) * half] = dims(x, g, 0, 0).astype(BF16)

    for u in range(2):
        legs.got_row(1, u, rowd)
        legs.got_row(0, u, rown)
        unit(0, u, rown[u], rowd.at[u], orow.at[u], gnr.at[u])
        kept.append(legs.home_row(2, u, orow, orow_t))
        kept.append(legs.home_row(3, u, gnr, gnr_t))
    wgrad(0, rown[...].reshape(n, width))

    @pl.when(at.core == 1)
    def _():
        weights.swap(w2.at[0]).start()

    for u in range(2):
        legs.got_col(1, u, cold)
        legs.got_col(0, u, coln)
        c4 = cols // 8
        x = coln[u * c4 : (u + 1) * c4].reshape(size, width)
        dd[...] = cold[u * c4 : (u + 1) * c4].reshape(size, half)
        unit(1, u, x, dd, oo, gg)
        ocol[u * c4 : (u + 1) * c4] = oo[...].reshape(c4, 4 * rows, half)
        gnc[u * c4 : (u + 1) * c4] = gg[...].reshape(c4, 4 * rows, width)
        kept.append(legs.home_col(2, u, ocol, ocol_t))
        kept.append(legs.home_col(3, u, gnc, gnc_t))
        if u == 0:

            @pl.when(at.core == 0)
            def _():
                weights.along_x(lambda block: w2[0, block, :].astype(F32))

    wgrad(1, coln[...].reshape(n, width))

    @pl.when(at.core == 0)
    def _():
        weights.swap(w2.at[1]).start()
        weights.scatter_yz()

    @pl.when(at.core == 1)
    def _():
        weights.along_x(lambda block: w2[1, block, :].astype(F32))

    @pl.when(at.core == 0)
    def _():
        weights.gather_yz()

    for c in kept:
        c.wait()
    for u in range(2):
        legs.back_row(2, u, orow_t)
        legs.back_col(2, u, ocol_t)
    att[:, 0:half] = orow_t[...].reshape(n, half)
    att[:, half:width] = dims(perm[...], ocol_t[...].reshape(n, half), 0, 0).astype(BF16)

    def cot_half(h):
        return cot[:, pl.ds(pl.multiple_of(h * half, LANES), half)]

    go_out[...] = dims(att[...], cot_half(1 - at.core), 0, 0).astype(BF16)
    outs.swap(go_out).start()
    go_own[...] = dims(att[...], cot_half(at.core), 0, 0)
    mixed[...] = (res[...] + dims(att[...], wo[...], 1, 0)).astype(BF16)

    @pl.when(at.core == 0)
    def _():
        weights.swap_back()

    @pl.when(at.core == 1)
    def _():
        weights.scatter_yz()

    outs.along_x(lambda block: go_own[block, :])

    @pl.when(at.core == 1)
    def _():
        weights.gather_yz()

    outs.scatter_yz()
    for u in range(2):
        legs.back_row(3, u, gnr_t)
        legs.back_col(3, u, gnc_t)
    residual = res[...]
    grad_normed = gnr_t[...].reshape(n, width).astype(F32) + dims(perm[...], gnc_t[...].reshape(n, width), 0, 0)
    inv = lax.rsqrt(jnp.mean(residual * residual, axis=-1, keepdims=True) + 1e-06)
    pre = residual * inv
    sm_gain = jnp.sum(grad_normed * pre, axis=0, keepdims=True)
    g = grad_normed * gain[...]
    grad_residual = inv * (g - pre * jnp.mean(g * pre, axis=-1, keepdims=True)) + cot[...].astype(F32)
    gf = grad_residual.astype(BF16)
    gfine[...] = gf
    coarse_row = lax.broadcasted_iota(jnp.int32, (n, 8 * part), 1)

    def dense(core):
        named = coarse_row // part * own + lax.rem(coarse_row, part) + core * part
        return dims(onehot(named == ptok[...]), gf, 0, 0)

    co_out[...] = dense(1 - at.core).astype(BF16)
    go(co_out, co_in, co_s.at[0], co_r.at[0], partner)
    levels = dims(lv[...], gf, 0, 0)[0:8]
    row = lax.broadcasted_iota(jnp.int32, (8, half), 0)
    sm_own[0] = jnp.where(row == 0, sm_gain[:, 0:half], levels[:, 0:half])
    sm_own[1] = jnp.where(row == 0, sm_gain[:, half:width], levels[:, half:width])
    for i, dev in enumerate(dp_dev):
        go(sm_own, sm_in.at[i], s1_s.at[i], s1_r.at[i], dev)
    co_own[...] = dense(at.core)
    rcopy(co_out, co_in, co_s.at[0], co_r.at[0], partner).wait_recv()
    for i, (a, b) in enumerate(FXP):
        owner = at.fx_at(a, b)
        block = pl.ds(pl.multiple_of(owner * part, part), part)
        cf_out[i] = (co_own[block, :] + co_in[block, :].astype(F32)).astype(BF16)
        go(cf_out.at[i], cf_in.at[i], cf_s.at[i], cf_r.at[i], fx_dev[i])
    total = sm_own[...]
    for i, dev in enumerate(dp_dev):
        rcopy(sm_own, sm_in.at[i], s1_s.at[i], s1_r.at[i], dev).wait_recv()
        total = total + sm_in[i]
    sm_mid[...] = total
    for i, (a, b) in enumerate(YZP):
        go(sm_mid, sm_in2.at[i], s2_s.at[i], s2_r.at[i], at.yz(a, b)[0])
    outs.gather_yz()

    @pl.when(at.core == 1)
    def _():
        weights.swap_back()

    weights.finish()
    for h in range(2):
        for j in range(3):
            for b in range(half // LANES):
                c0 = (2 * j + h) * half + b * LANES
                gq[:, c0 : c0 + LANES] = weights.block(h, j * (half // LANES) + b) * grad_scale
    block = pl.ds(pl.multiple_of(at.fx * part, part), part)
    value = co_own[block, :] + co_in[block, :].astype(F32)
    for i in range(7):
        rcopy(cf_out.at[i], cf_in.at[i], cf_s.at[i], cf_r.at[i], fx_dev[i]).wait_recv()
        value = value + cf_in[i].astype(F32)
    cy_out[...] = value.astype(BF16)
    for i, (a, c) in enumerate(FYP):
        go(cy_out, cy_in.at[i], cy_s.at[i], cy_r.at[i], fy_dev[i])
    outs.swap_back()
    total = sm_mid[...]
    for i, (a, b) in enumerate(YZP):
        rcopy(sm_mid, sm_in2.at[i], s2_s.at[i], s2_r.at[i], at.yz(a, b)[0]).wait_recv()
        total = total + sm_in2[i]
    small[...] = total * grad_scale
    for i in range(3):
        rcopy(cy_out, cy_in.at[i], cy_s.at[i], cy_r.at[i], fy_dev[i]).wait_recv()
    gcoarse[pl.ds(pl.multiple_of(at.core * part, part), part), :] = cy_out[...].astype(F32) + cy_in[1].astype(F32)
    gcoarse[pl.ds(pl.multiple_of((1 - at.core) * part, part), part), :] = cy_in[0].astype(F32) + cy_in[2].astype(F32)
    outs.finish()
    for h in range(2):
        for b in range(half // LANES):
            c0 = h * half + b * LANES
            gout[:, c0 : c0 + LANES] = outs.block(h, b) * grad_scale
    for c in sent:
        c.wait_send()
    weights.drain()
    outs.drain()


def layer(fine, cot, ptok, coarse, level, table, gain, wq, wo, rows, cols, scale, grad_scale):
    n, width = fine.shape
    half = width // 2
    own = coarse.shape[0]
    part = own // 2
    dma = pltpu.SemaphoreType.DMA
    vmem = pltpu.VMEM
    hbm = pl.BlockSpec(memory_space=pl.ANY)
    here = pl.BlockSpec(memory_space=pltpu.VMEM)
    r2, c8, c4 = rows // 8, cols * 8, cols // 4
    return pl.pallas_call(
        functools.partial(layer_kernel, rows, cols, scale, grad_scale),
        name="layer",
        out_shape=[
            jax.ShapeDtypeStruct((n, width), BF16),
            jax.ShapeDtypeStruct((n, width), BF16),
            jax.ShapeDtypeStruct((own, width), F32),
            jax.ShapeDtypeStruct((width // 4, 6 * half), F32),
            jax.ShapeDtypeStruct((width // 4, width), F32),
            jax.ShapeDtypeStruct((2, 8, half), F32),
        ],
        in_specs=[hbm, hbm, here, here, here, here, here, hbm, hbm],
        out_specs=[here] * 6,
        scratch_shapes=[
            vmem((n, width), BF16), vmem((n, width), BF16), vmem((width, 6 * half), BF16), vmem((width, width), BF16),
            vmem((8 * own, width + LANES), BF16), vmem((n, n), BF16), vmem((n, width), F32), vmem((n, LANES), BF16),
            vmem((rows, cols, width), BF16), vmem((rows, cols, half), BF16),
            vmem((cols, rows, width), BF16), vmem((cols, rows, half), BF16),
            vmem((r2, c8, width), BF16), vmem((r2, c8, half), BF16),
            vmem((c4, rows * 4, width), BF16), vmem((c4, rows * 4, half), BF16),
            vmem((n // 2, 3 * half), BF16), vmem((2, n, 3 * half), BF16), vmem((2, width, 3 * half), BF16),
            vmem((r2, c8, half), BF16), vmem((r2, c8, width), BF16),
            vmem((c4, rows * 4, half), BF16), vmem((c4, rows * 4, width), BF16),
            vmem((rows, cols, half), BF16), vmem((rows, cols, width), BF16),
            vmem((cols, rows, half), BF16), vmem((cols, rows, width), BF16),
            vmem((n // 2, half), BF16), vmem((n // 2, half), BF16), vmem((n // 2, width), BF16),
            vmem((n, width), BF16), vmem((width, half), BF16), vmem((width, half), F32),
            vmem((8 * part, width), BF16), vmem((8 * part, width), BF16), vmem((8 * part, width), F32),
            vmem((7, part, width), BF16), vmem((7, part, width), BF16),
            vmem((part, width), BF16), vmem((3, part, width), BF16),
            vmem((2, 8, half), F32), vmem((7, 2, 8, half), F32), vmem((2, 8, half), F32), vmem((15, 2, 8, half), F32),
            dma((4,)), dma((7,)), dma((7,)), dma((7,)), dma((7,)),
            dma((4, 2, 7)), dma((4, 2, 7)), dma((4, 2, 3)), dma((4, 2, 3)), dma((4, 4)),
            dma((1,)), dma((1,)), dma((7,)), dma((7,)), dma((3,)), dma((3,)),
            dma((7,)), dma((7,)), dma((15,)), dma((15,)),
            *Reduce.scratch(width // 4, 3 * half // LANES),
            *Reduce.scratch(width // 4, half // LANES),
        ],
        compiler_params=pltpu.CompilerParams(
            collective_id=0, has_side_effects=True, vmem_limit_bytes=62 << 20
        ),
    )(fine, cot, ptok, coarse, level, table, gain, wq, wo)


def local(
    fine_tokens,
    parent,
    coarse_tokens,
    tile_level,
    level_table,
    norm_gain,
    qkv_weight,
    out_weight,
    cotangent,
):
    _, rows, cols, width = fine_tokens.shape
    half = width // 2
    n = rows * cols
    own = coarse_tokens.shape[1]
    scale = (width // HEADS) ** (-0.5)
    total_tokens = n * lax.axis_size("dp") * lax.axis_size("fy") * lax.axis_size("fx")
    grad_scale = 1.0 / math.sqrt(total_tokens)
    fine = fine_tokens.reshape(n, width)
    cot = cotangent.reshape(n, width)
    ptok = jnp.broadcast_to(parent.reshape(n // BLK, 1), (n // BLK, BLK)).reshape(n, 1)
    gain = norm_gain.reshape(1, width)
    mixed, gfine, gcoarse, gq, gout, small = layer(
        fine, cot, ptok, coarse_tokens.reshape(own, width), tile_level.reshape(own, 1),
        level_table, gain, qkv_weight, out_weight, rows, cols, scale, grad_scale,
    )
    vectors = jnp.concatenate([small[0], small[1]], axis=-1)
    share = width // 4
    ggain = lax.dynamic_slice_in_dim(vectors[0], lax.axis_index("dp") * share, share)
    return (
        mixed.reshape(fine_tokens.shape),
        gfine.reshape(fine_tokens.shape),
        gcoarse[None],
        gq,
        gout,
        ggain,
        vectors[1 : 1 + LEVELS],
    )


def solution(mesh):
    return jax.shard_map(
        local,
        mesh=mesh,
        in_specs=(
            P("dp", "fy", "fx", None),
            P("dp", "fy", "fx"),
            P("dp", "fx", None),
            P("dp", "fx"),
            P(),
            P(),
            P(),
            P(),
            P("dp", "fy", "fx", None),
        ),
        out_specs=(
            P("dp", "fy", "fx", None),
            P("dp", "fy", "fx", None),
            P("dp", "fx", None),
            P("dp", None),
            P("dp", None),
            P("dp"),
            P(),
        ),
        check_vma=False,
    )
```

time: 169 us -> 121 us (0.72)
  Pallas kernels: 153 us -> 107 us
    pallas_call x4 -> x1, Pallas kernels: 153 us -> 107 us  [layer(): pl.pallas_call(functools.partial(layer_kernel, rows, cols, scale, grad_sc...]
    unnamed x20 -> x14, local copies, waits for them, and re-layouts: 10.4 us -> 6.8 us
where the time goes in v2:
time: 121 us; the launch traced here: 120 us
  Pallas kernels  107 us (88%)
  local copies, waits for them, and re-layouts  11.2 us (9%)
  other arithmetic  1.24 us (1%)
    pallas_call x1, Pallas kernels, layer(): pl.pallas_call(functools.partial(layer_kernel, rows, cols, scale, grad_sc...  107 us
    unnamed x14, local copies, waits for them, and re-layouts  6.8 us

profile of v2, /device:TPU:0, one launch (start us, length us, event | category | flops | bytes accessed | tf_op | source)
XLA Modules:
  0.0 120.2 jit_solution(2926586139891200416)
XLA Ops:
  0.6 1.3 %reshape.46.gain = f32[1,768]{1,0:T(1,128)} reshape(f32[768]{0:T(1024)} %param.14) | data formatting | bytes 6144 | tf_op jit(solution)/shard_map/reshape | solution.py:655
  1.9 0.8 copy.18
  2.7 0.1 broadcast_in_dim.10
  2.8 1.4 %copy.20.level = s32[64,1]{1,0:T(8,128)} copy(s32[64,1]{0,1:T(1,128)} %bitcast.19) | data formatting | bytes 512 | tf_op jit(solution)/shard_map/reshape | solution.py:657
  4.1 0.1 broadcast_in_dim.11
  4.2 0.8 reshape.49.ptok
  5.0 107.0 %layer.1 = (bf16[512,768]{1,0:T(8,128)(2,1)}, bf16[512,768]{1,0:T(8,128)(2,1)}, f32[64,768]{1,0:T(8,128)}, f32[192,2304]{1,0:T(8,128)}, f32[192,768]{1,0:T(8,128)}, /*index=5*/f32[2,8,384]{2,1,0:T(8,128)}) custom-call(bf16[512,768]{1,0:T(8,128)(2,1)} %bitcast.12, bf16[512,768]{1,0:T(8,128)(2,1)} %bitcast.13, s32[512,1]{1,0:T(8,128)} %reshape.49.ptok, ...), custom_call_target="tpu_custom_call" | custom-call | tf_op jit(solution)/shard_map/layer/pallas_call | solution.py:590
  112.1 0.0 copy-start.1
  112.1 0.0 copy-start.3
  112.1 0.8 slice_bitcast_fusion
  112.9 0.6 fusion
  113.5 0.6 pad_maximum_fusion
  114.2 0.0 copy-start
  114.2 2.2 %copy.26 = bf16[1,16,32,768]{3,2,1,0:T(8,128)(2,1)} copy(bf16[1,16,32,768]{3,2,1,0:T(8,128)(2,1)} %bitcast.15) | data formatting | bytes 1572864
  116.3 0.0 copy-done.1
  116.3 0.9 copy.27
  117.2 0.0 copy-done.3
  117.2 0.7 copy.28
  117.9 0.0 copy-done
  117.9 0.0 copy-start.2
  117.9 1.2 %copy.29 = f32[192,2304]{1,0:T(8,128)} copy(f32[192,2304]{1,0:T(8,128)S(1)} %copy-done) | data formatting | bytes 3538944
  119.1 0.3 copy-done.2
  119.4 0.8 copy.30
Async XLA Ops:
  112.1 4.3 %copy-start.1 = (bf16[512,768]{1,0:T(8,128)(2,1)S(1)}, bf16[512,768]{1,0:T(8,128)(2,1)}, u32[]{:S(2)}) copy-start(bf16[512,768]{1,0:T(8,128)(2,1)} %get-tuple-element.14) | copy-start | bytes 2359300
  112.1 5.1 %copy-start.3 = (f32[64,768]{1,0:T(8,128)S(1)}, f32[64,768]{1,0:T(8,128)}, u32[]{:S(2)}) copy-start(f32[64,768]{1,0:T(8,128)} %get-tuple-element.15) | copy-start | bytes 589828
  114.2 3.8 %copy-start = (f32[192,2304]{1,0:T(8,128)S(1)}, f32[192,2304]{1,0:T(8,128)}, u32[]{:S(2)}) copy-start(f32[192,2304]{1,0:T(8,128)} %get-tuple-element.31) | copy-start | bytes 5308420
  117.9 1.5 %copy-start.2 = (f32[192,768]{1,0:T(8,128)S(1)}, f32[192,768]{1,0:T(8,128)}, u32[]{:S(2)}) copy-start(f32[192,768]{1,0:T(8,128)} %get-tuple-element.32) | copy-start | bytes 1769476

commit v3 on v2

--- a/solution.py
+++ b/solution.py
@@ -18,6 +18,7 @@
 FYP = [(0, 1), (1, 0), (1, 1)]
 YZP = [(a, b) for a in range(4) for b in range(4) if (a, b) != (0, 0)]
 LANES = 128
+VMEM_LIMIT = 52 << 20
 
 
 def dims(a, b, ca, cb):
@@ -103,9 +104,13 @@
 
 class Reduce:
     @staticmethod
+    def gathered(rows, nb):
+        return (2, -(-(rows * nb // 16) // 16) * 256, LANES)
+
+    @staticmethod
     def scratch(rows, nb):
         dma = pltpu.SemaphoreType.DMA
-        piece = -(-(rows * nb // 16) // 16) * 16
+        piece = Reduce.gathered(rows, nb)[1] // 16
         return [
             pltpu.VMEM((4 * rows, nb * LANES), BF16),
             pltpu.VMEM((3, rows, nb * LANES), BF16),
@@ -113,12 +118,12 @@
             pltpu.VMEM((rows, nb * LANES), F32),
             pltpu.VMEM((16 * piece, LANES), BF16),
             pltpu.VMEM((15, piece, LANES), BF16),
-            pltpu.VMEM((2, 16 * piece, LANES), BF16),
             dma((2,)), dma((2,)), dma((3,)), dma((3,)), dma((15,)), dma((15,)), dma((15,)), dma((15,)),
         ]
 
-    def __init__(self, at, refs, rows, nb):
-        (self.cx, self.xs, self.xr, self.acc, self.p16, self.r16, self.ag,
+    def __init__(self, at, ag, refs, rows, nb):
+        self.ag = ag
+        (self.cx, self.xs, self.xr, self.acc, self.p16, self.r16,
          self.c_s, self.c_r, self.x_s, self.x_r, self.r_s, self.r_r, self.g_s, self.g_r) = refs
         self.at, self.rows, self.nb = at, rows, nb
         self.piece = self.r16.shape[1]
@@ -202,9 +207,6 @@
         ref = self.ag.at[1 - self.at.core]
         rcopy(ref, ref, self.c_s.at[1], self.c_r.at[1], self.partner).wait_recv()
 
-    def block(self, half, b):
-        return self.ag[half, b * self.rows : (b + 1) * self.rows, :].astype(F32)
-
 
 class Legs:
     def __init__(self, at, rows, cols, sems):
@@ -298,18 +300,18 @@
     return [{"fy": at.fy_at(1, 0), "fx": at.fx_at(a, b)} for a, b in FXP]
 
 
-N_RED = 15
+N_RED = 14
 
 
 def layer_kernel(
-    rows, cols, scale, grad_scale, fine_h, cot_h, ptok, coarse, level, table, gain, wq_h, wo_h,
-    mixed, gfine, gcoarse, gq, gout, small,
-    fine, cot, wq, wo, tab, perm, res, lv,
+    rows, cols, scale, fine_h, cot_h, parent, coarse, level, table, gain, wq_h, wo_h,
+    mixed_h, gfine_h, gcoarse_h, wsum_h, osum_h, small_h,
+    fine, cot, wq, wo, tab, perm, pick, res, lv,
     sn, sd, snc, sdc, rown, rowd, coln, cold, qkv, grads, w2,
     orow, gnr, ocol, gnc, orow_t, gnr_t, ocol_t, gnc_t, dd, oo, gg,
     att, go_out, go_own, co_out, co_in, co_own, cf_out, cf_in, cy_out, cy_in,
-    sm_own, sm_in, sm_mid, sm_in2,
-    ld, ag_s, ag_r, fw_s, fw_r, row_s, row_r, col_s, col_r, loc,
+    sm_own, sm_in, sm_mid, sm_in2, mixed, gfine, gcoarse, wsum, osum, small,
+    ld, st, ag_s, ag_r, fw_s, fw_r, row_s, row_r, col_s, col_r, loc,
     co_s, co_r, cf_s, cf_r, cy_s, cy_r, s1_s, s1_r, s2_s, s2_r, *red,
 ):
     at = Place()
@@ -317,15 +319,22 @@
     half = width // 2
     own = coarse.shape[0]
     part = own // 2
+    halfway = part * 8
     legs = Legs(at, rows, cols, (row_s, row_r, col_s, col_r, loc))
     fx_dev, fy_dev = legs.fx_dev, legs.fy_dev
     partner = fy_dev[0]
     dp_off = [(d, c) for d in range(4) for c in range(2) if (d, c) != (0, 0)]
     dp_dev = [{"dp": at.dp_at(d), "fy": at.fy_at(0, c)} for d, c in dp_off]
-    weights = Reduce(at, red[:N_RED], width // 4, 3 * half // LANES)
-    outs = Reduce(at, red[N_RED:], width // 4, half // LANES)
+    weights = Reduce(at, wsum, red[:N_RED], width // 4, 3 * half // LANES)
+    outs = Reduce(at, osum, red[N_RED:], width // 4, half // LANES)
     sent = legs.sent
     go = legs.send
+    stores = []
+
+    def store(src, dst):
+        c = pltpu.make_async_copy(src, dst, st.at[len(stores)])
+        c.start()
+        stores.append(c)
 
     loads = [
         pltpu.make_async_copy(a, b, ld.at[i])
@@ -333,17 +342,19 @@
     ]
     for c in loads:
         c.start()
-    mine = pl.ds(at.fx * own, own)
-    lev = level[...]
-    add = jnp.where(lev == 0, table[0:1, :], jnp.where(lev == 1, table[1:2, :], table[2:3, :]))
-    tab[mine, 0:width] = (coarse[...].astype(F32) + add).astype(BF16)
-    lane = lax.broadcasted_iota(jnp.int32, (own, LANES), 1)
-    tab[mine, width : width + LANES] = onehot(lane == lev + 1)
-    perm[...] = to_columns(rows, cols)
+    as_row = onehot(lax.broadcasted_iota(jnp.int32, (8, own), 0) == level[...] + 1)
+    same = lax.broadcasted_iota(jnp.int32, (8, LANES), 0) == lax.broadcasted_iota(jnp.int32, (8, LANES), 1)
+    lev = dims(as_row, onehot(same), 0, 0)
+    add = jnp.where(lev[:, 1:2] > 0.5, table[0:1, :], jnp.where(lev[:, 2:3] > 0.5, table[1:2, :], table[2:3, :]))
+    summary = (coarse[...].astype(F32) + add).astype(BF16)
+    for h in range(2):
+        mine = pl.ds(h * halfway + at.fx * part, part)
+        tab[mine, 0:width] = summary[h * part : (h + 1) * part]
+        tab[mine, width : width + LANES] = lev[h * part : (h + 1) * part].astype(BF16)
     greet(fx_dev + fy_dev[1:] + extra_devs(at) + dp_dev)
 
     def chunk(owner, core):
-        return tab.at[pl.ds(owner * own + core * part, part)]
+        return tab.at[pl.ds(core * halfway + owner * part, part)]
 
     def across(a, b):
         fx = at.fx_at(a, b)
@@ -351,6 +362,17 @@
 
     for i, (a, b) in enumerate(FXP):
         go(chunk(at.fx, at.core), chunk(at.fx, at.core), ag_s.at[i], ag_r.at[i], across(a, b))
+    perm[...] = to_columns(rows, cols)
+    p = parent[0]
+    p = lax.rem(p, own) // part * halfway + p // own * part + lax.rem(p, part)
+    token = lax.broadcasted_iota(jnp.int32, (n, rows), 0)
+    spread = onehot(token // cols == lax.broadcasted_iota(jnp.int32, (n, rows), 1))
+    high = dims(spread, (p // 16).astype(F32).astype(BF16), 1, 0)
+    low = dims(spread, lax.rem(p, 16).astype(F32).astype(BF16), 1, 0)
+    token = lax.broadcasted_iota(jnp.int32, high.shape, 0)
+    reads = lax.rem(token, cols) // BLK == lax.broadcasted_iota(jnp.int32, high.shape, 1)
+    ptok = jnp.sum(jnp.where(reads, high * 16.0 + low, 0.0), axis=-1, keepdims=True)
+    pick[...] = onehot(lax.broadcasted_iota(jnp.int32, (n, n), 1).astype(F32) == ptok)
     loads[0].wait()
     loads[1].wait()
     d = dims(cot[...], wo[...], 1, 1).astype(BF16)
@@ -366,13 +388,12 @@
     for i, (a, b) in enumerate(FXP):
         src = chunk(at.fx_at(a, 4 - b), 1 - at.core)
         rcopy(src, src, fw_s.at[i], fw_r.at[i], partner).wait_recv()
-    pick = onehot(lax.broadcasted_iota(jnp.int32, (n, tab.shape[0]), 1) == ptok[...])
-    read = dims(pick, tab[...], 1, 0)
+    read = dims(pick[...], tab[...], 1, 0)
     lv[...] = read[:, width : width + LANES].astype(BF16)
     residual = fine[...].astype(F32) + read[:, 0:width]
     res[...] = residual
     inv = lax.rsqrt(jnp.mean(residual * residual, axis=-1, keepdims=True) + 1e-06)
-    normed = (residual * inv * gain[...]).astype(BF16)
+    normed = (residual * inv * gain[...].reshape(1, width)).astype(BF16)
     sn[...] = normed.reshape(rows, cols, width)
     kept += [legs.out_row(0, u, sn, rown) for u in range(2)]
     snc[...] = dims(perm[...], normed, 1, 0).astype(BF16).reshape(cols, rows, width)
@@ -461,10 +482,6 @@
     def _():
         weights.along_x(lambda block: w2[1, block, :].astype(F32))
 
-    @pl.when(at.core == 0)
-    def _():
-        weights.gather_yz()
-
     for c in kept:
         c.wait()
     for u in range(2):
@@ -481,21 +498,8 @@
     go_own[...] = dims(att[...], cot_half(at.core), 0, 0)
     mixed[...] = (res[...] + dims(att[...], wo[...], 1, 0)).astype(BF16)
 
-    @pl.when(at.core == 0)
-    def _():
-        weights.swap_back()
-
-    @pl.when(at.core == 1)
-    def _():
-        weights.scatter_yz()
-
+    store(mixed, mixed_h)
     outs.along_x(lambda block: go_own[block, :])
-
-    @pl.when(at.core == 1)
-    def _():
-        weights.gather_yz()
-
-    outs.scatter_yz()
     for u in range(2):
         legs.back_row(3, u, gnr_t)
         legs.back_col(3, u, gnc_t)
@@ -504,31 +508,43 @@
     inv = lax.rsqrt(jnp.mean(residual * residual, axis=-1, keepdims=True) + 1e-06)
     pre = residual * inv
     sm_gain = jnp.sum(grad_normed * pre, axis=0, keepdims=True)
-    g = grad_normed * gain[...]
+    g = grad_normed * gain[...].reshape(1, width)
     grad_residual = inv * (g - pre * jnp.mean(g * pre, axis=-1, keepdims=True)) + cot[...].astype(F32)
     gf = grad_residual.astype(BF16)
     gfine[...] = gf
-    coarse_row = lax.broadcasted_iota(jnp.int32, (n, 8 * part), 1)
 
     def dense(core):
-        named = coarse_row // part * own + lax.rem(coarse_row, part) + core * part
-        return dims(onehot(named == ptok[...]), gf, 0, 0)
+        return dims(pick[:, pl.ds(pl.multiple_of(core * halfway, LANES), halfway)], gfine[...], 0, 0)
 
     co_out[...] = dense(1 - at.core).astype(BF16)
     go(co_out, co_in, co_s.at[0], co_r.at[0], partner)
-    levels = dims(lv[...], gf, 0, 0)[0:8]
+    levels = dims(lv[...], gfine[...], 0, 0)[0:8]
     row = lax.broadcasted_iota(jnp.int32, (8, half), 0)
-    sm_own[0] = jnp.where(row == 0, sm_gain[:, 0:half], levels[:, 0:half])
-    sm_own[1] = jnp.where(row == 0, sm_gain[:, half:width], levels[:, half:width])
+    for h in range(2):
+        c = h * half
+        both = jnp.where(row == 0, sm_gain[:, c : c + half], levels[:, c : c + half])
+        sm_own[4 * h : 4 * h + 4, :] = both[0:4]
     for i, dev in enumerate(dp_dev):
         go(sm_own, sm_in.at[i], s1_s.at[i], s1_r.at[i], dev)
     co_own[...] = dense(at.core)
+    store(gfine, gfine_h)
+
+    @pl.when(at.core == 0)
+    def _():
+        weights.gather_yz()
+
     rcopy(co_out, co_in, co_s.at[0], co_r.at[0], partner).wait_recv()
     for i, (a, b) in enumerate(FXP):
         owner = at.fx_at(a, b)
         block = pl.ds(pl.multiple_of(owner * part, part), part)
         cf_out[i] = (co_own[block, :] + co_in[block, :].astype(F32)).astype(BF16)
         go(cf_out.at[i], cf_in.at[i], cf_s.at[i], cf_r.at[i], fx_dev[i])
+
+    @pl.when(at.core == 1)
+    def _():
+        weights.scatter_yz()
+
+    outs.scatter_yz()
     total = sm_own[...]
     for i, dev in enumerate(dp_dev):
         rcopy(sm_own, sm_in.at[i], s1_s.at[i], s1_r.at[i], dev).wait_recv()
@@ -536,18 +552,11 @@
     sm_mid[...] = total
     for i, (a, b) in enumerate(YZP):
         go(sm_mid, sm_in2.at[i], s2_s.at[i], s2_r.at[i], at.yz(a, b)[0])
-    outs.gather_yz()
-
-    @pl.when(at.core == 1)
+
+    @pl.when(at.core == 0)
     def _():
         weights.swap_back()
 
-    weights.finish()
-    for h in range(2):
-        for j in range(3):
-            for b in range(half // LANES):
-                c0 = (2 * j + h) * half + b * LANES
-                gq[:, c0 : c0 + LANES] = weights.block(h, j * (half // LANES) + b) * grad_scale
     block = pl.ds(pl.multiple_of(at.fx * part, part), part)
     value = co_own[block, :] + co_in[block, :].astype(F32)
     for i in range(7):
@@ -556,28 +565,42 @@
     cy_out[...] = value.astype(BF16)
     for i, (a, c) in enumerate(FYP):
         go(cy_out, cy_in.at[i], cy_s.at[i], cy_r.at[i], fy_dev[i])
-    outs.swap_back()
+
+    @pl.when(at.core == 1)
+    def _():
+        weights.gather_yz()
+
+    outs.gather_yz()
     total = sm_mid[...]
     for i, (a, b) in enumerate(YZP):
         rcopy(sm_mid, sm_in2.at[i], s2_s.at[i], s2_r.at[i], at.yz(a, b)[0]).wait_recv()
         total = total + sm_in2[i]
-    small[...] = total * grad_scale
+    small[...] = total
+    store(small, small_h)
     for i in range(3):
         rcopy(cy_out, cy_in.at[i], cy_s.at[i], cy_r.at[i], fy_dev[i]).wait_recv()
     gcoarse[pl.ds(pl.multiple_of(at.core * part, part), part), :] = cy_out[...].astype(F32) + cy_in[1].astype(F32)
     gcoarse[pl.ds(pl.multiple_of((1 - at.core) * part, part), part), :] = cy_in[0].astype(F32) + cy_in[2].astype(F32)
+    store(gcoarse, gcoarse_h)
+
+    @pl.when(at.core == 1)
+    def _():
+        weights.swap_back()
+
+    outs.swap_back()
+    weights.finish()
+    store(wsum, wsum_h)
     outs.finish()
-    for h in range(2):
-        for b in range(half // LANES):
-            c0 = h * half + b * LANES
-            gout[:, c0 : c0 + LANES] = outs.block(h, b) * grad_scale
+    store(osum, osum_h)
     for c in sent:
         c.wait_send()
     weights.drain()
     outs.drain()
-
-
-def layer(fine, cot, ptok, coarse, level, table, gain, wq, wo, rows, cols, scale, grad_scale):
+    for c in stores:
+        c.wait()
+
+
+def layer(fine, cot, parent, coarse, level, table, gain, wq, wo, rows, cols, scale):
     n, width = fine.shape
     half = width // 2
     own = coarse.shape[0]
@@ -588,21 +611,21 @@
     here = pl.BlockSpec(memory_space=pltpu.VMEM)
     r2, c8, c4 = rows // 8, cols * 8, cols // 4
     return pl.pallas_call(
-        functools.partial(layer_kernel, rows, cols, scale, grad_scale),
+        functools.partial(layer_kernel, rows, cols, scale),
         name="layer",
         out_shape=[
             jax.ShapeDtypeStruct((n, width), BF16),
             jax.ShapeDtypeStruct((n, width), BF16),
             jax.ShapeDtypeStruct((own, width), F32),
-            jax.ShapeDtypeStruct((width // 4, 6 * half), F32),
-            jax.ShapeDtypeStruct((width // 4, width), F32),
-            jax.ShapeDtypeStruct((2, 8, half), F32),
+            jax.ShapeDtypeStruct(Reduce.gathered(width // 4, 3 * half // LANES), BF16),
+            jax.ShapeDtypeStruct(Reduce.gathered(width // 4, half // LANES), BF16),
+            jax.ShapeDtypeStruct((8, half), F32),
         ],
         in_specs=[hbm, hbm, here, here, here, here, here, hbm, hbm],
-        out_specs=[here] * 6,
+        out_specs=[hbm] * 6,
         scratch_shapes=[
             vmem((n, width), BF16), vmem((n, width), BF16), vmem((width, 6 * half), BF16), vmem((width, width), BF16),
-            vmem((8 * own, width + LANES), BF16), vmem((n, n), BF16), vmem((n, width), F32), vmem((n, LANES), BF16),
+            vmem((8 * own, width + LANES), BF16), vmem((n, n), BF16), vmem((n, n), BF16), vmem((n, width), F32), vmem((n, LANES), BF16),
             vmem((rows, cols, width), BF16), vmem((rows, cols, half), BF16),
             vmem((cols, rows, width), BF16), vmem((cols, rows, half), BF16),
             vmem((r2, c8, width), BF16), vmem((r2, c8, half), BF16),
@@ -617,8 +640,11 @@
             vmem((8 * part, width), BF16), vmem((8 * part, width), BF16), vmem((8 * part, width), F32),
             vmem((7, part, width), BF16), vmem((7, part, width), BF16),
             vmem((part, width), BF16), vmem((3, part, width), BF16),
-            vmem((2, 8, half), F32), vmem((7, 2, 8, half), F32), vmem((2, 8, half), F32), vmem((15, 2, 8, half), F32),
-            dma((4,)), dma((7,)), dma((7,)), dma((7,)), dma((7,)),
+            vmem((8, half), F32), vmem((7, 8, half), F32), vmem((8, half), F32), vmem((15, 8, half), F32),
+            vmem((n, width), BF16), vmem((n, width), BF16), vmem((own, width), F32),
+            vmem(Reduce.gathered(width // 4, 3 * half // LANES), BF16),
+            vmem(Reduce.gathered(width // 4, half // LANES), BF16), vmem((8, half), F32),
+            dma((4,)), dma((6,)), dma((7,)), dma((7,)), dma((7,)), dma((7,)),
             dma((4, 2, 7)), dma((4, 2, 7)), dma((4, 2, 3)), dma((4, 2, 3)), dma((4, 4)),
             dma((1,)), dma((1,)), dma((7,)), dma((7,)), dma((3,)), dma((3,)),
             dma((7,)), dma((7,)), dma((15,)), dma((15,)),
@@ -626,9 +652,56 @@
             *Reduce.scratch(width // 4, half // LANES),
         ],
         compiler_params=pltpu.CompilerParams(
-            collective_id=0, has_side_effects=True, vmem_limit_bytes=62 << 20
+            collective_id=0, has_side_effects=True, vmem_limit_bytes=VMEM_LIMIT
         ),
-    )(fine, cot, ptok, coarse, level, table, gain, wq, wo)
+    )(fine, cot, parent, coarse, level, table, gain, wq, wo)
+
+
+def emit_kernel(rows, grad_scale, mixed, gfine, gcoarse, wsum, osum, small, mixed_o, gfine_o, gcoarse_o, gq, gout, ggain, glevel):
+    mixed_o[...] = mixed[...]
+    gfine_o[...] = gfine[...]
+    gcoarse_o[...] = gcoarse[...]
+    half = small.shape[1]
+    nb = half // LANES
+    for h in range(2):
+        for j in range(3):
+            for b in range(nb):
+                c = (2 * j + h) * half + b * LANES
+                k = (j * nb + b) * rows
+                gq[:, c : c + LANES] = wsum[h, k : k + rows, :].astype(F32) * grad_scale
+        for b in range(nb):
+            c = h * half + b * LANES
+            gout[:, c : c + LANES] = osum[h, b * rows : (b + 1) * rows, :].astype(F32) * grad_scale
+        glevel[:, h * half : (h + 1) * half] = small[4 * h + 1 : 4 * h + 4, :] * grad_scale
+    dp = lax.axis_index("dp")
+    vector = jnp.concatenate([small[0:1, :], small[4:5, :]], axis=1) * grad_scale
+    share = vector[:, 0:rows]
+    for i in range(1, 4):
+        share = jnp.where(dp == i, vector[:, i * rows : (i + 1) * rows], share)
+    ggain[...] = share
+
+
+def emit(parts, grad_scale):
+    mixed, gfine, gcoarse, wsum, osum, small = parts
+    n, width = mixed.shape
+    rows = width // 4
+    here = pl.BlockSpec(memory_space=pltpu.VMEM)
+    return pl.pallas_call(
+        functools.partial(emit_kernel, rows, grad_scale),
+        name="emit",
+        out_shape=[
+            jax.ShapeDtypeStruct(mixed.shape, BF16),
+            jax.ShapeDtypeStruct(gfine.shape, BF16),
+            jax.ShapeDtypeStruct(gcoarse.shape, F32),
+            jax.ShapeDtypeStruct((rows, 3 * width), F32),
+            jax.ShapeDtypeStruct((rows, width), F32),
+            jax.ShapeDtypeStruct((1, rows), F32),
+            jax.ShapeDtypeStruct((LEVELS, width), F32),
+        ],
+        in_specs=[here] * 6,
+        out_specs=[here] * 7,
+        compiler_params=pltpu.CompilerParams(vmem_limit_bytes=24 << 20),
+    )(*parts)
 
 
 def local(
@@ -651,23 +724,19 @@
     grad_scale = 1.0 / math.sqrt(total_tokens)
     fine = fine_tokens.reshape(n, width)
     cot = cotangent.reshape(n, width)
-    ptok = jnp.broadcast_to(parent.reshape(n // BLK, 1), (n // BLK, BLK)).reshape(n, 1)
-    gain = norm_gain.reshape(1, width)
-    mixed, gfine, gcoarse, gq, gout, small = layer(
-        fine, cot, ptok, coarse_tokens.reshape(own, width), tile_level.reshape(own, 1),
-        level_table, gain, qkv_weight, out_weight, rows, cols, scale, grad_scale,
+    parts = layer(
+        fine, cot, parent, coarse_tokens.reshape(own, width), tile_level,
+        level_table, norm_gain, qkv_weight, out_weight, rows, cols, scale,
     )
-    vectors = jnp.concatenate([small[0], small[1]], axis=-1)
-    share = width // 4
-    ggain = lax.dynamic_slice_in_dim(vectors[0], lax.axis_index("dp") * share, share)
+    mixed, gfine, gcoarse, gq, gout, ggain, glevel = emit(parts, grad_scale)
     return (
         mixed.reshape(fine_tokens.shape),
         gfine.reshape(fine_tokens.shape),
         gcoarse[None],
         gq,
         gout,
-        ggain,
-        vectors[1 : 1 + LEVELS],
+        ggain.reshape(-1),
+        glevel,
     )
 
 

time: 121 us -> 108 us (0.89)
  Pallas kernels: 107 us -> 100 us
  local copies, waits for them, and re-layouts: 11.2 us -> 6 us
  other arithmetic: 1.24 us -> 0 us
    pallas_call x1 -> x2, Pallas kernels: 107 us -> 100 us  [the longest x1 97.9 us: layer(): pl.pallas_call(functools.partial(layer_kernel, rows, cols, scale), name='...]
    reshape x3 -> x0, local copies, waits for them, and re-layouts: 3.46 us -> none  [the longest x1 1.36 us: local(): tile_level.reshape(own, 1)]
    unnamed x14 -> x13, local copies, waits for them, and re-layouts: 6.8 us -> 6 us
where the time goes in v3:
time: 108 us; the launch traced here: 107 us
  Pallas kernels  100 us (93%)
  local copies, waits for them, and re-layouts  6 us (6%)
    pallas_call x1, Pallas kernels, layer(): pl.pallas_call(functools.partial(layer_kernel, rows, cols, scale), name='...  97.9 us
    unnamed x13, local copies, waits for them, and re-layouts  6 us
    pallas_call x1, Pallas kernels, emit(): pl.pallas_call(functools.partial(emit_kernel, rows, grad_scale), name='em...  2.2 us

profile of v3, /device:TPU:0, one launch (start us, length us, event | category | flops | bytes accessed | tf_op | source)
XLA Modules:
  0.0 106.7 jit_solution(12445309937385096523)
XLA Ops:
  0.6 0.8 copy.16.parent
  1.4 0.0 copy-start.2
  1.4 0.9 copy-done.2
  2.3 0.0 copy-start.3
  2.3 0.7 copy-done.3
  3.0 0.0 copy-start.4
  3.0 0.7 copy-done.4
  3.7 0.0 copy-start.5
  3.7 0.7 copy-done.5
  4.3 97.9 %layer.1 = (bf16[512,768]{1,0:T(8,128)(2,1)S(1)}, bf16[512,768]{1,0:T(8,128)(2,1)}, f32[64,768]{1,0:T(8,128)S(1)}, bf16[2,1792,128]{2,1,0:T(8,128)(2,1)}, bf16[2...) custom-call(bf16[512,768]{1,0:T(8,128)(2,1)} %bitcast.8, bf16[512,768]{1,0:T(8,128)(2,1)} %bitcast.9, ...), custom_call_target="tpu_custom_call" | custom-call | tf_op jit(solution)/shard_map/layer/pallas_call | solution.py:613
  102.2 0.0 copy-start
  102.2 1.2 %copy-done = bf16[2,1792,128]{2,1,0:T(8,128)(2,1)S(1)} copy-done((bf16[2,1792,128]{2,1,0:T(8,128)(2,1)S(1)}, bf16[2,1792,128]{2,1,0:T(8,128)(2,1)}, u32[]{:S(2)}) %copy-start) | copy-done | bytes 917528
  103.4 0.0 copy-start.1
  103.4 1.1 %copy-done.1 = bf16[512,768]{1,0:T(8,128)(2,1)S(1)} copy-done((bf16[512,768]{1,0:T(8,128)(2,1)S(1)}, bf16[512,768]{1,0:T(8,128)(2,1)}, u32[]{:S(2)}) %copy-start.1) | copy-done | bytes 786456
  104.5 2.2 %emit.1 = (bf16[512,768]{1,0:T(8,128)(2,1)}, bf16[512,768]{1,0:T(8,128)(2,1)}, f32[64,768]{1,0:T(8,128)}, f32[192,2304]{1,0:T(8,128)}, f32[192,768]{1,0:T(8,128)}, /*index=5*/f32[1,192]{1,0:T(1,128)}, f32[3,768]{1,0:T(4,128)}) custom-call(bf16[512,768]{1,0:T(8,128)(2,1)S(1)} %get-tuple-element.20.mixed, bf16[512,768]{1,0:T(8,128)(2,1)S(1)} %copy-done.1, ...), custom_call_target="tpu_custom_call" | custom-call | tf_op jit(solution)/shard_map/emit/pallas_call | solution.py:689
Async XLA Ops:
  1.4 0.9 copy-start.2
  2.3 0.7 copy-start.3
  3.0 0.7 copy-start.4
  3.7 0.7 copy-start.5
  102.2 1.2 %copy-start = (bf16[2,1792,128]{2,1,0:T(8,128)(2,1)S(1)}, bf16[2,1792,128]{2,1,0:T(8,128)(2,1)}, u32[]{:S(2)}) copy-start(bf16[2,1792,128]{2,1,0:T(8,128)(2,1)} %get-tuple-element.23.wsum) | copy-start | bytes 2752516
  103.4 1.1 %copy-start.1 = (bf16[512,768]{1,0:T(8,128)(2,1)S(1)}, bf16[512,768]{1,0:T(8,128)(2,1)}, u32[]{:S(2)}) copy-start(bf16[512,768]{1,0:T(8,128)(2,1)} %get-tuple-element.21.gfine) | copy-start | bytes 2359300

commit v4 on v3

--- a/solution.py
+++ b/solution.py
@@ -18,6 +18,7 @@
 FYP = [(0, 1), (1, 0), (1, 1)]
 YZP = [(a, b) for a in range(4) for b in range(4) if (a, b) != (0, 0)]
 LANES = 128
+X_ORDER = (2, 1, 3, 0)
 VMEM_LIMIT = 52 << 20
 
 
@@ -43,7 +44,7 @@
     def yz(self, a, b):
         z, y = lax.rem(self.z + a, 4), lax.rem(self.y + b, 4)
         dev = {"fy": (z // 2) * 2 + self.core, "fx": (z % 2) * 4 + y}
-        return dev, z * 4 + y
+        return dev, y * 4 + z
 
     def dp_at(self, d):
         return lax.rem(self.dp + d, 4)
@@ -117,52 +118,65 @@
             pltpu.VMEM((3, rows, nb * LANES), BF16),
             pltpu.VMEM((rows, nb * LANES), F32),
             pltpu.VMEM((16 * piece, LANES), BF16),
-            pltpu.VMEM((15, piece, LANES), BF16),
-            dma((2,)), dma((2,)), dma((3,)), dma((3,)), dma((15,)), dma((15,)), dma((15,)), dma((15,)),
+            pltpu.VMEM((3, 4 * piece, LANES), BF16),
+            pltpu.VMEM((4 * piece, LANES), BF16),
+            pltpu.VMEM((3, piece, LANES), BF16),
+            dma((2,)), dma((5,)), dma((1,)), dma((1,)), dma((2,)), dma((2,)), dma((2,)), dma((2,)),
         ]
 
     def __init__(self, at, ag, refs, rows, nb):
         self.ag = ag
-        (self.cx, self.xs, self.xr, self.acc, self.p16, self.r16,
+        (self.cx, self.xs, self.xr, self.acc, self.p16, self.ry, self.py, self.rz,
          self.c_s, self.c_r, self.x_s, self.x_r, self.r_s, self.r_r, self.g_s, self.g_r) = refs
         self.at, self.rows, self.nb = at, rows, nb
-        self.piece = self.r16.shape[1]
+        self.piece = self.rz.shape[1]
         self.partner = {"fy": at.fy_at(0, 1)}
 
     def go(self, c):
         c.start()
 
+    def x_block(self, d):
+        return pl.ds(pl.multiple_of(self.at.dp_at(d) * self.rows, self.rows), self.rows)
+
+    def swap_block(self, src, d):
+        rows = self.x_block(d)
+        return rcopy(src.at[rows], self.cx.at[rows], self.c_s.at[0], self.c_r.at[d], self.partner)
+
     def swap(self, src):
-        return rcopy(src, self.cx, self.c_s.at[0], self.c_r.at[0], self.partner)
-
-    def drain(self):
-        rcopy(self.cx, self.cx, self.c_s.at[0], self.c_r.at[0], self.partner).wait_send()
-        ref = self.ag.at[self.at.core]
-        rcopy(ref, ref, self.c_s.at[1], self.c_r.at[1], self.partner).wait_send()
-        for d in range(3):
-            rcopy(self.xs.at[d], self.xr.at[d], self.x_s.at[d], self.x_r.at[d], self.partner).wait_send()
-        for i in range(15):
-            ref = self.r16.at[i]
-            rcopy(ref, ref, self.r_s.at[i], self.r_r.at[i], self.partner).wait_send()
-            rcopy(ref, ref, self.g_s.at[i], self.g_r.at[i], self.partner).wait_send()
-
-    def along_x(self, mine):
-        self.swap(self.cx).wait_recv()
-        for d in (2, 1, 3, 0):
+        for d in X_ORDER:
+            self.swap_block(src, d).start()
+
+    def along_x(self, mine, order=X_ORDER):
+        for d in order:
+            self.swap_block(self.cx, d).wait_recv()
             i = self.at.dp_at(d)
-            block = pl.ds(pl.multiple_of(i * self.rows, self.rows), self.rows)
+            block = self.x_block(d)
             value = mine(block) + self.cx[block, :].astype(F32)
             if d == 0:
                 self.acc[...] = value
             else:
                 self.xs[d - 1] = value.astype(BF16)
-                self.go(rcopy(
-                    self.xs.at[d - 1], self.xr.at[d - 1], self.x_s.at[d - 1], self.x_r.at[d - 1], {"dp": i}
-                ))
-
-    def scatter_yz(self):
-        for d in range(3):
-            rcopy(self.xs.at[d], self.xr.at[d], self.x_s.at[d], self.x_r.at[d], {"dp": self.at.dp}).wait_recv()
+                rcopy(self.xs.at[d - 1], self.xr.at[d - 1], self.x_s.at[0], self.x_r.at[0], {"dp": i}).start()
+
+
+    def ahead(self, z_first, k, stage):
+        return self.at.yz(k, 0)[0] if z_first == (stage == 0) else self.at.yz(0, k)[0]
+
+    def major(self, z_first):
+        return self.at.z if z_first else self.at.y
+
+    def minor(self, z_first):
+        return self.at.y if z_first else self.at.z
+
+    def column(self, z_first, k):
+        size = 4 * self.piece
+        return pl.ds(pl.multiple_of(lax.rem(self.major(z_first) + k, 4) * size, size), size)
+
+    def slot(self, q):
+        return pl.ds(pl.multiple_of(q * self.piece, self.piece), self.piece)
+
+    def scatter(self, z_first):
+        rcopy(self.xs, self.xr, self.x_s.at[0], self.x_r.at[0], self.partner).wait_recv()
         rows = self.rows
         for b in range(self.nb):
             lanes = slice(b * LANES, (b + 1) * LANES)
@@ -173,39 +187,61 @@
         used = self.nb * rows
         if used < self.p16.shape[0]:
             self.p16[used:, :] = jnp.zeros((self.p16.shape[0] - used, LANES), BF16)
-        for i, (a, b) in enumerate(YZP):
-            dev, q = self.at.yz(a, b)
-            self.go(rcopy(self.p16.at[self.slot(q)], self.r16.at[i], self.r_s.at[i], self.r_r.at[i], dev))
-
-    def slot(self, q):
-        return pl.ds(pl.multiple_of(q * self.piece, self.piece), self.piece)
-
-    def gather_yz(self):
+        for k in range(1, 4):
+            src = self.p16.at[self.column(z_first, k)]
+            rcopy(src, self.ry.at[k - 1], self.r_s.at[0], self.r_r.at[0], self.ahead(z_first, k, 0)).start()
+
+    def scatter_again(self, z_first):
+        rcopy(self.ry, self.ry, self.r_s.at[0], self.r_r.at[0], self.partner).wait_recv()
+        value = self.p16[self.column(z_first, 0), :].astype(F32)
+        for i in range(3):
+            value = value + self.ry[i].astype(F32)
+        self.py[...] = value.astype(BF16)
+        for k in range(1, 4):
+            src = self.py.at[self.slot(lax.rem(self.minor(z_first) + k, 4))]
+            rcopy(src, self.rz.at[k - 1], self.r_s.at[1], self.r_r.at[1], self.ahead(z_first, k, 1)).start()
+
+    def gather(self, z_first):
         at = self.at
-        _, q = at.yz(0, 0)
-        value = self.p16[self.slot(q), :].astype(F32)
-        for i in range(15):
-            dev, _ = at.yz(*YZP[i])
-            rcopy(self.r16.at[i], self.r16.at[i], self.r_s.at[i], self.r_r.at[i], dev).wait_recv()
-            value = value + self.r16[i].astype(F32)
-        self.ag[at.core, self.slot(q), :] = value.astype(BF16)
-        src = self.ag.at[at.core, self.slot(q)]
-        for i, (a, b) in enumerate(YZP):
-            dev, _ = at.yz(a, b)
-            self.go(rcopy(src, src, self.g_s.at[i], self.g_r.at[i], dev))
+        rcopy(self.rz, self.rz, self.r_s.at[1], self.r_r.at[1], self.partner).wait_recv()
+        value = self.py[self.slot(self.minor(z_first)), :].astype(F32)
+        for i in range(3):
+            value = value + self.rz[i].astype(F32)
+        mine = self.slot(self.major(z_first) * 4 + self.minor(z_first))
+        self.ag[at.core, mine, :] = value.astype(BF16)
+        src = self.ag.at[at.core, mine]
+        for k in range(1, 4):
+            rcopy(src, src, self.g_s.at[0], self.g_r.at[0], self.ahead(z_first, k, 1)).start()
+
+    def pieces(self, stage):
+        size = 3 * self.piece * (4 if stage else 1)
+        ref = self.ag.at[self.at.core, pl.ds(0, size)]
+        return rcopy(ref, ref, self.g_s.at[stage], self.g_r.at[stage], self.partner)
+
+    def gather_again(self, z_first):
+        self.pieces(0).wait_recv()
+        src = self.ag.at[self.at.core, self.column(z_first, 0)]
+        for k in range(1, 4):
+            rcopy(src, src, self.g_s.at[1], self.g_r.at[1], self.ahead(z_first, k, 0)).start()
 
     def swap_back(self):
-        at = self.at
-        for i, (a, b) in enumerate(YZP):
-            dev, q = at.yz(4 - a, 4 - b)
-            ref = self.ag.at[at.core, self.slot(q)]
-            rcopy(ref, ref, self.g_s.at[i], self.g_r.at[i], dev).wait_recv()
-        ref = self.ag.at[at.core]
-        self.go(rcopy(ref, ref, self.c_s.at[1], self.c_r.at[1], self.partner))
+        self.pieces(1).wait_recv()
+        ref = self.ag.at[self.at.core]
+        rcopy(ref, ref, self.c_s.at[1], self.c_r.at[4], self.partner).start()
 
     def finish(self):
         ref = self.ag.at[1 - self.at.core]
-        rcopy(ref, ref, self.c_s.at[1], self.c_r.at[1], self.partner).wait_recv()
+        rcopy(ref, ref, self.c_s.at[1], self.c_r.at[4], self.partner).wait_recv()
+
+    def drain(self):
+        rcopy(self.cx, self.cx, self.c_s.at[0], self.c_r.at[0], self.partner).wait_send()
+        rcopy(self.xs, self.xr, self.x_s.at[0], self.x_r.at[0], self.partner).wait_send()
+        rcopy(self.ry, self.ry, self.r_s.at[0], self.r_r.at[0], self.partner).wait_send()
+        rcopy(self.rz, self.rz, self.r_s.at[1], self.r_r.at[1], self.partner).wait_send()
+        self.pieces(0).wait_send()
+        self.pieces(1).wait_send()
+        ref = self.ag.at[self.at.core]
+        rcopy(ref, ref, self.c_s.at[1], self.c_r.at[4], self.partner).wait_send()
 
 
 class Legs:
@@ -217,15 +253,13 @@
         self.sent = []
         self.kept = []
 
-    def send(self, src, dst, ss, rs, dev):
-        c = rcopy(src, dst, ss, rs, dev)
-        c.start()
-        self.sent.append(c)
+    def gone(self, ref, ss, rs):
+        self.sent.append(rcopy(ref, ref, ss, rs, self.fx_dev[0]))
 
     def keep(self, src, dst, sem):
         c = pltpu.make_async_copy(src, dst, sem)
         c.start()
-        return c
+        self.kept.append(c)
 
     def token_row(self, ref, u, owner):
         return ref.at[pl.ds(owner * 2 + u, 1)]
@@ -239,77 +273,90 @@
     def owner_col(self, ref, u, member):
         return ref.at[pl.ds(u * (self.cols // 8), self.cols // 8), pl.ds(member * self.rows, self.rows)]
 
+    def tokens_row(self, ref):
+        return ref.at[pl.ds(0, 7)]
+
+    def tokens_col(self, ref):
+        return ref.at[pl.ds(0, 3 * (self.cols // 8))]
+
+    def owners_row(self, ref, u):
+        return ref.at[pl.ds(u, 1), pl.ds(0, 7 * self.cols)]
+
+    def owners_col(self, ref, u):
+        return ref.at[pl.ds(u * (self.cols // 8), self.cols // 8), pl.ds(0, 3 * self.rows)]
+
     def out_row(self, kind, u, src, dst):
-        at = self.at
+        at, ss, rs = self.at, self.row_s.at[kind, u], self.row_r.at[kind, u]
         for i, (a, b) in enumerate(FXP):
-            self.send(
-                self.token_row(src, u, at.fx_at(a, b)), self.owner_row(dst, u, at.fx),
-                self.row_s.at[kind, u, i], self.row_r.at[kind, u, i], self.fx_dev[i],
-            )
-        return self.keep(self.token_row(src, u, at.fx), self.owner_row(dst, u, at.fx), self.loc.at[kind, u])
+            rcopy(
+                self.token_row(src, u, at.fx_at(a, b)), self.owner_row(dst, u, at.fx), ss, rs, self.fx_dev[i]
+            ).start()
+        self.gone(self.tokens_row(src), ss, rs)
+        self.keep(self.token_row(src, u, at.fx), self.owner_row(dst, u, at.fx), self.loc.at[kind, u])
 
     def out_col(self, kind, u, src, dst):
-        at = self.at
+        at, ss, rs = self.at, self.col_s.at[kind, u], self.col_r.at[kind, u]
         for i, (a, c) in enumerate(FYP):
-            self.send(
-                self.token_col(src, u, at.fy_at(a, c)), self.owner_col(dst, u, at.fy),
-                self.col_s.at[kind, u, i], self.col_r.at[kind, u, i], self.fy_dev[i],
-            )
-        return self.keep(self.token_col(src, u, at.fy), self.owner_col(dst, u, at.fy), self.loc.at[kind, 2 + u])
+            rcopy(
+                self.token_col(src, u, at.fy_at(a, c)), self.owner_col(dst, u, at.fy), ss, rs, self.fy_dev[i]
+            ).start()
+        self.gone(self.tokens_col(src), ss, rs)
+        self.keep(self.token_col(src, u, at.fy), self.owner_col(dst, u, at.fy), self.loc.at[kind, 2 + u])
 
     def got_row(self, kind, u, dst):
+        ref = self.owners_row(dst, u)
+        rcopy(ref, ref, self.row_s.at[kind, u], self.row_r.at[kind, u], self.fx_dev[0]).wait_recv()
+
+    def got_col(self, kind, u, dst):
+        ref = self.owners_col(dst, u)
+        rcopy(ref, ref, self.col_s.at[kind, u], self.col_r.at[kind, u], self.fx_dev[0]).wait_recv()
+
+    def home_row(self, kind, u, src, dst):
+        at, ss, rs = self.at, self.row_s.at[kind, u], self.row_r.at[kind, u]
         for i, (a, b) in enumerate(FXP):
-            ref = self.owner_row(dst, u, self.at.fx_at(a, 4 - b))
-            rcopy(ref, ref, self.row_s.at[kind, u, i], self.row_r.at[kind, u, i], self.fx_dev[i]).wait_recv()
-
-    def got_col(self, kind, u, dst):
+            rcopy(
+                self.owner_row(src, u, at.fx_at(a, b)), self.token_row(dst, u, at.fx), ss, rs, self.fx_dev[i]
+            ).start()
+        self.gone(self.owners_row(src, u), ss, rs)
+        self.keep(self.owner_row(src, u, at.fx), self.token_row(dst, u, at.fx), self.loc.at[kind, u])
+
+    def home_col(self, kind, u, src, dst):
+        at, ss, rs = self.at, self.col_s.at[kind, u], self.col_r.at[kind, u]
         for i, (a, c) in enumerate(FYP):
-            ref = self.owner_col(dst, u, self.at.fy_at(a, c))
-            rcopy(ref, ref, self.col_s.at[kind, u, i], self.col_r.at[kind, u, i], self.fy_dev[i]).wait_recv()
-
-    def home_row(self, kind, u, src, dst):
-        at = self.at
-        for i, (a, b) in enumerate(FXP):
-            self.send(
-                self.owner_row(src, u, at.fx_at(a, b)), self.token_row(dst, u, at.fx),
-                self.row_s.at[kind, u, i], self.row_r.at[kind, u, i], self.fx_dev[i],
-            )
-        return self.keep(self.owner_row(src, u, at.fx), self.token_row(dst, u, at.fx), self.loc.at[kind, u])
-
-    def home_col(self, kind, u, src, dst):
-        at = self.at
-        for i, (a, c) in enumerate(FYP):
-            self.send(
-                self.owner_col(src, u, at.fy_at(a, c)), self.token_col(dst, u, at.fy),
-                self.col_s.at[kind, u, i], self.col_r.at[kind, u, i], self.fy_dev[i],
-            )
-        return self.keep(self.owner_col(src, u, at.fy), self.token_col(dst, u, at.fy), self.loc.at[kind, 2 + u])
+            rcopy(
+                self.owner_col(src, u, at.fy_at(a, c)), self.token_col(dst, u, at.fy), ss, rs, self.fy_dev[i]
+            ).start()
+        self.gone(self.owners_col(src, u), ss, rs)
+        self.keep(self.owner_col(src, u, at.fy), self.token_col(dst, u, at.fy), self.loc.at[kind, 2 + u])
 
     def back_row(self, kind, u, dst):
-        for i, (a, b) in enumerate(FXP):
-            ref = self.token_row(dst, u, self.at.fx_at(a, 4 - b))
-            rcopy(ref, ref, self.row_s.at[kind, u, i], self.row_r.at[kind, u, i], self.fx_dev[i]).wait_recv()
+        ref = self.tokens_row(dst)
+        rcopy(ref, ref, self.row_s.at[kind, u], self.row_r.at[kind, u], self.fx_dev[0]).wait_recv()
 
     def back_col(self, kind, u, dst):
-        for i, (a, c) in enumerate(FYP):
-            ref = self.token_col(dst, u, self.at.fy_at(a, c))
-            rcopy(ref, ref, self.col_s.at[kind, u, i], self.col_r.at[kind, u, i], self.fy_dev[i]).wait_recv()
+        ref = self.tokens_col(dst)
+        rcopy(ref, ref, self.col_s.at[kind, u], self.col_r.at[kind, u], self.fx_dev[0]).wait_recv()
+
+    def settle(self):
+        for c in self.kept:
+            c.wait()
+        self.kept = []
 
 
 def extra_devs(at):
     return [{"fy": at.fy_at(1, 0), "fx": at.fx_at(a, b)} for a, b in FXP]
 
 
-N_RED = 14
+N_RED = 16
 
 
 def layer_kernel(
-    rows, cols, scale, fine_h, cot_h, parent, coarse, level, table, gain, wq_h, wo_h,
+    rows, cols, scale, fine_h, cot_h, parent_h, coarse_h, level_h, table_h, gain_h, wq_h, wo_h,
     mixed_h, gfine_h, gcoarse_h, wsum_h, osum_h, small_h,
-    fine, cot, wq, wo, tab, perm, pick, res, lv,
+    parent, coarse, level, table, gain, fine, cot, wq, wo, tab, perm, pick, res, lv,
     sn, sd, snc, sdc, rown, rowd, coln, cold, qkv, grads, w2,
     orow, gnr, ocol, gnc, orow_t, gnr_t, ocol_t, gnc_t, dd, oo, gg,
-    att, go_out, go_own, co_out, co_in, co_own, cf_out, cf_in, cy_out, cy_in,
+    att, go_out, go_own, co_out, co_in, co_own, cf_out, cf_in, cz, cy_out, cy_in, cc_out, cc_in,
     sm_own, sm_in, sm_mid, sm_in2, mixed, gfine, gcoarse, wsum, osum, small,
     ld, st, ag_s, ag_r, fw_s, fw_r, row_s, row_r, col_s, col_r, loc,
     co_s, co_r, cf_s, cf_r, cy_s, cy_r, s1_s, s1_r, s2_s, s2_r, *red,
@@ -328,7 +375,6 @@
     weights = Reduce(at, wsum, red[:N_RED], width // 4, 3 * half // LANES)
     outs = Reduce(at, osum, red[N_RED:], width // 4, half // LANES)
     sent = legs.sent
-    go = legs.send
     stores = []
 
     def store(src, dst):
@@ -338,10 +384,15 @@
 
     loads = [
         pltpu.make_async_copy(a, b, ld.at[i])
-        for i, (a, b) in enumerate(((cot_h, cot), (wo_h, wo), (fine_h, fine), (wq_h, wq)))
+        for i, (a, b) in enumerate((
+            (cot_h, cot), (wo_h, wo), (fine_h, fine), (wq_h, wq),
+            (level_h, level), (table_h, table), (coarse_h, coarse), (parent_h, parent), (gain_h, gain),
+        ))
     ]
-    for c in loads:
-        c.start()
+    for i in (4, 5, 6, 7, 8, 0, 1, 2, 3):
+        loads[i].start()
+    for i in (4, 5, 6, 7, 8):
+        loads[i].wait()
     as_row = onehot(lax.broadcasted_iota(jnp.int32, (8, own), 0) == level[...] + 1)
     same = lax.broadcasted_iota(jnp.int32, (8, LANES), 0) == lax.broadcasted_iota(jnp.int32, (8, LANES), 1)
     lev = dims(as_row, onehot(same), 0, 0)
@@ -361,14 +412,14 @@
         return {"fx": fx} if a == 0 else {"fx": fx, "fy": at.fy_at(at.core, 0)}
 
     for i, (a, b) in enumerate(FXP):
-        go(chunk(at.fx, at.core), chunk(at.fx, at.core), ag_s.at[i], ag_r.at[i], across(a, b))
+        rcopy(chunk(at.fx, at.core), chunk(at.fx, at.core), ag_s.at[0], ag_r.at[i], across(a, b)).start()
     perm[...] = to_columns(rows, cols)
     p = parent[0]
     p = lax.rem(p, own) // part * halfway + p // own * part + lax.rem(p, part)
     token = lax.broadcasted_iota(jnp.int32, (n, rows), 0)
     spread = onehot(token // cols == lax.broadcasted_iota(jnp.int32, (n, rows), 1))
-    high = dims(spread, (p // 16).astype(F32).astype(BF16), 1, 0)
-    low = dims(spread, lax.rem(p, 16).astype(F32).astype(BF16), 1, 0)
+    high = dims(spread, (p // 16).astype(F32).astype(BF16), 1, 1)
+    low = dims(spread, lax.rem(p, 16).astype(F32).astype(BF16), 1, 1)
     token = lax.broadcasted_iota(jnp.int32, high.shape, 0)
     reads = lax.rem(token, cols) // BLK == lax.broadcasted_iota(jnp.int32, high.shape, 1)
     ptok = jnp.sum(jnp.where(reads, high * 16.0 + low, 0.0), axis=-1, keepdims=True)
@@ -377,17 +428,20 @@
     loads[1].wait()
     d = dims(cot[...], wo[...], 1, 1).astype(BF16)
     sd[...] = d[:, 0:half].reshape(rows, cols, half)
-    kept = [legs.out_row(1, u, sd, rowd) for u in range(2)]
+    for u in range(2):
+        legs.out_row(1, u, sd, rowd)
     sdc[...] = dims(perm[...], d[:, half:width], 1, 0).astype(BF16).reshape(cols, rows, half)
-    kept += [legs.out_col(1, u, sdc, cold) for u in range(2)]
+    for u in range(2):
+        legs.out_col(1, u, sdc, cold)
     for i, (a, b) in enumerate(FXP):
         src = chunk(at.fx_at(a, 4 - b), at.core)
-        rcopy(src, src, ag_s.at[i], ag_r.at[i], across(a, b)).wait_recv()
-        go(src, src, fw_s.at[i], fw_r.at[i], partner)
+        rcopy(src, src, ag_s.at[0], ag_r.at[i], across(a, b)).wait_recv()
+        rcopy(src, src, fw_s.at[0], fw_r.at[0], partner).start()
     loads[2].wait()
-    for i, (a, b) in enumerate(FXP):
-        src = chunk(at.fx_at(a, 4 - b), 1 - at.core)
-        rcopy(src, src, fw_s.at[i], fw_r.at[i], partner).wait_recv()
+    seven = tab.at[pl.ds(0, 7 * part)]
+    legs.gone(seven, ag_s.at[0], ag_r.at[0])
+    legs.gone(seven, fw_s.at[0], fw_r.at[0])
+    rcopy(seven, seven, fw_s.at[0], fw_r.at[0], partner).wait_recv()
     read = dims(pick[...], tab[...], 1, 0)
     lv[...] = read[:, width : width + LANES].astype(BF16)
     residual = fine[...].astype(F32) + read[:, 0:width]
@@ -395,13 +449,13 @@
     inv = lax.rsqrt(jnp.mean(residual * residual, axis=-1, keepdims=True) + 1e-06)
     normed = (residual * inv * gain[...].reshape(1, width)).astype(BF16)
     sn[...] = normed.reshape(rows, cols, width)
-    kept += [legs.out_row(0, u, sn, rown) for u in range(2)]
+    for u in range(2):
+        legs.out_row(0, u, sn, rown)
     snc[...] = dims(perm[...], normed, 1, 0).astype(BF16).reshape(cols, rows, width)
-    kept += [legs.out_col(0, u, snc, coln) for u in range(2)]
+    for u in range(2):
+        legs.out_col(0, u, snc, coln)
     loads[3].wait()
-    for c in kept:
-        c.wait()
-    kept = []
+    legs.settle()
 
     size = n // 2
     pair = 2 * 4 * rows
@@ -409,7 +463,7 @@
     j = lax.broadcasted_iota(jnp.int32, (2 * pair, pair), 1)
     mask = lax.rem(i, pair) // (4 * rows) == j // (4 * rows)
 
-    def unit(which, u, x, d, out, gn):
+    def unit(which, u, x, d, out, gn, between=None):
         for j in range(3):
             c0 = (2 * j + which) * half
             qkv[:, j * half : (j + 1) * half] = dims(x, wq[:, c0 : c0 + half], 1, 0).astype(BF16)
@@ -428,7 +482,12 @@
                     grads[which, g, j * half + c : j * half + c + LANES] = value
             return 0
 
-        lax.fori_loop(0, size // t_size, one, 0)
+        if between is None:
+            lax.fori_loop(0, size // t_size, one, 0)
+        else:
+            one(0, 0)
+            between()
+            lax.fori_loop(1, size // t_size, one, 0)
         total = None
         for j in range(3):
             c0 = (2 * j + which) * half
@@ -446,44 +505,57 @@
         legs.got_row(1, u, rowd)
         legs.got_row(0, u, rown)
         unit(0, u, rown[u], rowd.at[u], orow.at[u], gnr.at[u])
-        kept.append(legs.home_row(2, u, orow, orow_t))
-        kept.append(legs.home_row(3, u, gnr, gnr_t))
     wgrad(0, rown[...].reshape(n, width))
 
     @pl.when(at.core == 1)
     def _():
-        weights.swap(w2.at[0]).start()
+        weights.swap(w2.at[0])
 
     for u in range(2):
         legs.got_col(1, u, cold)
         legs.got_col(0, u, coln)
+        if u == 0:
+            for v in range(2):
+                legs.home_row(2, v, orow, orow_t)
+            legs.home_row(3, 0, gnr, gnr_t)
         c4 = cols // 8
         x = coln[u * c4 : (u + 1) * c4].reshape(size, width)
         dd[...] = cold[u * c4 : (u + 1) * c4].reshape(size, half)
-        unit(1, u, x, dd, oo, gg)
+        def early():
+            @pl.when(at.core == 0)
+            def _():
+                weights.along_x(lambda block: w2[0, block, :].astype(F32), X_ORDER[:2])
+
+        unit(1, u, x, dd, oo, gg, early if u == 0 else None)
         ocol[u * c4 : (u + 1) * c4] = oo[...].reshape(c4, 4 * rows, half)
         gnc[u * c4 : (u + 1) * c4] = gg[...].reshape(c4, 4 * rows, width)
-        kept.append(legs.home_col(2, u, ocol, ocol_t))
-        kept.append(legs.home_col(3, u, gnc, gnc_t))
+        legs.home_col(2, u, ocol, ocol_t)
+        if u == 0:
+            legs.home_row(3, 1, gnr, gnr_t)
         if u == 0:
 
             @pl.when(at.core == 0)
             def _():
-                weights.along_x(lambda block: w2[0, block, :].astype(F32))
+                weights.along_x(lambda block: w2[0, block, :].astype(F32), X_ORDER[2:])
 
     wgrad(1, coln[...].reshape(n, width))
+    legs.home_col(3, 0, gnc, gnc_t)
+
 
     @pl.when(at.core == 0)
     def _():
-        weights.swap(w2.at[1]).start()
-        weights.scatter_yz()
+        weights.swap(w2.at[1])
+
+    @pl.when(at.core == 0)
+    def _():
+        weights.scatter(False)
 
     @pl.when(at.core == 1)
     def _():
         weights.along_x(lambda block: w2[1, block, :].astype(F32))
 
-    for c in kept:
-        c.wait()
+    legs.home_col(3, 1, gnc, gnc_t)
+    legs.settle()
     for u in range(2):
         legs.back_row(2, u, orow_t)
         legs.back_col(2, u, ocol_t)
@@ -494,12 +566,22 @@
         return cot[:, pl.ds(pl.multiple_of(h * half, LANES), half)]
 
     go_out[...] = dims(att[...], cot_half(1 - at.core), 0, 0).astype(BF16)
-    outs.swap(go_out).start()
+    outs.swap(go_out)
     go_own[...] = dims(att[...], cot_half(at.core), 0, 0)
     mixed[...] = (res[...] + dims(att[...], wo[...], 1, 0)).astype(BF16)
 
     store(mixed, mixed_h)
+
+    @pl.when(at.core == 0)
+    def _():
+        weights.scatter_again(False)
+
     outs.along_x(lambda block: go_own[block, :])
+
+    @pl.when(at.core == 0)
+    def _():
+        weights.gather(False)
+
     for u in range(2):
         legs.back_row(3, u, gnr_t)
         legs.back_col(3, u, gnc_t)
@@ -517,7 +599,8 @@
         return dims(pick[:, pl.ds(pl.multiple_of(core * halfway, LANES), halfway)], gfine[...], 0, 0)
 
     co_out[...] = dense(1 - at.core).astype(BF16)
-    go(co_out, co_in, co_s.at[0], co_r.at[0], partner)
+    rcopy(co_out, co_in, co_s.at[0], co_r.at[0], partner).start()
+    legs.gone(co_out, co_s.at[0], co_r.at[0])
     levels = dims(lv[...], gfine[...], 0, 0)[0:8]
     row = lax.broadcasted_iota(jnp.int32, (8, half), 0)
     for h in range(2):
@@ -525,63 +608,90 @@
         both = jnp.where(row == 0, sm_gain[:, c : c + half], levels[:, c : c + half])
         sm_own[4 * h : 4 * h + 4, :] = both[0:4]
     for i, dev in enumerate(dp_dev):
-        go(sm_own, sm_in.at[i], s1_s.at[i], s1_r.at[i], dev)
+        rcopy(sm_own, sm_in.at[i], s1_s.at[0], s1_r.at[0], dev).start()
     co_own[...] = dense(at.core)
     store(gfine, gfine_h)
 
     @pl.when(at.core == 0)
     def _():
-        weights.gather_yz()
+        weights.gather_again(False)
 
     rcopy(co_out, co_in, co_s.at[0], co_r.at[0], partner).wait_recv()
-    for i, (a, b) in enumerate(FXP):
-        owner = at.fx_at(a, b)
-        block = pl.ds(pl.multiple_of(owner * part, part), part)
-        cf_out[i] = (co_own[block, :] + co_in[block, :].astype(F32)).astype(BF16)
-        go(cf_out.at[i], cf_in.at[i], cf_s.at[i], cf_r.at[i], fx_dev[i])
+
+    def block(zl, y):
+        return pl.ds(pl.multiple_of((zl * 4 + y) * part, part), part)
+
+    for b in range(1, 4):
+        dev, _ = at.yz(0, b)
+        y = lax.rem(at.y + b, 4)
+        for zl in range(2):
+            rows_ = block(zl, y)
+            cf_out[b - 1, zl] = (co_own[rows_, :] + co_in[rows_, :].astype(F32)).astype(BF16)
+        rcopy(cf_out.at[b - 1], cf_in.at[b - 1], cf_s.at[0], cf_r.at[0], dev).start()
 
     @pl.when(at.core == 1)
     def _():
-        weights.scatter_yz()
-
-    outs.scatter_yz()
+        weights.scatter(True)
+
+    outs.scatter(True)
+    rcopy(sm_in, sm_in, s1_s.at[0], s1_r.at[0], partner).wait_recv()
     total = sm_own[...]
-    for i, dev in enumerate(dp_dev):
-        rcopy(sm_own, sm_in.at[i], s1_s.at[i], s1_r.at[i], dev).wait_recv()
+    for i in range(7):
         total = total + sm_in[i]
-    sm_mid[...] = total
-    for i, (a, b) in enumerate(YZP):
-        go(sm_mid, sm_in2.at[i], s2_s.at[i], s2_r.at[i], at.yz(a, b)[0])
+    sm_mid[0] = total
+    for i in range(3):
+        dev, _ = at.yz(i + 1, 0)
+        rcopy(sm_mid.at[0], sm_in2.at[0, i], s2_s.at[0], s2_r.at[0], dev).start()
+
+    @pl.when(at.core == 1)
+    def _():
+        weights.scatter_again(True)
+
+    outs.scatter_again(True)
+    rcopy(cf_in, cf_in, cf_s.at[0], cf_r.at[0], partner).wait_recv()
+    for zl in range(2):
+        rows_ = block(zl, at.y)
+        value = co_own[rows_, :] + co_in[rows_, :].astype(F32)
+        for i in range(3):
+            value = value + cf_in[i, zl].astype(F32)
+        cz[zl] = value
+        cy_out[zl] = value.astype(BF16)
+    for a in range(1, 4):
+        dev, _ = at.yz(a, 0)
+        rcopy(cy_out.at[lax.rem(at.zl + a, 2)], cy_in.at[a - 1], cy_s.at[0], cy_r.at[0], dev).start()
 
     @pl.when(at.core == 0)
     def _():
         weights.swap_back()
 
-    block = pl.ds(pl.multiple_of(at.fx * part, part), part)
-    value = co_own[block, :] + co_in[block, :].astype(F32)
-    for i in range(7):
-        rcopy(cf_out.at[i], cf_in.at[i], cf_s.at[i], cf_r.at[i], fx_dev[i]).wait_recv()
-        value = value + cf_in[i].astype(F32)
-    cy_out[...] = value.astype(BF16)
-    for i, (a, c) in enumerate(FYP):
-        go(cy_out, cy_in.at[i], cy_s.at[i], cy_r.at[i], fy_dev[i])
+    rcopy(sm_in2.at[0], sm_in2.at[0], s2_s.at[0], s2_r.at[0], partner).wait_recv()
+    sm_mid[1] = sm_mid[0] + sm_in2[0, 0] + sm_in2[0, 1] + sm_in2[0, 2]
+    for i in range(3):
+        dev, _ = at.yz(0, i + 1)
+        rcopy(sm_mid.at[1], sm_in2.at[1, i], s2_s.at[1], s2_r.at[1], dev).start()
 
     @pl.when(at.core == 1)
     def _():
-        weights.gather_yz()
-
-    outs.gather_yz()
-    total = sm_mid[...]
-    for i, (a, b) in enumerate(YZP):
-        rcopy(sm_mid, sm_in2.at[i], s2_s.at[i], s2_r.at[i], at.yz(a, b)[0]).wait_recv()
-        total = total + sm_in2[i]
-    small[...] = total
+        weights.gather(True)
+
+    outs.gather(True)
+    rcopy(cy_in, cy_in, cy_s.at[0], cy_r.at[0], partner).wait_recv()
+    value = cz[at.zl] + cy_in[0].astype(F32) + cy_in[1].astype(F32) + cy_in[2].astype(F32)
+    gcoarse[pl.ds(pl.multiple_of(at.core * part, part), part), :] = value
+    cc_out[...] = value.astype(BF16)
+    rcopy(cc_out, cc_in, co_s.at[1], co_r.at[1], partner).start()
+
+    @pl.when(at.core == 1)
+    def _():
+        weights.gather_again(True)
+
+    outs.gather_again(True)
+    rcopy(cc_out, cc_in, co_s.at[1], co_r.at[1], partner).wait_recv()
+    gcoarse[pl.ds(pl.multiple_of((1 - at.core) * part, part), part), :] = cc_in[...].astype(F32)
+    store(gcoarse, gcoarse_h)
+    rcopy(sm_in2.at[1], sm_in2.at[1], s2_s.at[1], s2_r.at[1], partner).wait_recv()
+    small[...] = sm_mid[1] + sm_in2[1, 0] + sm_in2[1, 1] + sm_in2[1, 2]
     store(small, small_h)
-    for i in range(3):
-        rcopy(cy_out, cy_in.at[i], cy_s.at[i], cy_r.at[i], fy_dev[i]).wait_recv()
-    gcoarse[pl.ds(pl.multiple_of(at.core * part, part), part), :] = cy_out[...].astype(F32) + cy_in[1].astype(F32)
-    gcoarse[pl.ds(pl.multiple_of((1 - at.core) * part, part), part), :] = cy_in[0].astype(F32) + cy_in[2].astype(F32)
-    store(gcoarse, gcoarse_h)
 
     @pl.when(at.core == 1)
     def _():
@@ -592,6 +702,13 @@
     store(wsum, wsum_h)
     outs.finish()
     store(osum, osum_h)
+    legs.gone(sm_in, s1_s.at[0], s1_r.at[0])
+    legs.gone(cf_in, cf_s.at[0], cf_r.at[0])
+    legs.gone(cy_in, cy_s.at[0], cy_r.at[0])
+    legs.gone(cc_in, co_s.at[1], co_r.at[1])
+    legs.gone(sm_in2.at[0], s2_s.at[0], s2_r.at[0])
+    legs.gone(sm_in2.at[1], s2_s.at[1], s2_r.at[1])
+    legs.settle()
     for c in sent:
         c.wait_send()
     weights.drain()
@@ -608,7 +725,6 @@
     dma = pltpu.SemaphoreType.DMA
     vmem = pltpu.VMEM
     hbm = pl.BlockSpec(memory_space=pl.ANY)
-    here = pl.BlockSpec(memory_space=pltpu.VMEM)
     r2, c8, c4 = rows // 8, cols * 8, cols // 4
     return pl.pallas_call(
         functools.partial(layer_kernel, rows, cols, scale),
@@ -621,9 +737,11 @@
             jax.ShapeDtypeStruct(Reduce.gathered(width // 4, half // LANES), BF16),
             jax.ShapeDtypeStruct((8, half), F32),
         ],
-        in_specs=[hbm, hbm, here, here, here, here, here, hbm, hbm],
+        in_specs=[hbm] * 2 + [pl.BlockSpec(memory_space=pltpu.MemorySpace.HBM)] * 5 + [hbm] * 2,
         out_specs=[hbm] * 6,
         scratch_shapes=[
+            vmem(parent.shape, jnp.int32), vmem((own, width), BF16), vmem(level.shape, jnp.int32),
+            vmem(table.shape, F32), vmem(gain.shape, F32),
             vmem((n, width), BF16), vmem((n, width), BF16), vmem((width, 6 * half), BF16), vmem((width, width), BF16),
             vmem((8 * own, width + LANES), BF16), vmem((n, n), BF16), vmem((n, n), BF16), vmem((n, width), F32), vmem((n, LANES), BF16),
             vmem((rows, cols, width), BF16), vmem((rows, cols, half), BF16),
@@ -638,16 +756,17 @@
             vmem((n // 2, half), BF16), vmem((n // 2, half), BF16), vmem((n // 2, width), BF16),
             vmem((n, width), BF16), vmem((width, half), BF16), vmem((width, half), F32),
             vmem((8 * part, width), BF16), vmem((8 * part, width), BF16), vmem((8 * part, width), F32),
-            vmem((7, part, width), BF16), vmem((7, part, width), BF16),
-            vmem((part, width), BF16), vmem((3, part, width), BF16),
-            vmem((8, half), F32), vmem((7, 8, half), F32), vmem((8, half), F32), vmem((15, 8, half), F32),
+            vmem((3, 2, part, width), BF16), vmem((3, 2, part, width), BF16), vmem((2, part, width), F32),
+            vmem((2, part, width), BF16), vmem((3, part, width), BF16),
+            vmem((part, width), BF16), vmem((part, width), BF16),
+            vmem((8, half), F32), vmem((7, 8, half), F32), vmem((2, 8, half), F32), vmem((2, 3, 8, half), F32),
             vmem((n, width), BF16), vmem((n, width), BF16), vmem((own, width), F32),
             vmem(Reduce.gathered(width // 4, 3 * half // LANES), BF16),
             vmem(Reduce.gathered(width // 4, half // LANES), BF16), vmem((8, half), F32),
-            dma((4,)), dma((6,)), dma((7,)), dma((7,)), dma((7,)), dma((7,)),
-            dma((4, 2, 7)), dma((4, 2, 7)), dma((4, 2, 3)), dma((4, 2, 3)), dma((4, 4)),
-            dma((1,)), dma((1,)), dma((7,)), dma((7,)), dma((3,)), dma((3,)),
-            dma((7,)), dma((7,)), dma((15,)), dma((15,)),
+            dma((9,)), dma((6,)), dma((1,)), dma((7,)), dma((1,)), dma((1,)),
+            dma((4, 2)), dma((4, 2)), dma((4, 2)), dma((4, 2)), dma((4, 4)),
+            dma((2,)), dma((2,)), dma((1,)), dma((1,)), dma((1,)), dma((1,)),
+            dma((1,)), dma((1,)), dma((2,)), dma((2,)),
             *Reduce.scratch(width // 4, 3 * half // LANES),
             *Reduce.scratch(width // 4, half // LANES),
         ],
@@ -725,7 +844,7 @@
     fine = fine_tokens.reshape(n, width)
     cot = cotangent.reshape(n, width)
     parts = layer(
-        fine, cot, parent, coarse_tokens.reshape(own, width), tile_level,
+        fine, cot, parent.swapaxes(1, 2), coarse_tokens.reshape(own, width), tile_level,
         level_table, norm_gain, qkv_weight, out_weight, rows, cols, scale,
     )
     mixed, gfine, gcoarse, gq, gout, ggain, glevel = emit(parts, grad_scale)

time: 108 us -> 101 us (0.935)
  Pallas kernels: 100 us -> 93.4 us
    pallas_call x1, Pallas kernels: 97.9 us -> 91.2 us  [layer(): pl.pallas_call(functools.partial(layer_kernel, rows, cols, scale), name='...]
    unnamed x13 -> x14, local copies, waits for them, and re-layouts: 6 us -> 5.92 us
where the time goes in v4:
time: 101 us; the launch traced here: 100 us
  Pallas kernels  93.4 us (92%)
  local copies, waits for them, and re-layouts  5.92 us (6%)
    pallas_call x1, Pallas kernels, layer(): pl.pallas_call(functools.partial(layer_kernel, rows, cols, scale), name='...  91.2 us
    unnamed x14, local copies, waits for them, and re-layouts  5.92 us
    pallas_call x1, Pallas kernels, emit(): pl.pallas_call(functools.partial(emit_kernel, rows, grad_scale), name='em...  2.2 us

profile of v4, /device:TPU:0, one launch (start us, length us, event | category | flops | bytes accessed | tf_op | source)
XLA Modules:
  0.0 100.0 jit_solution(12070225097214763673)
XLA Ops:
  0.6 0.0 copy-start.2
  0.6 0.9 copy-done.2
  1.5 0.0 copy-start.3
  1.5 0.7 copy-done.3
  2.2 0.0 copy-start.4
  2.2 0.7 copy-done.4
  2.9 0.0 copy-start.5
  2.9 0.7 copy-done.5
  3.6 0.0 copy-start.6
  3.6 0.7 copy-done.6
  4.3 91.2 %layer.1 = (bf16[512,768]{1,0:T(8,128)(2,1)S(1)}, bf16[512,768]{1,0:T(8,128)(2,1)}, f32[64,768]{1,0:T(8,128)S(1)}, bf16[2,1792,128]{2,1,0:T(8,128)(2,1)}, bf16[2...) custom-call(bf16[512,768]{1,0:T(8,128)(2,1)} %bitcast.10, bf16[512,768]{1,0:T(8,128)(2,1)} %bitcast.11, ...), custom_call_target="tpu_custom_call" | custom-call | tf_op jit(solution)/shard_map/layer/pallas_call | solution.py:729
  95.5 0.0 copy-start
  95.5 1.2 %copy-done = bf16[2,1792,128]{2,1,0:T(8,128)(2,1)S(1)} copy-done((bf16[2,1792,128]{2,1,0:T(8,128)(2,1)S(1)}, bf16[2,1792,128]{2,1,0:T(8,128)(2,1)}, u32[]{:S(2)}) %copy-start) | copy-done | bytes 917528
  96.7 0.0 copy-start.1
  96.7 1.1 %copy-done.1 = bf16[512,768]{1,0:T(8,128)(2,1)S(1)} copy-done((bf16[512,768]{1,0:T(8,128)(2,1)S(1)}, bf16[512,768]{1,0:T(8,128)(2,1)}, u32[]{:S(2)}) %copy-start.1) | copy-done | bytes 786456
  97.8 2.2 %emit.1 = (bf16[512,768]{1,0:T(8,128)(2,1)}, bf16[512,768]{1,0:T(8,128)(2,1)}, f32[64,768]{1,0:T(8,128)}, f32[192,2304]{1,0:T(8,128)}, f32[192,768]{1,0:T(8,128)}, /*index=5*/f32[1,192]{1,0:T(1,128)}, f32[3,768]{1,0:T(4,128)}) custom-call(bf16[512,768]{1,0:T(8,128)(2,1)S(1)} %get-tuple-element.20.mixed, bf16[512,768]{1,0:T(8,128)(2,1)S(1)} %copy-done.1, ...), custom_call_target="tpu_custom_call" | custom-call | tf_op jit(solution)/shard_map/emit/pallas_call | solution.py:808
Async XLA Ops:
  0.6 0.9 copy-start.2
  1.5 0.7 copy-start.3
  2.2 0.7 copy-start.4
  2.9 0.7 copy-start.5
  3.6 0.7 copy-start.6
  95.5 1.2 %copy-start = (bf16[2,1792,128]{2,1,0:T(8,128)(2,1)S(1)}, bf16[2,1792,128]{2,1,0:T(8,128)(2,1)}, u32[]{:S(2)}) copy-start(bf16[2,1792,128]{2,1,0:T(8,128)(2,1)} %get-tuple-element.23.wsum) | copy-start | bytes 2752516
  96.7 1.1 %copy-start.1 = (bf16[512,768]{1,0:T(8,128)(2,1)S(1)}, bf16[512,768]{1,0:T(8,128)(2,1)}, u32[]{:S(2)}) copy-start(bf16[512,768]{1,0:T(8,128)(2,1)} %get-tuple-element.21.gfine) | copy-start | bytes 2359300

commit v5 on v4

--- a/solution.py
+++ b/solution.py
@@ -19,7 +19,8 @@
 YZP = [(a, b) for a in range(4) for b in range(4) if (a, b) != (0, 0)]
 LANES = 128
 X_ORDER = (2, 1, 3, 0)
-VMEM_LIMIT = 52 << 20
+VMEM_LIMIT = 67043328
+EMIT_LIMIT = 67043328
 
 
 def dims(a, b, ca, cb):
@@ -124,8 +125,9 @@
             dma((2,)), dma((5,)), dma((1,)), dma((1,)), dma((2,)), dma((2,)), dma((2,)), dma((2,)),
         ]
 
-    def __init__(self, at, ag, refs, rows, nb):
+    def __init__(self, at, ag, refs, rows, nb, direct):
         self.ag = ag
+        self.direct = direct
         (self.cx, self.xs, self.xr, self.acc, self.p16, self.ry, self.py, self.rz,
          self.c_s, self.c_r, self.x_s, self.x_r, self.r_s, self.r_r, self.g_s, self.g_r) = refs
         self.at, self.rows, self.nb = at, rows, nb
@@ -210,15 +212,21 @@
         mine = self.slot(self.major(z_first) * 4 + self.minor(z_first))
         self.ag[at.core, mine, :] = value.astype(BF16)
         src = self.ag.at[at.core, mine]
+        if self.direct:
+            for a, b in YZP:
+                rcopy(src, src, self.g_s.at[1], self.g_r.at[1], at.yz(a, b)[0]).start()
+            return
         for k in range(1, 4):
             rcopy(src, src, self.g_s.at[0], self.g_r.at[0], self.ahead(z_first, k, 1)).start()
 
     def pieces(self, stage):
-        size = 3 * self.piece * (4 if stage else 1)
+        size = self.piece * (15 if self.direct else 12 if stage else 3)
         ref = self.ag.at[self.at.core, pl.ds(0, size)]
         return rcopy(ref, ref, self.g_s.at[stage], self.g_r.at[stage], self.partner)
 
     def gather_again(self, z_first):
+        if self.direct:
+            return
         self.pieces(0).wait_recv()
         src = self.ag.at[self.at.core, self.column(z_first, 0)]
         for k in range(1, 4):
@@ -238,7 +246,8 @@
         rcopy(self.xs, self.xr, self.x_s.at[0], self.x_r.at[0], self.partner).wait_send()
         rcopy(self.ry, self.ry, self.r_s.at[0], self.r_r.at[0], self.partner).wait_send()
         rcopy(self.rz, self.rz, self.r_s.at[1], self.r_r.at[1], self.partner).wait_send()
-        self.pieces(0).wait_send()
+        if not self.direct:
+            self.pieces(0).wait_send()
         self.pieces(1).wait_send()
         ref = self.ag.at[self.at.core]
         rcopy(ref, ref, self.c_s.at[1], self.c_r.at[4], self.partner).wait_send()
@@ -372,8 +381,8 @@
     partner = fy_dev[0]
     dp_off = [(d, c) for d in range(4) for c in range(2) if (d, c) != (0, 0)]
     dp_dev = [{"dp": at.dp_at(d), "fy": at.fy_at(0, c)} for d, c in dp_off]
-    weights = Reduce(at, wsum, red[:N_RED], width // 4, 3 * half // LANES)
-    outs = Reduce(at, osum, red[N_RED:], width // 4, half // LANES)
+    weights = Reduce(at, wsum, red[:N_RED], width // 4, 3 * half // LANES, True)
+    outs = Reduce(at, osum, red[N_RED:], width // 4, half // LANES, True)
     sent = legs.sent
     stores = []
 
@@ -776,21 +785,38 @@
     )(fine, cot, parent, coarse, level, table, gain, wq, wo)
 
 
-def emit_kernel(rows, grad_scale, mixed, gfine, gcoarse, wsum, osum, small, mixed_o, gfine_o, gcoarse_o, gq, gout, ggain, glevel):
-    mixed_o[...] = mixed[...]
-    gfine_o[...] = gfine[...]
-    gcoarse_o[...] = gcoarse[...]
+def emit_kernel(
+    rows, grad_scale, mixed_h, gfine_h, gcoarse_h, wsum_h, osum_h, small_h,
+    mixed_o, gfine_o, gcoarse_o, gq_o, gout_o, ggain, glevel,
+    mixed, gfine, gcoarse, wsum, osum, small, gq, gout, ld, st,
+):
+    ins = ((wsum_h, wsum), (osum_h, osum), (small_h, small), (mixed_h, mixed), (gfine_h, gfine), (gcoarse_h, gcoarse))
+    loads = [pltpu.make_async_copy(a, b, ld.at[i]) for i, (a, b) in enumerate(ins)]
+    outs = ((gq, gq_o), (gout, gout_o), (mixed, mixed_o), (gfine, gfine_o), (gcoarse, gcoarse_o))
+    stores = [pltpu.make_async_copy(a, b, st.at[i]) for i, (a, b) in enumerate(outs)]
+    for c in loads:
+        c.start()
     half = small.shape[1]
     nb = half // LANES
+    loads[0].wait()
     for h in range(2):
         for j in range(3):
             for b in range(nb):
                 c = (2 * j + h) * half + b * LANES
                 k = (j * nb + b) * rows
                 gq[:, c : c + LANES] = wsum[h, k : k + rows, :].astype(F32) * grad_scale
+    stores[0].start()
+    for i in range(3):
+        loads[3 + i].wait()
+        stores[2 + i].start()
+    loads[1].wait()
+    for h in range(2):
         for b in range(nb):
             c = h * half + b * LANES
             gout[:, c : c + LANES] = osum[h, b * rows : (b + 1) * rows, :].astype(F32) * grad_scale
+    stores[1].start()
+    loads[2].wait()
+    for h in range(2):
         glevel[:, h * half : (h + 1) * half] = small[4 * h + 1 : 4 * h + 4, :] * grad_scale
     dp = lax.axis_index("dp")
     vector = jnp.concatenate([small[0:1, :], small[4:5, :]], axis=1) * grad_scale
@@ -798,6 +824,8 @@
     for i in range(1, 4):
         share = jnp.where(dp == i, vector[:, i * rows : (i + 1) * rows], share)
     ggain[...] = share
+    for c in stores:
+        c.wait()
 
 
 def emit(parts, grad_scale):
@@ -805,21 +833,28 @@
     n, width = mixed.shape
     rows = width // 4
     here = pl.BlockSpec(memory_space=pltpu.VMEM)
+    far = pl.BlockSpec(memory_space=pl.ANY)
+    shapes = [
+        jax.ShapeDtypeStruct(mixed.shape, BF16),
+        jax.ShapeDtypeStruct(gfine.shape, BF16),
+        jax.ShapeDtypeStruct(gcoarse.shape, F32),
+        jax.ShapeDtypeStruct((rows, 3 * width), F32),
+        jax.ShapeDtypeStruct((rows, width), F32),
+        jax.ShapeDtypeStruct((1, rows), F32),
+        jax.ShapeDtypeStruct((LEVELS, width), F32),
+    ]
     return pl.pallas_call(
         functools.partial(emit_kernel, rows, grad_scale),
         name="emit",
-        out_shape=[
-            jax.ShapeDtypeStruct(mixed.shape, BF16),
-            jax.ShapeDtypeStruct(gfine.shape, BF16),
-            jax.ShapeDtypeStruct(gcoarse.shape, F32),
-            jax.ShapeDtypeStruct((rows, 3 * width), F32),
-            jax.ShapeDtypeStruct((rows, width), F32),
-            jax.ShapeDtypeStruct((1, rows), F32),
-            jax.ShapeDtypeStruct((LEVELS, width), F32),
+        out_shape=shapes,
+        in_specs=[far] * 6,
+        out_specs=[far] * 5 + [here] * 2,
+        scratch_shapes=[
+            *[pltpu.VMEM(p.shape, p.dtype) for p in parts],
+            pltpu.VMEM(shapes[3].shape, F32), pltpu.VMEM(shapes[4].shape, F32),
+            pltpu.SemaphoreType.DMA((6,)), pltpu.SemaphoreType.DMA((5,)),
         ],
-        in_specs=[here] * 6,
-        out_specs=[here] * 7,
-        compiler_params=pltpu.CompilerParams(vmem_limit_bytes=24 << 20),
+        compiler_params=pltpu.CompilerParams(vmem_limit_bytes=EMIT_LIMIT),
     )(*parts)
 
 

time: 101 us -> 95.4 us (0.945)
  local copies, waits for them, and re-layouts: 5.92 us -> 0 us
    unnamed x14 -> x0, local copies, waits for them, and re-layouts: 5.92 us -> none
    pallas_call x1, Pallas kernels: 2.2 us -> 3.98 us  [emit(): pl.pallas_call(functools.partial(emit_kernel, rows, grad_scale), name='em...]
    pallas_call x1, Pallas kernels: 91.2 us -> 89.8 us  [layer(): pl.pallas_call(functools.partial(layer_kernel, rows, cols, scale), name='...]
where the time goes in v5:
time: 95.4 us; the launch traced here: 94.6 us
  Pallas kernels  93.8 us (98%)
    pallas_call x1, Pallas kernels, layer(): pl.pallas_call(functools.partial(layer_kernel, rows, cols, scale), name='...  89.8 us
    pallas_call x1, Pallas kernels, emit(): pl.pallas_call(functools.partial(emit_kernel, rows, grad_scale), name='em...  3.98 us

profile of v5, /device:TPU:0, one launch (start us, length us, event | category | flops | bytes accessed | tf_op | source)
XLA Modules:
  0.0 94.6 jit_solution(16725383965775213903)
XLA Ops:
  0.6 89.8 %layer.1 = (bf16[512,768]{1,0:T(8,128)(2,1)}, bf16[512,768]{1,0:T(8,128)(2,1)}, f32[64,768]{1,0:T(8,128)}, bf16[2,1792,128]{2,1,0:T(8,128)(2,1)}, bf16[2,768,128]{2,1,0:T(8,128)(2,1)}, /*index=5*/f32[8,384]{1,0:T(8,128)}) custom-call(bf16[512,768]{1,0:T(8,128)(2,1)} %bitcast.8, bf16[512,768]{1,0:T(8,128)(2,1)} %bitcast.9, s32[1,8,16]{2,1,0:T(8,128)} %bitcast.11, ...), custom_call_target="tpu_custom_call" | custom-call | tf_op jit(solution)/shard_map/layer/pallas_call | solution.py:738
  90.4 4.0 %emit.1 = (bf16[512,768]{1,0:T(8,128)(2,1)}, bf16[512,768]{1,0:T(8,128)(2,1)}, f32[64,768]{1,0:T(8,128)}, f32[192,2304]{1,0:T(8,128)}, f32[192,768]{1,0:T(8,128)}, /*index=5*/f32[1,192]{1,0:T(1,128)}, f32[3,768]{1,0:T(4,128)}) custom-call(bf16[512,768]{1,0:T(8,128)(2,1)} %get-tuple-element.20.mixed_h, bf16[512,768]{1,0:T(8,128)(2,1)} %get-tuple-element.21.gfine_h, ...), custom_call_target="tpu_custom_call" | custom-call | tf_op jit(solution)/shard_map/emit/pallas_call | solution.py:846
